TPU v7x, 32 devices: a whole 2x2x4 slice. The times are simulated.
32 devices in a mesh: comp: 8 (over y, x, core), strip: 4 (over z).
Axes of the slice: x: 2, y: 2, z: 4, core: 2. Of those that a mesh axis runs over, the one named last changes fastest.
Arguments:
- energy: bfloat16 [1152, 64, 512], P('comp', 'strip'), may hold values from 0.049804688 to 2
- heading: float32 [1152], P('comp'), may hold values from -3.140625 to 3.140625
- growth: float32 [1152], P('comp'), may hold values from 0.005 to 0.05
- courant: float32 [1152, 2], P('comp'), may hold values from -0.45 to 0.45
- dissip: float32 [1152], replicated, may hold values from 0.05 to 0.5
- mixing: bfloat16 [1152, 1152], replicated, may hold values from -0.1875 to 0.1875
- transfer: bfloat16 [1152, 1152], replicated, may hold values from -0.046875 to 0.046875
- pattern: int32 [1152], replicated, may hold values from 0 to 1151, each once
- regime_winds: float32 [8, 2], replicated, may hold values from -8 to 8
- regime: int32 [32, 32], P('strip'), may hold values from 0 to 7
- seeds: int32 [32, 32], P('strip'), may hold values from 0 to 1023
- sea_mask: int32 [64, 512], P('strip'), may hold values 0 or 1
Outputs:
- energy_out: float32 [1152, 64, 512], P('comp', 'strip')
Inputs may be any that keep to these rules, and one draw needn't show every extreme that they name: `pattern`: each component is named exactly once.
All inputs are finite; a program needn't handle non-finite values. No bound on the sum of `sea_mask` on one device may be relied on, other than what follows from the above.
Results may differ from a plain program's by a relative error of at most 0.0008.
Values may be sent and summed in bfloat16 or wider, within the bound.
No kernel may reach another device: no remote copies, remote signals or barrier semaphores. Data moves between devices by JAX's collectives and lax.ppermute only.
A program may use at most 192 MiB of HBM per device.

v0:
```python
import jax
import jax.numpy as jnp
from jax import lax
from jax.sharding import PartitionSpec as P

SUBSTEPS = 4
TILE_ROWS = 2
TILE_COLS = 16


def with_halo(block, sides, width):
    for axis, dim in sides:
        count = lax.axis_size(axis)
        forward = [(i, i + 1) for i in range(count - 1)]
        backward = [(target, source) for source, target in forward]
        low = lax.ppermute(
            lax.slice_in_dim(block, block.shape[dim] - width, None, axis=dim), axis, forward
        )
        high = lax.ppermute(lax.slice_in_dim(block, 0, width, axis=dim), axis, backward)
        block = jnp.concatenate([low, block, high], axis=dim)
    return block


def strip_winds(regime_winds, regime, seeds):
    levels = jnp.arange(regime_winds.shape[0], dtype=jnp.int32)
    onehot = (regime[..., None] == levels).astype(jnp.float32)
    base_u = jnp.sum(onehot * regime_winds[:, 0], axis=-1)
    base_v = jnp.sum(onehot * regime_winds[:, 1], axis=-1)
    tile_u = base_u + 0.25 * (seeds % 13 - 6).astype(jnp.float32)
    tile_v = base_v + 0.4 * (seeds % 7 - 3).astype(jnp.float32)
    wind_u = jnp.repeat(jnp.repeat(tile_u, TILE_ROWS, axis=0), TILE_COLS, axis=1)
    wind_v = jnp.repeat(jnp.repeat(tile_v, TILE_ROWS, axis=0), TILE_COLS, axis=1)
    return (wind_u, wind_v)


def cell_terms(spectra, mixing, transfer, pattern, dissip):
    spectrum_shape = spectra.shape
    flattened = spectra.reshape(spectrum_shape[0], -1)
    mixed_terms = jnp.dot(mixing, flattened, preferred_element_type=jnp.float32)
    partner = jnp.take(flattened, pattern, axis=0)
    product = (mixed_terms * partner.astype(jnp.float32)).astype(jnp.bfloat16)
    nonlinear = jnp.dot(transfer, product, preferred_element_type=jnp.float32)
    widened = flattened.astype(jnp.float32)
    mean_energy = jnp.sum(widened, axis=0) / spectrum_shape[0]
    result = nonlinear - dissip[:, None] * mean_energy[None, :] * widened
    return result.astype(jnp.bfloat16).reshape(spectrum_shape)


def advect(padded, sea_field, courant_x, courant_y):
    flux_y = (
        jnp.maximum(courant_y, 0.0) * padded[..., :-1, :]
        + jnp.minimum(courant_y, 0.0) * padded[..., 1:, :]
    )
    center = padded[..., 1:-1, :]
    widths = [(0, 0)] * (center.ndim - 1) + [(1, 1)]
    padded_x = jnp.pad(center, widths)
    flux_x = (
        jnp.maximum(courant_x, 0.0) * padded_x[..., :-1]
        + jnp.minimum(courant_x, 0.0) * padded_x[..., 1:]
    )
    return (
        center - (flux_x[..., 1:] - flux_x[..., :-1]) - (flux_y[..., 1:, :] - flux_y[..., :-1, :])
    ) * sea_field


def per_device(
    energy,
    heading,
    growth,
    courant,
    dissip,
    mixing,
    transfer,
    pattern,
    regime_winds,
    regime,
    seeds,
    sea_mask,
):
    wind_u, wind_v = strip_winds(regime_winds, regime, seeds)
    widened = energy.astype(jnp.float32)
    drive = (
        wind_u[None] * jnp.cos(heading)[:, None, None]
        + wind_v[None] * jnp.sin(heading)[:, None, None]
    )
    input_term = growth[:, None, None] * jnp.maximum(0.0, drive) * widened
    returned = lax.all_to_all(
        cell_terms(
            lax.all_to_all(energy, "comp", split_axis=1, concat_axis=0, tiled=True),
            mixing,
            transfer,
            pattern,
            dissip,
        ),
        "comp",
        split_axis=0,
        concat_axis=1,
        tiled=True,
    )
    energy_field = widened + input_term + returned.astype(jnp.float32)
    sea_field = sea_mask.astype(jnp.float32)
    courant_x = courant[:, 0][:, None, None]
    courant_y = courant[:, 1][:, None, None]
    for substep in range(SUBSTEPS):
        padded = with_halo(energy_field, (("strip", 1),), 1)
        energy_field = advect(padded, sea_field, courant_x, courant_y)
    return energy_field


def solution(mesh):
    placed = (
        P("comp", "strip", None),
        P("comp"),
        P("comp"),
        P("comp", None),
        P(),
        P(),
        P(),
        P(),
        P(),
        P("strip", None),
        P("strip", None),
        P("strip", None),
    )
    return jax.shard_map(
        per_device, mesh=mesh, in_specs=placed, out_specs=P("comp", "strip", None), check_vma=False
    )
```

profile of v0, /device:TPU:26, one launch (start us, length us, event | category | flops | bytes accessed | tf_op | source)
XLA Modules:
  0.0 194.6 jit_solution(15152616332735893977)
XLA Ops:
  0.0 4.5 %copy.33 = bf16[144,16,512]{2,0,1:T(8,128)(2,1)} copy(bf16[144,16,512]{2,1,0:T(8,128)(2,1)} %param.12) | data formatting | bytes 4718592 | tf_op args[0]
  4.5 4.8 %all-to-all-start = ((bf16[144,16,512]{2,0,1:T(8,128)(2,1)}), bf16[144,16,512]{2,0,1:T(8,128)(2,1)}, u32[]{:S(2)}, u32[]{:S(2)}) async-start(bf16[144,16,512]{2,0,1:T(8,128)(2,1)} %copy.33), calls=%async_computation | async-start | bytes 4718592 | tf_op jit(solution)/shard_map/all_to_all | solution.py:89
  9.4 28.0 %all-to-all-done = bf16[144,16,512]{2,0,1:T(8,128)(2,1)} async-done(((bf16[144,16,512]{2,0,1:T(8,128)(2,1)}), bf16[144,16,512]{2,0,1:T(8,128)(2,1)}, u32[]{:S(2)}, u32[]{:S(2)}) %all-to-all-start) | async-done | bytes 2359328 | tf_op jit(solution)/shard_map/all_to_all | solution.py:89
  37.4 4.2 %convert_reduce_fusion = f32[2,512]{1,0:T(2,128)S(1)} fusion(bf16[144,8,2,512]{3,0,2,1:T(8,128)(2,1)} %bitcast.4), kind=kLoop, calls=%fused_computation.59 | loop fusion | flops 2358272 | bytes 2363392 | tf_op jit(solution)/shard_map/reduce_sum | solution.py:44
  41.6 4.1 %copy.35 = bf16[144,8,2,512]{3,2,0,1:T(2,128)(2,1)S(1)} copy(bf16[144,8,2,512]{3,0,2,1:T(8,128)(2,1)} %bitcast.4) | data formatting | bytes 4718592 | tf_op jit(solution)/shard_map/all_to_all | solution.py:89
  45.7 2.0 %copy.41 = bf16[144,8,2,512]{3,1,2,0:T(8,128)(2,1)} copy(bf16[144,8,2,512]{3,2,1,0:T(2,128)(2,1)S(1)} %bitcast.37) | data formatting | bytes 4718592
  47.7 4.4 %copy.36 = bf16[1152,1024]{0,1:T(8,128)(2,1)} copy(bf16[1152,1024]{1,0:T(8,128)(2,1)} %bitcast.33) | data formatting | bytes 4718592 | tf_op jit(solution)/shard_map/reshape | solution.py:38
  52.1 8.6 %gather_fusion = bf16[1152,1024]{1,0:T(8,128)(2,1)} fusion(bf16[1152,1024]{1,0:T(8,128)(2,1)} %bitcast.34, s32[2048]{0:T(1024)S(1)} %pad_clamp_fusion), kind=kCustom, calls=%fused_computation | custom fusion | bytes 4723200 | tf_op jit(solution)/shard_map/jit(_take)/gather | solution.py:40
  60.7 12.2 %fusion.29 = bf16[1152,1024]{0,1:T(8,128)(2,1)} fusion(bf16[1152,1024]{0,1:T(8,128)(2,1)} %copy.36, bf16[1152,1152]{1,0:T(8,128)(2,1)S(1)} %copy-done, f32[1024]{0:T(1024)S(1)} %bitcast.57, f32[1152]{0:T(1024)S(1)} %copy-done.11, bf16[1152,1152]{1,0:T(8,128)(2,1)} %param.17, bf16[1152,1024]{1,0:T(8,128)(2,1)} %bitcast.35, ...), kind=kOutput, calls=%fused_computation.58 | convolution fusion | flops 5446434816 | bytes 14755456 | tf_op jit(solution)/shard_map/dot_general | solution.py:42
  72.9 6.8 %copy.37 = bf16[1152,2,512]{2,1,0:T(2,128)(2,1)} copy(bf16[1152,2,512]{0,2,1:T(8,128)(2,1)} %bitcast.38) | data formatting | bytes 4718592 | tf_op jit(solution)/shard_map/reshape | solution.py:46
  79.7 5.8 %all-to-all-start.1 = ((bf16[1152,2,512]{2,1,0:T(2,128)(2,1)}), bf16[1152,2,512]{2,1,0:T(2,128)(2,1)}, u32[]{:S(2)}, u32[]{:S(2)}) async-start(bf16[1152,2,512]{2,1,0:T(2,128)(2,1)} %copy.37), calls=%async_computation.1 | async-start | bytes 4718592 | tf_op jit(solution)/shard_map/all_to_all | solution.py:87
  86.3 27.2 %all-to-all-done.1 = bf16[1152,2,512]{2,1,0:T(2,128)(2,1)} async-done(((bf16[1152,2,512]{2,1,0:T(2,128)(2,1)}), bf16[1152,2,512]{2,1,0:T(2,128)(2,1)}, u32[]{:S(2)}, u32[]{:S(2)}) %all-to-all-start.1) | async-done | bytes 2359328 | tf_op jit(solution)/shard_map/all_to_all | solution.py:87
  113.6 2.0 %copy.38 = bf16[1152,2,512]{2,0,1:T(8,128)(2,1)S(1)} copy(bf16[1152,2,512]{2,1,0:T(2,128)(2,1)} %all-to-all-done.1) | data formatting | bytes 4718592 | tf_op jit(solution)/shard_map/all_to_all | solution.py:87
  118.0 2.4 %fusion.16 = f32[144,16,512]{2,0,1:T(8,128)S(1)} fusion(f32[144,8,2,512]{3,0,2,1:T(8,128)S(1)} %copy.39, f32[144]{0:T(256)S(1)} %get-tuple-element.22, f32[16,512]{1,0:T(8,128)S(1)} %mul.117, f32[144]{0:T(256)S(1)} %get-tuple-element.21, f32[16,512]{1,0:T(8,128)S(1)} %mul.108, f32[144]{0:T(256)S(1)} %copy-done.8, bf16[144,16,512]{2,1,0:T(8,128)(2,1)S(1)} %copy-done.2), kind=kLoop, calls=%fused_computation.35 | loop fusion | flops 10616832 | bytes 11863744 | tf_op jit(solution)/shard_map/add | solution.py:100
  120.4 2.4 %collective-permute-start.1 = (f32[144,1,512]{2,0,1:T(8,128)S(1)}, f32[144,1,512]{2,0,1:T(8,128)S(1)}, u32[]{:S(2)}, u32[]{:S(2)}) collective-permute-start(f32[144,1,512]{2,0,1:T(8,128)S(1)} %get-tuple-element.13), channel_id=1, source_target_pairs={{1,0},{2,1},{3,2},{5,4},{6,5},{7,6},{9,8},{10,9},{11,10},{13,12},{... | collective-permute-start | bytes 884744 | tf_op jit(solution)/shard_map/ppermute | solution.py:19
  124.0 1.9 fusion.1
  125.9 3.3 %collective-permute-done.1 = f32[144,1,512]{2,0,1:T(8,128)S(1)} collective-permute-done((f32[144,1,512]{2,0,1:T(8,128)S(1)}, f32[144,1,512]{2,0,1:T(8,128)S(1)}, u32[]{:S(2)}, u32[]{:S(2)}) %collective-permute-start.1) | collective-permute-done | bytes 294944 | tf_op jit(solution)/shard_map/ppermute | solution.py:19
  129.2 4.1 %collective-permute-done = f32[144,1,512]{2,0,1:T(8,128)S(1)} collective-permute-done((f32[144,1,512]{2,0,1:T(8,128)S(1)}, f32[144,1,512]{2,0,1:T(8,128)S(1)}, u32[]{:S(2)}, u32[]{:S(2)}) %collective-permute-start) | collective-permute-done | bytes 294944 | tf_op jit(solution)/shard_map/ppermute | solution.py:16
  134.9 2.4 %fusion.27 = f32[144,16,512]{2,0,1:T(8,128)S(1)} fusion(f32[144,17,512]{2,0,1:T(8,128)S(1)} %fusion.12, f32[144,16,512]{2,0,1:T(8,128)S(1)} %fusion.16, f32[144,16,513]{2,0,1:T(8,128)S(1)} %fusion.1, f32[16,512]{1,0:T(8,128)S(1)} %convert_element_type.57), kind=kLoop, calls=%fused_computation.53 | loop fusion | flops 5898240 | bytes 28344320 | tf_op jit(solution)/shard_map/mul | solution.py:61
  137.3 2.4 %collective-permute-start.3 = (f32[144,1,512]{2,0,1:T(8,128)S(1)}, f32[144,1,512]{2,0,1:T(8,128)S(1)}, u32[]{:S(2)}, u32[]{:S(2)}) collective-permute-start(f32[144,1,512]{2,0,1:T(8,128)S(1)} %get-tuple-element.11), channel_id=1, source_target_pairs={{1,0},{2,1},{3,2},{5,4},{6,5},{7,6},{9,8},{10,9},{11,10},{13,12},{... | collective-permute-start | bytes 884744 | tf_op jit(solution)/shard_map/ppermute | solution.py:19
  141.0 3.6 %fusion.4 = f32[144,16,513]{2,0,1:T(8,128)} fusion(f32[144,16,512]{2,0,1:T(8,128)S(1)} %fusion.27, f32[144]{0:T(256)S(1)} %bitcast.54, f32[144]{0:T(256)S(1)} %bitcast.50), kind=kLoop, calls=%fused_computation.14 | loop fusion | flops 3545856 | bytes 9447552 | tf_op jit(solution)/shard_map/add | solution.py:58
  145.0 4.1 %collective-permute-done.2 = f32[144,1,512]{2,0,1:T(8,128)S(1)} collective-permute-done((f32[144,1,512]{2,0,1:T(8,128)S(1)}, f32[144,1,512]{2,0,1:T(8,128)S(1)}, u32[]{:S(2)}, u32[]{:S(2)}) %collective-permute-start.2) | collective-permute-done | bytes 294944 | tf_op jit(solution)/shard_map/ppermute | solution.py:16
  150.7 5.5 %fusion.24 = f32[144,16,512]{2,0,1:T(8,128)S(1)} fusion(f32[144,17,512]{2,0,1:T(8,128)S(1)} %fusion.13, f32[144,16,512]{2,0,1:T(8,128)S(1)} %fusion.27, f32[144,16,513]{2,0,1:T(8,128)} %fusion.4, f32[16,512]{1,0:T(8,128)S(1)} %convert_element_type.57), kind=kLoop, calls=%fused_computation.48 | loop fusion | flops 5898240 | bytes 28344320 | tf_op jit(solution)/shard_map/mul | solution.py:61
  156.3 2.5 %collective-permute-start.5 = (f32[144,1,512]{2,0,1:T(8,128)S(1)}, f32[144,1,512]{2,0,1:T(8,128)S(1)}, u32[]{:S(2)}, u32[]{:S(2)}) collective-permute-start(f32[144,1,512]{2,0,1:T(8,128)S(1)} %get-tuple-element.9), channel_id=1, source_target_pairs={{1,0},{2,1},{3,2},{5,4},{6,5},{7,6},{9,8},{10,9},{11,10},{13,12},{... | collective-permute-start | bytes 884744 | tf_op jit(solution)/shard_map/ppermute | solution.py:19
  160.3 3.6 %fusion.7 = f32[144,16,513]{2,0,1:T(8,128)} fusion(f32[144,16,512]{2,0,1:T(8,128)S(1)} %fusion.24, f32[144]{0:T(256)S(1)} %bitcast.55, f32[144]{0:T(256)S(1)} %bitcast.51), kind=kLoop, calls=%fused_computation.17 | loop fusion | flops 3545856 | bytes 9447552 | tf_op jit(solution)/shard_map/add | solution.py:58
  164.0 3.5 %collective-permute-done.4 = f32[144,1,512]{2,0,1:T(8,128)S(1)} collective-permute-done((f32[144,1,512]{2,0,1:T(8,128)S(1)}, f32[144,1,512]{2,0,1:T(8,128)S(1)}, u32[]{:S(2)}, u32[]{:S(2)}) %collective-permute-start.4) | collective-permute-done | bytes 294944 | tf_op jit(solution)/shard_map/ppermute | solution.py:16
  169.0 5.5 %fusion.21 = f32[144,16,512]{2,0,1:T(8,128)S(1)} fusion(f32[144,17,512]{2,0,1:T(8,128)S(1)} %fusion.14, f32[144,16,512]{2,0,1:T(8,128)S(1)} %fusion.24, f32[144,16,513]{2,0,1:T(8,128)} %fusion.7, f32[16,512]{1,0:T(8,128)S(1)} %convert_element_type.57), kind=kLoop, calls=%fused_computation.43 | loop fusion | flops 5898240 | bytes 28344320 | tf_op jit(solution)/shard_map/mul | solution.py:61
  174.6 2.4 %collective-permute-start.7 = (f32[144,1,512]{2,0,1:T(8,128)S(1)}, f32[144,1,512]{2,0,1:T(8,128)S(1)}, u32[]{:S(2)}, u32[]{:S(2)}) collective-permute-start(f32[144,1,512]{2,0,1:T(8,128)S(1)} %get-tuple-element.7), channel_id=1, source_target_pairs={{1,0},{2,1},{3,2},{5,4},{6,5},{7,6},{9,8},{10,9},{11,10},{13,12},{... | collective-permute-start | bytes 884744 | tf_op jit(solution)/shard_map/ppermute | solution.py:19
  178.3 1.9 fusion.10
  181.2 4.4 %collective-permute-done.6 = f32[144,1,512]{2,0,1:T(8,128)S(1)} collective-permute-done((f32[144,1,512]{2,0,1:T(8,128)S(1)}, f32[144,1,512]{2,0,1:T(8,128)S(1)}, u32[]{:S(2)}, u32[]{:S(2)}) %collective-permute-start.6) | collective-permute-done | bytes 294944 | tf_op jit(solution)/shard_map/ppermute | solution.py:16
  187.2 2.5 %fusion.18 = f32[144,16,512]{2,0,1:T(8,128)S(1)} fusion(f32[144,17,512]{2,0,1:T(8,128)S(1)} %fusion.15, f32[144,16,512]{2,0,1:T(8,128)S(1)} %fusion.21, f32[144,16,513]{2,0,1:T(8,128)S(1)} %fusion.10, f32[16,512]{1,0:T(8,128)S(1)} %convert_element_type.57), kind=kLoop, calls=%fused_computation.38 | loop fusion | flops 5898240 | bytes 28344320 | tf_op jit(solution)/shard_map/mul | solution.py:61
  189.6 4.9 %copy.40 = f32[144,16,512]{2,1,0:T(8,128)} copy(f32[144,16,512]{2,0,1:T(8,128)S(1)} %fusion.18) | data formatting | bytes 9437184 | tf_op jit(solution)/shard_map/mul | solution.py:61
  (58 shorter events, 16.2 us)
Async XLA Ops:
  0.0 60.7 %copy-start = (bf16[1152,1152]{1,0:T(8,128)(2,1)S(1)}, bf16[1152,1152]{1,0:T(8,128)(2,1)}, u32[]{:S(2)}) copy-start(bf16[1152,1152]{1,0:T(8,128)(2,1)} %param.18) | copy-start | bytes 7962628
  0.0 9.3 %copy-start.3 = (s32[1152]{0:T(1024)S(1)}, s32[1152]{0:T(1024)}, u32[]{:S(2)}) copy-start(s32[1152]{0:T(1024)} %param.19) | copy-start | bytes 13828
  4.5 32.9 %all-to-all-start = ((bf16[144,16,512]{2,0,1:T(8,128)(2,1)}), bf16[144,16,512]{2,0,1:T(8,128)(2,1)}, u32[]{:S(2)}, u32[]{:S(2)}) async-start(bf16[144,16,512]{2,0,1:T(8,128)(2,1)} %copy.33), calls=%async_computation | async-start | bytes 4718592 | tf_op jit(solution)/shard_map/all_to_all | solution.py:89
  52.1 8.6 %copy-start.11 = (f32[1152]{0:T(1024)S(1)}, f32[1152]{0:T(1024)}, u32[]{:S(2)}) copy-start(f32[1152]{0:T(1024)} %param.16) | copy-start | bytes 13828
  72.9 12.6 %copy-start.4 = (s32[16,512]{1,0:T(8,128)S(1)}, s32[16,512]{1,0:T(8,128)}, u32[]{:S(2)}) copy-start(s32[16,512]{1,0:T(8,128)} %param.23) | copy-start | bytes 98308
  72.9 12.7 %copy-start.10 = (f32[8,2]{0,1:T(2,128)S(1)}, f32[8,2]{0,1:T(2,128)}, u32[]{:S(2)}) copy-start(f32[8,2]{0,1:T(2,128)} %param.20) | copy-start | bytes 196
  72.9 12.7 %copy-start.6 = (s32[8,32]{1,0:T(8,128)S(1)}, s32[8,32]{1,0:T(8,128)}, u32[]{:S(2)}) copy-start(s32[8,32]{1,0:T(8,128)} %param.21) | copy-start | bytes 3076
  72.9 12.8 %copy-start.5 = (s32[8,32]{1,0:T(8,128)S(1)}, s32[8,32]{1,0:T(8,128)}, u32[]{:S(2)}) copy-start(s32[8,32]{1,0:T(8,128)} %param.22) | copy-start | bytes 3076
  72.9 13.4 %copy-start.9 = (f32[144]{0:T(256)S(1)}, f32[144]{0:T(256)}, u32[]{:S(2)}) copy-start(f32[144]{0:T(256)} %param.13) | copy-start | bytes 1732
  72.9 13.4 %copy-start.7 = (f32[144,2]{0,1:T(2,128)S(1)}, f32[144,2]{0,1:T(2,128)}, u32[]{:S(2)}) copy-start(f32[144,2]{0,1:T(2,128)} %param.15) | copy-start | bytes 3460
  79.7 33.9 %all-to-all-start.1 = ((bf16[1152,2,512]{2,1,0:T(2,128)(2,1)}), bf16[1152,2,512]{2,1,0:T(2,128)(2,1)}, u32[]{:S(2)}, u32[]{:S(2)}) async-start(bf16[1152,2,512]{2,1,0:T(2,128)(2,1)} %copy.37), calls=%async_computation.1 | async-start | bytes 4718592 | tf_op jit(solution)/shard_map/all_to_all | solution.py:87
  116.3 1.7 copy-start.2
  116.3 1.7 copy-start.8
  120.4 8.8 %collective-permute-start.1 = (f32[144,1,512]{2,0,1:T(8,128)S(1)}, f32[144,1,512]{2,0,1:T(8,128)S(1)}, u32[]{:S(2)}, u32[]{:S(2)}) collective-permute-start(f32[144,1,512]{2,0,1:T(8,128)S(1)} %get-tuple-element.13), channel_id=1, source_target_pairs={{1,0},{2,1},{3,2},{5,4},{6,5},{7,6},{9,8},{10,9},{11,10},{13,12},{... | collective-permute-start | bytes 884744 | tf_op jit(solution)/shard_map/ppermute | solution.py:19
  122.7 10.6 %collective-permute-start = (f32[144,1,512]{2,0,1:T(8,128)S(1)}, f32[144,1,512]{2,0,1:T(8,128)S(1)}, u32[]{:S(2)}, u32[]{:S(2)}) collective-permute-start(f32[144,1,512]{2,0,1:T(8,128)S(1)} %get-tuple-element.14), channel_id=1, source_target_pairs={{0,1},{1,2},{2,3},{4,5},{5,6},{6,7},{8,9},{9,10},{10,11},{12,13},{... | collective-permute-start | bytes 884744 | tf_op jit(solution)/shard_map/ppermute | solution.py:16
  137.3 7.7 %collective-permute-start.3 = (f32[144,1,512]{2,0,1:T(8,128)S(1)}, f32[144,1,512]{2,0,1:T(8,128)S(1)}, u32[]{:S(2)}, u32[]{:S(2)}) collective-permute-start(f32[144,1,512]{2,0,1:T(8,128)S(1)} %get-tuple-element.11), channel_id=1, source_target_pairs={{1,0},{2,1},{3,2},{5,4},{6,5},{7,6},{9,8},{10,9},{11,10},{13,12},{... | collective-permute-start | bytes 884744 | tf_op jit(solution)/shard_map/ppermute | solution.py:19
  139.7 9.4 %collective-permute-start.2 = (f32[144,1,512]{2,0,1:T(8,128)S(1)}, f32[144,1,512]{2,0,1:T(8,128)S(1)}, u32[]{:S(2)}, u32[]{:S(2)}) collective-permute-start(f32[144,1,512]{2,0,1:T(8,128)S(1)} %get-tuple-element.12), channel_id=1, source_target_pairs={{0,1},{1,2},{2,3},{4,5},{5,6},{6,7},{8,9},{9,10},{10,11},{12,13},{... | collective-permute-start | bytes 884744 | tf_op jit(solution)/shard_map/ppermute | solution.py:16
  156.3 7.7 %collective-permute-start.5 = (f32[144,1,512]{2,0,1:T(8,128)S(1)}, f32[144,1,512]{2,0,1:T(8,128)S(1)}, u32[]{:S(2)}, u32[]{:S(2)}) collective-permute-start(f32[144,1,512]{2,0,1:T(8,128)S(1)} %get-tuple-element.9), channel_id=1, source_target_pairs={{1,0},{2,1},{3,2},{5,4},{6,5},{7,6},{9,8},{10,9},{11,10},{13,12},{... | collective-permute-start | bytes 884744 | tf_op jit(solution)/shard_map/ppermute | solution.py:19
  158.8 8.6 %collective-permute-start.4 = (f32[144,1,512]{2,0,1:T(8,128)S(1)}, f32[144,1,512]{2,0,1:T(8,128)S(1)}, u32[]{:S(2)}, u32[]{:S(2)}) collective-permute-start(f32[144,1,512]{2,0,1:T(8,128)S(1)} %get-tuple-element.10), channel_id=1, source_target_pairs={{0,1},{1,2},{2,3},{4,5},{5,6},{6,7},{8,9},{9,10},{10,11},{12,13},{... | collective-permute-start | bytes 884744 | tf_op jit(solution)/shard_map/ppermute | solution.py:16
  174.6 6.6 %collective-permute-start.7 = (f32[144,1,512]{2,0,1:T(8,128)S(1)}, f32[144,1,512]{2,0,1:T(8,128)S(1)}, u32[]{:S(2)}, u32[]{:S(2)}) collective-permute-start(f32[144,1,512]{2,0,1:T(8,128)S(1)} %get-tuple-element.7), channel_id=1, source_target_pairs={{1,0},{2,1},{3,2},{5,4},{6,5},{7,6},{9,8},{10,9},{11,10},{13,12},{... | collective-permute-start | bytes 884744 | tf_op jit(solution)/shard_map/ppermute | solution.py:19
  177.0 8.6 %collective-permute-start.6 = (f32[144,1,512]{2,0,1:T(8,128)S(1)}, f32[144,1,512]{2,0,1:T(8,128)S(1)}, u32[]{:S(2)}, u32[]{:S(2)}) collective-permute-start(f32[144,1,512]{2,0,1:T(8,128)S(1)} %get-tuple-element.8), channel_id=1, source_target_pairs={{0,1},{1,2},{2,3},{4,5},{5,6},{6,7},{8,9},{9,10},{10,11},{12,13},{... | collective-permute-start | bytes 884744 | tf_op jit(solution)/shard_map/ppermute | solution.py:16
  187.2 7.4 %copy-start.1 = (bf16[1152,1152]{1,0:T(8,128)(2,1)S(1)}, bf16[1152,1152]{1,0:T(8,128)(2,1)}, u32[]{:S(2)}) copy-start(bf16[1152,1152]{1,0:T(8,128)(2,1)} %param.18) | copy-start | bytes 7962628
where the time goes:
time: 195 us
  waiting for transfers between devices  76 us (39%)
  other arithmetic  40.5 us (21%)
  local copies, waits for them, and re-layouts  39.9 us (20%)
  starting transfers between devices  25.6 us (13%)
  matrix products  12.2 us (6%)
    all_to_all x1, waiting for transfers between devices, per_device(): lax.all_to_all(energy, 'comp', split_axis=1, concat_axis=0, tiled=True)  28 us
    all_to_all x1, waiting for transfers between devices, per_device(): lax.all_to_all(cell_terms(lax.all_to_all(energy, 'comp', split_axis=1, co...  27.2 us
    ppermute x4, waiting for transfers between devices, with_halo(): lax.ppermute(lax.slice_in_dim(block, block.shape[dim] - width, None, axis...  16.1 us
    mul x4, other arithmetic, advect(): (center - (flux_x[..., 1:] - flux_x[..., :-1]) - (flux_y[..., 1:, :] - fl...  15.9 us
    dot_general x1, matrix products, cell_terms(): nonlinear = jnp.dot(transfer, product, preferred_element_type=jnp.float32)  12.2 us
    add x4, other arithmetic, advect(): jnp.maximum(courant_x, 0.0) * padded_x[..., :-1]  11 us
    ppermute x4, starting transfers between devices, with_halo(): lax.ppermute(lax.slice_in_dim(block, 0, width, axis=dim), axis, backward)  9.67 us
    gather x1, local copies, waits for them, and re-layouts, cell_terms(): partner = jnp.take(flattened, pattern, axis=0)  8.59 us
  transfers between devices with their start and end apart: 10, of which 9 were waited for; matrix products, arithmetic and copies ran while one was open for 6% of the time, Pallas kernels for 0%

commit v1 on v0

--- a/solution.py
+++ b/solution.py
@@ -1,11 +1,17 @@
+import functools
 import jax
 import jax.numpy as jnp
 from jax import lax
+from jax.experimental import pallas as pl
+from jax.experimental.pallas import tpu as pltpu
 from jax.sharding import PartitionSpec as P
 
 SUBSTEPS = 4
 TILE_ROWS = 2
 TILE_COLS = 16
+GROUP = 16
+LANES = 128
+MIB = 1 << 20
 
 
 def with_halo(block, sides, width):
@@ -106,6 +112,365 @@
         energy_field = advect(padded, sea_field, courant_x, courant_y)
     return energy_field
 
+def exchange(value, axis, distance):
+    count = lax.axis_size(axis)
+    return lax.ppermute(value, axis, [(i, i ^ distance) for i in range(count)])
+
+
+def spread_kernel(where, energy_ref, *refs):
+    outs, wide = refs[:-1], refs[-1]
+    group, rows, width = energy_ref.shape
+    per_chip = rows // len(outs)
+    for block in range(width // LANES):
+        lanes = slice(block * LANES, (block + 1) * LANES)
+        wide[block] = (
+            energy_ref[:, :, lanes].astype(jnp.float32).reshape(group * rows, LANES)
+        )
+    for m, out_ref in enumerate(outs):
+        first = per_chip * jnp.bitwise_xor(where[0], m)
+        for row in range(per_chip):
+            for block in range(width // LANES):
+                start = row * width + block * LANES
+                picked = wide[block, pl.ds(first + row, group, stride=rows), :]
+                out_ref[:, start : start + LANES] = picked.astype(jnp.bfloat16)
+
+
+def spread(where, energy, chips):
+    local, rows, width = energy.shape
+    cells = rows // chips * width
+    block = 3 * GROUP
+    return pl.pallas_call(
+        spread_kernel,
+        grid_spec=pltpu.PrefetchScalarGridSpec(
+            num_scalar_prefetch=1,
+            grid=(local // block,),
+            in_specs=[pl.BlockSpec((block, rows, width), lambda i, w: (i, 0, 0))],
+            out_specs=[pl.BlockSpec((block, cells), lambda i, w: (i, 0))] * chips,
+            scratch_shapes=[pltpu.VMEM((width // LANES, block * rows, LANES), jnp.float32)],
+        ),
+        out_shape=[jax.ShapeDtypeStruct((local, cells), jnp.bfloat16)] * chips,
+        compiler_params=pltpu.CompilerParams(vmem_limit_bytes=24 * MIB),
+        cost_estimate=pl.CostEstimate(
+            flops=energy.size, bytes_accessed=4 * energy.size, transcendentals=0
+        ),
+        name="spread",
+    )(where, energy)
+
+
+def weights_kernel(
+    chips, where, column_ref, row_ref, mixing_ref, transfer_ref, first_ref, second_ref, pick, pick_t
+):
+    total = mixing_ref.shape[0]
+    local = total // (2 * chips)
+    tile = 384 if total % 384 == 0 else total
+    pick[...] = (
+        column_ref[...] == lax.broadcasted_iota(jnp.int32, (total, total), 1)
+    ).astype(jnp.bfloat16)
+    pick_t[...] = (
+        row_ref[...] == lax.broadcasted_iota(jnp.int32, (total, total), 0)
+    ).astype(jnp.bfloat16)
+
+    for start in range(0, total, tile):
+        first_ref[pl.ds(start, tile), :] = jnp.dot(
+            pick_t[pl.ds(start, tile), :], mixing_ref[...], preferred_element_type=jnp.float32
+        ).astype(jnp.bfloat16)
+    extra = first_ref.shape[0] - total
+    first_ref[pl.ds(total, extra), :] = jnp.ones((extra, total), jnp.bfloat16)
+    for m in range(chips):
+        block = 2 * jnp.bitwise_xor(where[0], m) + where[1]
+        rows = transfer_ref[pl.ds(pl.multiple_of(block * local, GROUP), local), :]
+        second_ref[pl.ds(m * local, local), :] = jnp.dot(
+            rows, pick[...], preferred_element_type=jnp.float32
+        ).astype(jnp.bfloat16)
+
+
+def weights(where, pattern, mixing, transfer, chips):
+    total = mixing.shape[0]
+    whole = pl.BlockSpec(memory_space=pltpu.VMEM)
+    return pl.pallas_call(
+        functools.partial(weights_kernel, chips),
+        in_specs=[pl.BlockSpec(memory_space=pltpu.SMEM)] + [whole] * 4,
+        out_specs=[whole, whole],
+        out_shape=[
+            jax.ShapeDtypeStruct((total + GROUP, total), jnp.bfloat16),
+            jax.ShapeDtypeStruct((total // 2, total), jnp.bfloat16),
+        ],
+        scratch_shapes=[pltpu.VMEM((total, total), jnp.bfloat16)] * 2,
+        compiler_params=pltpu.CompilerParams(vmem_limit_bytes=32 * MIB),
+        cost_estimate=pl.CostEstimate(
+            flops=3 * total**3, bytes_accessed=8 * total**2, transcendentals=0
+        ),
+        name="weights",
+    )(where, pattern[:, None], pattern[None, :], mixing, transfer)
+
+
+def terms_kernel(chips, chunks, tile, where, first_ref, second_ref, dissip_ref, *refs):
+    pieces = refs[: 2 * chips]
+    outs = refs[2 * chips : -4]
+    spectra, product, mixed, sems = refs[-4:]
+    total, cells = spectra.shape
+    local = total // (2 * chips)
+    part = local // chunks
+
+    def start_of(m, other):
+        core = jnp.bitwise_xor(where[1], other)
+        block = 2 * jnp.bitwise_xor(where[0], m) + core
+        return pl.multiple_of(block * local, GROUP)
+
+    copies = []
+    for m in range(chips):
+        for other in range(2):
+            index = 2 * m + other
+            copies.append(
+                pltpu.make_async_copy(
+                    pieces[m if other == 0 else chips + m],
+                    spectra.at[pl.ds(start_of(m, other), local), :],
+                    sems.at[index],
+                )
+            )
+    for copy in copies:
+        copy.start()
+    for copy in copies:
+        copy.wait()
+
+    @pl.loop(0, cells // tile)
+    def _(step):
+        columns = pl.ds(pl.multiple_of(step * tile, tile), tile)
+        mixed[...] = jnp.dot(
+            first_ref[...], spectra[:, columns], preferred_element_type=jnp.float32
+        )
+        product[...] = (
+            mixed[pl.ds(0, total), :] * spectra[:, columns].astype(jnp.float32)
+        ).astype(jnp.bfloat16)
+        mean = mixed[pl.ds(total, 1), :] * (1.0 / total)
+        for m in range(chips):
+            rows = pl.ds(start_of(m, 0), local)
+            nonlinear = jnp.dot(
+                second_ref[pl.ds(m * local, local), :],
+                product[...],
+                preferred_element_type=jnp.float32,
+            )
+            own = spectra[rows, columns].astype(jnp.float32)
+            result = (nonlinear - dissip_ref[rows, :] * mean * own).astype(jnp.bfloat16)
+            for j in range(chunks):
+                outs[m * chunks + j][:, columns] = result[j * part : (j + 1) * part]
+
+
+def source_terms(where, first, second, dissip, near, far, chunks):
+    chips = len(near)
+    local, cells = near[0].shape
+    total = 2 * chips * local
+    tile = 256
+    whole = pl.BlockSpec(memory_space=pltpu.VMEM)
+    outs = pl.pallas_call(
+        functools.partial(terms_kernel, chips, chunks, tile),
+        in_specs=[pl.BlockSpec(memory_space=pltpu.SMEM)]
+        + [whole] * 3
+        + [pl.BlockSpec(memory_space=pl.ANY)] * (2 * chips),
+        out_specs=[whole] * (chips * chunks),
+        out_shape=[jax.ShapeDtypeStruct((local // chunks, cells), jnp.bfloat16)]
+        * (chips * chunks),
+        scratch_shapes=[
+            pltpu.VMEM((total, cells), jnp.bfloat16),
+            pltpu.VMEM((total, tile), jnp.bfloat16),
+            pltpu.VMEM((total + GROUP, tile), jnp.float32),
+            pltpu.SemaphoreType.DMA((2 * chips,)),
+        ],
+        compiler_params=pltpu.CompilerParams(vmem_limit_bytes=32 * MIB),
+        cost_estimate=pl.CostEstimate(
+            flops=3 * total * total * cells, bytes_accessed=8 * total * cells, transcendentals=0
+        ),
+        name="source_terms",
+    )(where, first, second, dissip[:, None], *near, *far)
+    return [outs[m * chunks : (m + 1) * chunks] for m in range(chips)]
+
+
+def propagate_kernel(chips, halo, where, coef_ref, wind_ref, mask_ref, *refs):
+    count = chips + 2
+    energies, terms = refs[:count], refs[count : 2 * count]
+    out_ref, field, turned = refs[-3:]
+    rows, group, width = field.shape
+    inner = rows - 2 * halo
+    per_chip = inner // chips
+
+    def column(index):
+        return jnp.broadcast_to(coef_ref[:, index : index + 1], (group, width))
+
+    def force(energy_ref, term_ref, first, number):
+        for row in range(number):
+            here = first + row
+            lanes = slice(row * width, (row + 1) * width)
+            level = energy_ref[:, lanes].astype(jnp.float32)
+            drive = (
+                wind_ref[0, pl.ds(here, 1), :] * column(0)
+                + wind_ref[1, pl.ds(here, 1), :] * column(1)
+            )
+            field[here] = level * (1.0 + jnp.maximum(drive, 0.0)) + term_ref[:, lanes].astype(
+                jnp.float32
+            )
+
+    for m in range(chips):
+        force(energies[m], terms[m], halo + per_chip * jnp.bitwise_xor(where[0], m), per_chip)
+    force(energies[chips], terms[chips], 0, halo)
+    force(energies[chips + 1], terms[chips + 1], halo + inner, halo)
+
+    lane = lax.broadcasted_iota(jnp.int32, (group, width), 1)
+    for substep in range(1, halo + 1):
+        before = field[substep - 1]
+        center = field[substep]
+        for row in range(substep, rows - substep):
+            after = field[row + 1]
+            west = jnp.where(lane == 0, 0.0, pltpu.roll(center, 1, 1))
+            east = jnp.where(lane == width - 1, 0.0, pltpu.roll(center, width - 1, 1))
+            value = (
+                center * column(2)
+                + west * column(3)
+                + east * column(4)
+                + before * column(5)
+                + after * column(6)
+            ) * mask_ref[pl.ds(row, 1), :]
+            if substep < halo:
+                field[row] = value
+            else:
+                for block in range(width // LANES):
+                    lanes = slice(block * LANES, (block + 1) * LANES)
+                    turned[block, pl.ds(row - halo, group, stride=inner), :] = value[:, lanes]
+            before, center = center, after
+    for block in range(width // LANES):
+        out_ref[:, block * LANES : (block + 1) * LANES] = turned[block]
+
+
+def propagate(where, coef, winds, mask, energies, terms, chunk, chunks, previous, halo):
+    chips = len(energies) - 2
+    local = energies[0].shape[0]
+    rows, width = mask.shape
+    inner = rows - 2 * halo
+    steps = local // chunks // GROUP
+    base = chunk * steps
+    cells, edge = energies[0].shape[1], energies[-1].shape[1]
+    shape = jax.ShapeDtypeStruct((local * inner, width), jnp.float32)
+    in_specs = (
+        [
+            pl.BlockSpec((GROUP, coef.shape[1]), lambda i, w: (base + i, 0)),
+            pl.BlockSpec(winds.shape, lambda i, w: (0, 0, 0)),
+            pl.BlockSpec(mask.shape, lambda i, w: (0, 0)),
+        ]
+        + [pl.BlockSpec((GROUP, cells), lambda i, w: (base + i, 0))] * chips
+        + [pl.BlockSpec((GROUP, edge), lambda i, w: (base + i, 0))] * 2
+        + [pl.BlockSpec((GROUP, cells), lambda i, w: (i, 0))] * chips
+        + [pl.BlockSpec((GROUP, edge), lambda i, w: (i, 0))] * 2
+    )
+    operands = [where, coef, winds, mask, *energies, *terms]
+    aliases = {}
+    kernel = functools.partial(propagate_kernel, chips, halo)
+    if previous is not None:
+        aliases = {len(operands): 0}
+        operands.append(previous)
+        in_specs.append(pl.BlockSpec(memory_space=pl.ANY))
+    return pl.pallas_call(
+        kernel,
+        grid_spec=pltpu.PrefetchScalarGridSpec(
+            num_scalar_prefetch=1,
+            grid=(steps,),
+            in_specs=in_specs,
+            out_specs=pl.BlockSpec((GROUP * inner, width), lambda i, w: (base + i, 0)),
+            scratch_shapes=[
+                pltpu.VMEM((rows, GROUP, width), jnp.float32),
+                pltpu.VMEM((width // LANES, GROUP * inner, LANES), jnp.float32),
+            ],
+        ),
+        out_shape=shape,
+        input_output_aliases=aliases,
+        compiler_params=pltpu.CompilerParams(vmem_limit_bytes=24 * MIB),
+        cost_estimate=pl.CostEstimate(
+            flops=60 * shape.size // chunks,
+            bytes_accessed=8 * shape.size // chunks,
+            transcendentals=0,
+        ),
+        name="propagate",
+    )(*operands)
+
+
+def chosen(values, index):
+    result = values[0]
+    for m in range(1, len(values)):
+        result = jnp.where(index == m, values[m], result)
+    return result
+
+
+def from_below(value):
+    count = lax.axis_size("strip")
+    return lax.ppermute(value, "strip", [(i, i + 1) for i in range(count - 1)])
+
+
+def from_above(value):
+    count = lax.axis_size("strip")
+    return lax.ppermute(value, "strip", [(i + 1, i) for i in range(count - 1)])
+
+
+def per_device_paired(
+    energy,
+    heading,
+    growth,
+    courant,
+    dissip,
+    mixing,
+    transfer,
+    pattern,
+    regime_winds,
+    regime,
+    seeds,
+    sea_mask,
+):
+    chips = lax.axis_size("comp") // 2
+    chunks = 3
+    local, rows, width = energy.shape
+    halo = SUBSTEPS
+    me = lax.axis_index("comp")
+    chip = me // 2
+    where = jnp.stack([chip, me % 2]).astype(jnp.int32)
+
+    spread_out = spread(where, energy, chips)
+    near = [spread_out[0]] + [exchange(spread_out[m], "comp", 2 * m) for m in range(1, chips)]
+    far = [exchange(value, "comp", 1) for value in near]
+
+    first, second = weights(where, pattern, mixing, transfer, chips)
+
+    wind_u, wind_v = strip_winds(regime_winds, regime, seeds)
+    fields = jnp.stack([wind_u, wind_v, sea_mask.astype(jnp.float32)])
+    fields = jnp.concatenate(
+        [from_below(fields[:, rows - halo :]), fields, from_above(fields[:, :halo])], axis=1
+    )
+    top, bottom = jnp.bitwise_xor(chip, chips - 1), chip
+    energies = list(spread_out) + [
+        from_below(chosen(spread_out, top)),
+        from_above(chosen(spread_out, bottom)),
+    ]
+    along, across = courant[:, 0], courant[:, 1]
+    coef = jnp.stack(
+        [
+            growth * jnp.cos(heading),
+            growth * jnp.sin(heading),
+            1.0 - jnp.abs(along) - jnp.abs(across),
+            jnp.maximum(along, 0.0),
+            -jnp.minimum(along, 0.0),
+            jnp.maximum(across, 0.0),
+            -jnp.minimum(across, 0.0),
+            jnp.zeros_like(along),
+        ],
+        axis=1,
+    )
+
+    sent = source_terms(where, first, second, dissip, near, far, chunks)
+    result = None
+    for j in range(chunks):
+        terms = [sent[0][j]] + [exchange(sent[m][j], "comp", 2 * m) for m in range(1, chips)]
+        terms = terms + [from_below(chosen(terms, top)), from_above(chosen(terms, bottom))]
+        result = propagate(
+            where, coef, fields[:2], fields[2], energies, terms, j, chunks, result, halo
+        )
+    return result.reshape(local, rows, width)
+
 
 def solution(mesh):
     placed = (
@@ -122,6 +487,8 @@
         P("strip", None),
         P("strip", None),
     )
+    paired = mesh.shape["comp"] == 8
+    body = per_device_paired if paired else per_device
     return jax.shard_map(
-        per_device, mesh=mesh, in_specs=placed, out_specs=P("comp", "strip", None), check_vma=False
-    )
+        body, mesh=mesh, in_specs=placed, out_specs=P("comp", "strip", None), check_vma=False
+    )

time: 195 us -> 161 us (0.83)
  the two profiles are of different devices: /device:TPU:26 before, /device:TPU:8 now
where the time goes in v1:
time: 161 us; the launch traced here: 160 us
  Pallas kernels  64.4 us (40%)
  starting transfers between devices  45.5 us (28%)
  waiting for transfers between devices  25.4 us (16%)
  local copies, waits for them, and re-layouts  17.1 us (11%)
  other arithmetic  7.3 us (5%)
    pallas_call x3, Pallas kernels, propagate(): pl.pallas_call(kernel, grid_spec=pltpu.PrefetchScalarGridSpec(num_scalar_...  35 us
    ppermute x16, waiting for transfers between devices, exchange(): return lax.ppermute(value, axis, [(i, i ^ distance) for i in range(count)])  25.4 us
    pallas_call x1, Pallas kernels, source_terms(): pl.pallas_call(functools.partial(terms_kernel, chips, chunks, tile), in_s...  19.7 us
    ppermute x5, starting transfers between devices, from_below(): return lax.ppermute(value, 'strip', [(i, i + 1) for i in range(count - 1)])  18.8 us
    ppermute x16, starting transfers between devices, exchange(): return lax.ppermute(value, axis, [(i, i ^ distance) for i in range(count)])  16.4 us
    ppermute x5, starting transfers between devices, from_above(): return lax.ppermute(value, 'strip', [(i + 1, i) for i in range(count - 1)])  10.3 us
    unnamed x56, local copies, waits for them, and re-layouts  9.55 us
    pallas_call x1, Pallas kernels, weights(): pl.pallas_call(functools.partial(weights_kernel, chips), in_specs=[pl.Blo...  6.77 us
  transfers between devices with their start and end apart: 26, of which 6 were waited for; matrix products, arithmetic and copies ran while one was open for 9% of the time, Pallas kernels for 31%

profile of v1, /device:TPU:8, one launch (start us, length us, event | category | flops | bytes accessed | tf_op | source)
XLA Modules:
  0.0 160.1 jit_solution(7518892744572367607)
XLA Ops:
  0.1 1.7 %copy-done = bf16[144,16,512]{2,1,0:T(8,128)(2,1)S(1)} copy-done((bf16[144,16,512]{2,1,0:T(8,128)(2,1)S(1)}, bf16[144,16,512]{2,1,0:T(8,128)(2,1)}, u32[]{:S(2)}) %copy-start) | copy-done | bytes 2359320
  1.7 2.8 %spread.1 = (bf16[144,2048]{1,0:T(8,128)(2,1)S(1)}, bf16[144,2048]{1,0:T(8,128)(2,1)S(1)}, bf16[144,2048]{1,0:T(8,128)(2,1)S(1)}, bf16[144,2048]{1,0:T(8,128)(2,1)S(1)}) custom-call(s32[2]{0:T(128)S(1)} %pad_add_fusion.where, bf16[144,16,512]{2,1,0:T(8,128)(2,1)S(1)} %copy-done), custom_call_target="tpu_custom_call" | custom-call | flops 1179648 | bytes 4718592 | tf_op jit(solution)/shard_map/spread/pallas_call | solution.py:142
  4.6 2.5 %collective-permute-start.6 = (bf16[144,2048]{1,0:T(8,128)(2,1)S(1)}, bf16[144,2048]{1,0:T(8,128)(2,1)}, u32[]{:S(2)}, u32[]{:S(2)}) collective-permute-start(bf16[144,2048]{1,0:T(8,128)(2,1)S(1)} %get-tuple-element.26.refs_3_), channel_id=1, source_target_pairs={{0,24},{4,28},{8,16},{12,20},{16,8},{20,12},{24,0},{28,4},{1,25},{... | collective-permute-start | bytes 1769480 | tf_op jit(solution)/shard_map/ppermute | solution.py:117
  8.2 1.2 select_select_fusion
  9.3 3.6 %collective-permute-start.2 = (bf16[144,2048]{1,0:T(8,128)(2,1)}, bf16[144,2048]{1,0:T(8,128)(2,1)S(1)}, u32[]{:S(2)}, u32[]{:S(2)}) collective-permute-start(bf16[144,2048]{1,0:T(8,128)(2,1)} %get-tuple-element.44), channel_id=1, source_target_pairs={{0,1},{1,2},{2,3},{4,5},{5,6},{6,7},{8,9},{9,10},{10,11},{12,13},{... | collective-permute-start | bytes 1769480 | tf_op jit(solution)/shard_map/ppermute | solution.py:403
  14.2 7.8 %collective-permute-done.6.refs_3_ = bf16[144,2048]{1,0:T(8,128)(2,1)} collective-permute-done((bf16[144,2048]{1,0:T(8,128)(2,1)S(1)}, bf16[144,2048]{1,0:T(8,128)(2,1)}, u32[]{:S(2)}, u32[]{:S(2)}) %collective-permute-start.6) | collective-permute-done | bytes 589856 | tf_op jit(solution)/shard_map/ppermute | solution.py:117
  22.0 11.5 %collective-permute-done.4.refs_1_ = bf16[144,2048]{1,0:T(8,128)(2,1)} collective-permute-done((bf16[144,2048]{1,0:T(8,128)(2,1)S(1)}, bf16[144,2048]{1,0:T(8,128)(2,1)}, u32[]{:S(2)}, u32[]{:S(2)}) %collective-permute-start.4) | collective-permute-done | bytes 589856 | tf_op jit(solution)/shard_map/ppermute | solution.py:117
  34.6 1.7 %copy-done.9 = bf16[1152,1152]{1,0:T(8,128)(2,1)S(1)} copy-done((bf16[1152,1152]{1,0:T(8,128)(2,1)S(1)}, bf16[1152,1152]{1,0:T(8,128)(2,1)}, u32[]{:S(2)}) %copy-start.9) | copy-done | bytes 2654232
  36.4 6.8 %weights.1 = (bf16[1168,1152]{1,0:T(8,128)(2,1)S(1)}, bf16[576,1152]{1,0:T(8,128)(2,1)S(1)}) custom-call(s32[2]{0:T(128)S(1)} %pad_add_fusion.where, s32[1152,1]{1,0:T(8,128)S(1)} %broadcast_in_dim.30.column_ref, s32[1,1152]{1,0:T(1,128)S(1)} %broadcast_in_dim.28.row_ref, bf16[1152,1152]{1,0:T(8,128)(2,1)S(1)} %copy-done.8, bf16[1152,1152]{1,0:T(8,128)(2,1)S(1)} %copy-done.9), custom_call_target="tpu_custom_call" | custom-call | flops 4586471424 | bytes 10616832 | tf_op jit(solution)/shard_map/weights/pallas_call | solution.py:190
  43.2 2.4 %collective-permute-start.3 = (bf16[144,2048]{1,0:T(8,128)(2,1)}, bf16[144,2048]{1,0:T(8,128)(2,1)S(1)}, u32[]{:S(2)}, u32[]{:S(2)}) collective-permute-start(bf16[144,2048]{1,0:T(8,128)(2,1)} %get-tuple-element.43), channel_id=1, source_target_pairs={{1,0},{2,1},{3,2},{5,4},{6,5},{7,6},{9,8},{10,9},{11,10},{13,12},{... | collective-permute-start | bytes 1769480 | tf_op jit(solution)/shard_map/ppermute | solution.py:408
  45.6 19.7 %source_terms.1 = (bf16[48,2048]{1,0:T(8,128)(2,1)S(1)}, bf16[48,2048]{1,0:T(8,128)(2,1)S(1)}, bf16[48,2048]{1,0:T(8,128)(2,1)S(1)}, bf16[48,2048]{1,0:T(8,128)(...) custom-call(s32[2]{0:T(128)S(1)} %pad_add_fusion.where, ...), custom_call_target="tpu_custom_call" | custom-call | flops 8153726976 | bytes 18874368 | tf_op jit(solution)/shard_map/source_terms/pallas_call | solution.py:265
  71.4 1.5 collective-permute-start.21
  76.4 1.7 %stack_reshape.6 = f32[1,16,512]{2,1,0:T(8,128)} reshape(f32[16,32,16]{2,1,0:T(8,128)} %broadcast_in_dim.24) | data formatting | bytes 65536 | tf_op jit(solution)/shard_map/stack;reshape | solution.py:440
  78.9 1.7 %stack_reshape.7 = f32[1,16,512]{2,1,0:T(8,128)} reshape(f32[16,32,16]{2,1,0:T(8,128)} %broadcast_in_dim.26) | data formatting | bytes 65536 | tf_op jit(solution)/shard_map/stack;reshape | solution.py:440
  83.5 1.6 collective-permute-start.16
  87.1 1.3 select_select_fusion.2
  88.4 3.0 %collective-permute-done.16.refs_7_ = bf16[48,2048]{1,0:T(8,128)(2,1)S(1)} collective-permute-done((bf16[48,2048]{1,0:T(8,128)(2,1)}, bf16[48,2048]{1,0:T(8,128)(2,1)S(1)}, u32[]{:S(2)}, u32[]{:S(2)}) %collective-permute-start.16) | collective-permute-done | bytes 196640 | tf_op jit(solution)/shard_map/ppermute | solution.py:117
  91.3 1.8 %collective-permute-start.11 = (bf16[48,2048]{1,0:T(8,128)(2,1)}, bf16[48,2048]{1,0:T(8,128)(2,1)S(1)}, u32[]{:S(2)}, u32[]{:S(2)}) collective-permute-start(bf16[48,2048]{1,0:T(8,128)(2,1)} %copy-done.12), channel_id=1, source_target_pairs={{0,8},{4,12},{8,0},{12,4},{16,24},{20,28},{24,16},{28,20},{1,9},{5... | collective-permute-start | bytes 589832 | tf_op jit(solution)/shard_map/ppermute | solution.py:117
  93.1 1.6 %collective-permute-done.17.refs_8_ = bf16[48,2048]{1,0:T(8,128)(2,1)S(1)} collective-permute-done((bf16[48,2048]{1,0:T(8,128)(2,1)}, bf16[48,2048]{1,0:T(8,128)(2,1)S(1)}, u32[]{:S(2)}, u32[]{:S(2)}) %collective-permute-start.17) | collective-permute-done | bytes 196640 | tf_op jit(solution)/shard_map/ppermute | solution.py:117
  94.8 1.7 %collective-permute-start.12 = (bf16[48,2048]{1,0:T(8,128)(2,1)}, bf16[48,2048]{1,0:T(8,128)(2,1)S(1)}, u32[]{:S(2)}, u32[]{:S(2)}) collective-permute-start(bf16[48,2048]{1,0:T(8,128)(2,1)} %copy-done.11), channel_id=1, source_target_pairs={{0,16},{4,20},{8,24},{12,28},{16,0},{20,4},{24,8},{28,12},{1,17},{... | collective-permute-start | bytes 589832 | tf_op jit(solution)/shard_map/ppermute | solution.py:117
  96.4 1.8 %collective-permute-start.13 = (bf16[48,2048]{1,0:T(8,128)(2,1)}, bf16[48,2048]{1,0:T(8,128)(2,1)S(1)}, u32[]{:S(2)}, u32[]{:S(2)}) collective-permute-start(bf16[48,2048]{1,0:T(8,128)(2,1)} %copy-done.10), channel_id=1, source_target_pairs={{0,24},{4,28},{8,16},{12,20},{16,8},{20,12},{24,0},{28,4},{1,25},{... | collective-permute-start | bytes 589832 | tf_op jit(solution)/shard_map/ppermute | solution.py:117
  99.8 3.5 %collective-permute-start = (f32[3,4,512]{2,1,0:T(4,128)S(1)}, f32[3,4,512]{2,1,0:T(4,128)S(1)}, u32[]{:S(2)}, u32[]{:S(2)}) collective-permute-start(f32[3,4,512]{2,1,0:T(4,128)S(1)} %get-tuple-element.51), channel_id=1, source_target_pairs={{0,1},{1,2},{2,3},{4,5},{5,6},{6,7},{8,9},{9,10},{10,11},{12,13},{... | collective-permute-start | bytes 73736 | tf_op jit(solution)/shard_map/ppermute | solution.py:403
  104.2 1.9 %collective-permute-start.1 = (f32[3,4,512]{2,1,0:T(4,128)S(1)}, f32[3,4,512]{2,1,0:T(4,128)S(1)}, u32[]{:S(2)}, u32[]{:S(2)}) collective-permute-start(f32[3,4,512]{2,1,0:T(4,128)S(1)} %get-tuple-element.52), channel_id=1, source_target_pairs={{1,0},{2,1},{3,2},{5,4},{6,5},{7,6},{9,8},{10,9},{11,10},{13,12},{... | collective-permute-start | bytes 73736 | tf_op jit(solution)/shard_map/ppermute | solution.py:408
  106.1 3.9 %collective-permute-start.24 = (bf16[48,2048]{1,0:T(8,128)(2,1)S(1)}, bf16[48,2048]{1,0:T(8,128)(2,1)S(1)}, u32[]{:S(2)}, u32[]{:S(2)}) collective-permute-start(bf16[48,2048]{1,0:T(8,128)(2,1)S(1)} %get-tuple-element.46), channel_id=1, source_target_pairs={{0,1},{1,2},{2,3},{4,5},{5,6},{6,7},{8,9},{9,10},{10,11},{12,13},{... | collective-permute-start | bytes 589832 | tf_op jit(solution)/shard_map/ppermute | solution.py:403
  111.0 1.9 %collective-permute-start.25 = (bf16[48,2048]{1,0:T(8,128)(2,1)S(1)}, bf16[48,2048]{1,0:T(8,128)(2,1)S(1)}, u32[]{:S(2)}, u32[]{:S(2)}) collective-permute-start(bf16[48,2048]{1,0:T(8,128)(2,1)S(1)} %get-tuple-element.45), channel_id=1, source_target_pairs={{1,0},{2,1},{3,2},{5,4},{6,5},{7,6},{9,8},{10,9},{11,10},{13,12},{... | collective-permute-start | bytes 589832 | tf_op jit(solution)/shard_map/ppermute | solution.py:408
  113.0 3.9 %collective-permute-start.19 = (bf16[48,2048]{1,0:T(8,128)(2,1)S(1)}, bf16[48,2048]{1,0:T(8,128)(2,1)S(1)}, u32[]{:S(2)}, u32[]{:S(2)}) collective-permute-start(bf16[48,2048]{1,0:T(8,128)(2,1)S(1)} %get-tuple-element.48), channel_id=1, source_target_pairs={{0,1},{1,2},{2,3},{4,5},{5,6},{6,7},{8,9},{9,10},{10,11},{12,13},{... | collective-permute-start | bytes 589832 | tf_op jit(solution)/shard_map/ppermute | solution.py:403
  116.9 1.9 %collective-permute-start.20 = (bf16[48,2048]{1,0:T(8,128)(2,1)S(1)}, bf16[48,2048]{1,0:T(8,128)(2,1)S(1)}, u32[]{:S(2)}, u32[]{:S(2)}) collective-permute-start(bf16[48,2048]{1,0:T(8,128)(2,1)S(1)} %get-tuple-element.47), channel_id=1, source_target_pairs={{1,0},{2,1},{3,2},{5,4},{6,5},{7,6},{9,8},{10,9},{11,10},{13,12},{... | collective-permute-start | bytes 589832 | tf_op jit(solution)/shard_map/ppermute | solution.py:408
  118.8 3.9 %collective-permute-start.14 = (bf16[48,2048]{1,0:T(8,128)(2,1)S(1)}, bf16[48,2048]{1,0:T(8,128)(2,1)S(1)}, u32[]{:S(2)}, u32[]{:S(2)}) collective-permute-start(bf16[48,2048]{1,0:T(8,128)(2,1)S(1)} %get-tuple-element.50), channel_id=1, source_target_pairs={{0,1},{1,2},{2,3},{4,5},{5,6},{6,7},{8,9},{9,10},{10,11},{12,13},{... | collective-permute-start | bytes 589832 | tf_op jit(solution)/shard_map/ppermute | solution.py:403
  122.8 2.1 %collective-permute-start.15 = (bf16[48,2048]{1,0:T(8,128)(2,1)S(1)}, bf16[48,2048]{1,0:T(8,128)(2,1)S(1)}, u32[]{:S(2)}, u32[]{:S(2)}) collective-permute-start(bf16[48,2048]{1,0:T(8,128)(2,1)S(1)} %get-tuple-element.49), channel_id=1, source_target_pairs={{1,0},{2,1},{3,2},{5,4},{6,5},{7,6},{9,8},{10,9},{11,10},{13,12},{... | collective-permute-start | bytes 589832 | tf_op jit(solution)/shard_map/ppermute | solution.py:408
  125.0 12.3 %propagate.3.refs_12_ = f32[2304,512]{1,0:T(8,128)} custom-call(s32[2]{0:T(128)S(1)} %pad_add_fusion.where, f32[144,8]{1,0:T(8,128)S(1)} %copy-done.1, f32[2,24,512]{2,1,0:T(8,128)S(1)} %slice.36.wind_ref, f32[24,512]{1,0:T(8,128)S(1)} %maximum_bitcast_fusion.mask_ref, bf16[144,2048]{1,0:T(8,128)(2,1)S(1)} %get-tuple-element.23.refs_0_, ...), custom_call_target="tpu_custom_call" | custom-call | flops 23592960 | bytes 3145728 | tf_op jit(solution)/shard_map/propagate/pallas_call | solution.py:370
  137.3 11.4 %propagate.4.refs_12_ = f32[2304,512]{1,0:T(8,128)} custom-call(s32[2]{0:T(128)S(1)} %pad_add_fusion.where, f32[144,8]{1,0:T(8,128)S(1)} %copy-done.1, f32[2,24,512]{2,1,0:T(8,128)S(1)} %slice.36.wind_ref, f32[24,512]{1,0:T(8,128)S(1)} %maximum_bitcast_fusion.mask_ref, ...), custom_call_target="tpu_custom_call", output_to_operand_aliasing={{}: (16, {})} | custom-call | flops 23592960 | bytes 3145728 | tf_op jit(solution)/shard_map/propagate/pallas_call | solution.py:370
  148.7 11.4 %propagate.5 = f32[2304,512]{1,0:T(8,128)} custom-call(s32[2]{0:T(128)S(1)} %pad_add_fusion.where, f32[144,8]{1,0:T(8,128)S(1)} %copy-done.1, f32[2,24,512]{2,1,0:T(8,128)S(1)} %slice.36.wind_ref, f32[24,512]{1,0:T(8,128)S(1)} %maximum_bitcast_fusion.mask_ref, bf16[144,2048]{1,0:T(8,128)(2,1)S(1)} %get-tuple-element.23.refs_0_, ...), custom_call_target="tpu_custom_call", output_to_operand_aliasing={{}: (16, {})} | custom-call | flops 23592960 | bytes 3145728 | tf_op jit(solution)/shard_map/propagate/pallas_call | solution.py:370
  (109 shorter events, 22.2 us)
Async XLA Ops:
  4.6 29.4 %copy-start.24 = (f32[144,2]{0,1:T(2,128)S(1)}, f32[144,2]{0,1:T(2,128)}, u32[]{:S(2)}) copy-start(f32[144,2]{0,1:T(2,128)} %param.15) | copy-start | bytes 3460
  4.6 17.3 %collective-permute-start.6 = (bf16[144,2048]{1,0:T(8,128)(2,1)S(1)}, bf16[144,2048]{1,0:T(8,128)(2,1)}, u32[]{:S(2)}, u32[]{:S(2)}) collective-permute-start(bf16[144,2048]{1,0:T(8,128)(2,1)S(1)} %get-tuple-element.26.refs_3_), channel_id=1, source_target_pairs={{0,24},{4,28},{8,16},{12,20},{16,8},{20,12},{24,0},{28,4},{1,25},{... | collective-permute-start | bytes 1769480 | tf_op jit(solution)/shard_map/ppermute | solution.py:117
  7.1 26.4 %collective-permute-start.4 = (bf16[144,2048]{1,0:T(8,128)(2,1)S(1)}, bf16[144,2048]{1,0:T(8,128)(2,1)}, u32[]{:S(2)}, u32[]{:S(2)}) collective-permute-start(bf16[144,2048]{1,0:T(8,128)(2,1)S(1)} %get-tuple-element.24.refs_1_), channel_id=1, source_target_pairs={{0,8},{4,12},{8,0},{12,4},{16,24},{20,28},{24,16},{28,20},{1,9},{5... | collective-permute-start | bytes 1769480 | tf_op jit(solution)/shard_map/ppermute | solution.py:117
  7.7 25.8 %collective-permute-start.5 = (bf16[144,2048]{1,0:T(8,128)(2,1)S(1)}, bf16[144,2048]{1,0:T(8,128)(2,1)}, u32[]{:S(2)}, u32[]{:S(2)}) collective-permute-start(bf16[144,2048]{1,0:T(8,128)(2,1)S(1)} %get-tuple-element.25.refs_2_), channel_id=1, source_target_pairs={{0,16},{4,20},{8,24},{12,28},{16,0},{20,4},{24,8},{28,12},{1,17},{... | collective-permute-start | bytes 1769480 | tf_op jit(solution)/shard_map/ppermute | solution.py:117
  8.2 35.0 %collective-permute-start.7 = (bf16[144,2048]{1,0:T(8,128)(2,1)S(1)}, bf16[144,2048]{1,0:T(8,128)(2,1)}, u32[]{:S(2)}, u32[]{:S(2)}) collective-permute-start(bf16[144,2048]{1,0:T(8,128)(2,1)S(1)} %get-tuple-element.23.refs_0_), channel_id=1, source_target_pairs={{0,4},{4,0},{8,12},{12,8},{16,20},{20,16},{24,28},{28,24},{1,5},{5... | collective-permute-start | bytes 1769480 | tf_op jit(solution)/shard_map/ppermute | solution.py:117
  9.3 107.5 %collective-permute-start.2 = (bf16[144,2048]{1,0:T(8,128)(2,1)}, bf16[144,2048]{1,0:T(8,128)(2,1)S(1)}, u32[]{:S(2)}, u32[]{:S(2)}) collective-permute-start(bf16[144,2048]{1,0:T(8,128)(2,1)} %get-tuple-element.44), channel_id=1, source_target_pairs={{0,1},{1,2},{2,3},{4,5},{5,6},{6,7},{8,9},{9,10},{10,11},{12,13},{... | collective-permute-start | bytes 1769480 | tf_op jit(solution)/shard_map/ppermute | solution.py:403
  22.0 23.6 %collective-permute-start.10 = (bf16[144,2048]{1,0:T(8,128)(2,1)}, bf16[144,2048]{1,0:T(8,128)(2,1)S(1)}, u32[]{:S(2)}, u32[]{:S(2)}) collective-permute-start(bf16[144,2048]{1,0:T(8,128)(2,1)} %collective-permute-done.6.refs_3_), channel_id=1, source_target_pairs={{0,4},{4,0},{8,12},{12,8},{16,20},{20,16},{24,28},{28,24},{1,5},{5... | collective-permute-start | bytes 1769480 | tf_op jit(solution)/shard_map/ppermute | solution.py:117
  33.5 12.0 %collective-permute-start.8 = (bf16[144,2048]{1,0:T(8,128)(2,1)}, bf16[144,2048]{1,0:T(8,128)(2,1)S(1)}, u32[]{:S(2)}, u32[]{:S(2)}) collective-permute-start(bf16[144,2048]{1,0:T(8,128)(2,1)} %collective-permute-done.4.refs_1_), channel_id=1, source_target_pairs={{0,4},{4,0},{8,12},{12,8},{16,20},{20,16},{24,28},{28,24},{1,5},{5... | collective-permute-start | bytes 1769480 | tf_op jit(solution)/shard_map/ppermute | solution.py:117
  33.5 12.0 %collective-permute-start.9 = (bf16[144,2048]{1,0:T(8,128)(2,1)}, bf16[144,2048]{1,0:T(8,128)(2,1)S(1)}, u32[]{:S(2)}, u32[]{:S(2)}) collective-permute-start(bf16[144,2048]{1,0:T(8,128)(2,1)} %collective-permute-done.5.refs_2_), channel_id=1, source_target_pairs={{0,4},{4,0},{8,12},{12,8},{16,20},{20,16},{24,28},{28,24},{1,5},{5... | collective-permute-start | bytes 1769480 | tf_op jit(solution)/shard_map/ppermute | solution.py:117
  43.2 75.7 %collective-permute-start.3 = (bf16[144,2048]{1,0:T(8,128)(2,1)}, bf16[144,2048]{1,0:T(8,128)(2,1)S(1)}, u32[]{:S(2)}, u32[]{:S(2)}) collective-permute-start(bf16[144,2048]{1,0:T(8,128)(2,1)} %get-tuple-element.43), channel_id=1, source_target_pairs={{1,0},{2,1},{3,2},{5,4},{6,5},{7,6},{9,8},{10,9},{11,10},{13,12},{... | collective-permute-start | bytes 1769480 | tf_op jit(solution)/shard_map/ppermute | solution.py:408
  71.4 12.1 %collective-permute-start.21 = (bf16[48,2048]{1,0:T(8,128)(2,1)}, bf16[48,2048]{1,0:T(8,128)(2,1)}, u32[]{:S(2)}, u32[]{:S(2)}) collective-permute-start(bf16[48,2048]{1,0:T(8,128)(2,1)} %get-tuple-element.38), channel_id=1, source_target_pairs={{0,8},{4,12},{8,0},{12,4},{16,24},{20,28},{24,16},{28,20},{1,9},{5... | collective-permute-start | bytes 589832 | tf_op jit(solution)/shard_map/ppermute | solution.py:117
  72.9 12.2 %collective-permute-start.22 = (bf16[48,2048]{1,0:T(8,128)(2,1)}, bf16[48,2048]{1,0:T(8,128)(2,1)}, u32[]{:S(2)}, u32[]{:S(2)}) collective-permute-start(bf16[48,2048]{1,0:T(8,128)(2,1)} %get-tuple-element.39), channel_id=1, source_target_pairs={{0,16},{4,20},{8,24},{12,28},{16,0},{20,4},{24,8},{28,12},{1,17},{... | collective-permute-start | bytes 589832 | tf_op jit(solution)/shard_map/ppermute | solution.py:117
  73.8 12.2 %collective-permute-start.23 = (bf16[48,2048]{1,0:T(8,128)(2,1)}, bf16[48,2048]{1,0:T(8,128)(2,1)}, u32[]{:S(2)}, u32[]{:S(2)}) collective-permute-start(bf16[48,2048]{1,0:T(8,128)(2,1)} %get-tuple-element.40), channel_id=1, source_target_pairs={{0,24},{4,28},{8,16},{12,20},{16,8},{20,12},{24,0},{28,4},{1,25},{... | collective-permute-start | bytes 589832 | tf_op jit(solution)/shard_map/ppermute | solution.py:117
  82.7 42.3 %copy-start.16 = (f32[1,16,512]{2,1,0:T(8,128)S(1)}, f32[1,16,512]{2,1,0:T(8,128)}, u32[]{:S(2)}) copy-start(f32[1,16,512]{2,1,0:T(8,128)} %convert_bitcast_fusion) | copy-start | bytes 98308
  82.7 42.3 %copy-start.17 = (f32[1,16,512]{2,1,0:T(8,128)S(1)}, f32[1,16,512]{2,1,0:T(8,128)}, u32[]{:S(2)}) copy-start(f32[1,16,512]{2,1,0:T(8,128)} %stack_reshape.6) | copy-start | bytes 98308
  82.7 42.3 %copy-start.18 = (f32[1,16,512]{2,1,0:T(8,128)S(1)}, f32[1,16,512]{2,1,0:T(8,128)}, u32[]{:S(2)}) copy-start(f32[1,16,512]{2,1,0:T(8,128)} %stack_reshape.7) | copy-start | bytes 98308
  82.7 42.4 %copy-start.1 = (f32[144,8]{1,0:T(8,128)S(1)}, f32[144,8]{1,0:T(8,128)}, u32[]{:S(2)}) copy-start(f32[144,8]{1,0:T(8,128)} %copy.32.coef_ref) | copy-start | bytes 13828
  82.7 42.4 %copy-start.7 = (bf16[48,2048]{1,0:T(8,128)(2,1)S(1)}, bf16[48,2048]{1,0:T(8,128)(2,1)}, u32[]{:S(2)}) copy-start(bf16[48,2048]{1,0:T(8,128)(2,1)} %copy-done.6) | copy-start | bytes 589828
  83.5 7.8 %collective-permute-start.16 = (bf16[48,2048]{1,0:T(8,128)(2,1)}, bf16[48,2048]{1,0:T(8,128)(2,1)S(1)}, u32[]{:S(2)}, u32[]{:S(2)}) collective-permute-start(bf16[48,2048]{1,0:T(8,128)(2,1)} %copy-done.15), channel_id=1, source_target_pairs={{0,8},{4,12},{8,0},{12,4},{16,24},{20,28},{24,16},{28,20},{1,9},{5... | collective-permute-start | bytes 589832 | tf_op jit(solution)/shard_map/ppermute | solution.py:117
  85.1 9.7 %collective-permute-start.17 = (bf16[48,2048]{1,0:T(8,128)(2,1)}, bf16[48,2048]{1,0:T(8,128)(2,1)S(1)}, u32[]{:S(2)}, u32[]{:S(2)}) collective-permute-start(bf16[48,2048]{1,0:T(8,128)(2,1)} %copy-done.14), channel_id=1, source_target_pairs={{0,16},{4,20},{8,24},{12,28},{16,0},{20,4},{24,8},{28,12},{1,17},{... | collective-permute-start | bytes 589832 | tf_op jit(solution)/shard_map/ppermute | solution.py:117
  86.0 10.4 %collective-permute-start.18 = (bf16[48,2048]{1,0:T(8,128)(2,1)}, bf16[48,2048]{1,0:T(8,128)(2,1)S(1)}, u32[]{:S(2)}, u32[]{:S(2)}) collective-permute-start(bf16[48,2048]{1,0:T(8,128)(2,1)} %copy-done.13), channel_id=1, source_target_pairs={{0,24},{4,28},{8,16},{12,20},{16,8},{20,12},{24,0},{28,4},{1,25},{... | collective-permute-start | bytes 589832 | tf_op jit(solution)/shard_map/ppermute | solution.py:117
  91.3 8.4 %collective-permute-start.11 = (bf16[48,2048]{1,0:T(8,128)(2,1)}, bf16[48,2048]{1,0:T(8,128)(2,1)S(1)}, u32[]{:S(2)}, u32[]{:S(2)}) collective-permute-start(bf16[48,2048]{1,0:T(8,128)(2,1)} %copy-done.12), channel_id=1, source_target_pairs={{0,8},{4,12},{8,0},{12,4},{16,24},{20,28},{24,16},{28,20},{1,9},{5... | collective-permute-start | bytes 589832 | tf_op jit(solution)/shard_map/ppermute | solution.py:117
  94.8 9.4 %collective-permute-start.12 = (bf16[48,2048]{1,0:T(8,128)(2,1)}, bf16[48,2048]{1,0:T(8,128)(2,1)S(1)}, u32[]{:S(2)}, u32[]{:S(2)}) collective-permute-start(bf16[48,2048]{1,0:T(8,128)(2,1)} %copy-done.11), channel_id=1, source_target_pairs={{0,16},{4,20},{8,24},{12,28},{16,0},{20,4},{24,8},{28,12},{1,17},{... | collective-permute-start | bytes 589832 | tf_op jit(solution)/shard_map/ppermute | solution.py:117
  96.4 9.6 %collective-permute-start.13 = (bf16[48,2048]{1,0:T(8,128)(2,1)}, bf16[48,2048]{1,0:T(8,128)(2,1)S(1)}, u32[]{:S(2)}, u32[]{:S(2)}) collective-permute-start(bf16[48,2048]{1,0:T(8,128)(2,1)} %copy-done.10), channel_id=1, source_target_pairs={{0,24},{4,28},{8,16},{12,20},{16,8},{20,12},{24,0},{28,4},{1,25},{... | collective-permute-start | bytes 589832 | tf_op jit(solution)/shard_map/ppermute | solution.py:117
  99.8 11.2 %collective-permute-start = (f32[3,4,512]{2,1,0:T(4,128)S(1)}, f32[3,4,512]{2,1,0:T(4,128)S(1)}, u32[]{:S(2)}, u32[]{:S(2)}) collective-permute-start(f32[3,4,512]{2,1,0:T(4,128)S(1)} %get-tuple-element.51), channel_id=1, source_target_pairs={{0,1},{1,2},{2,3},{4,5},{5,6},{6,7},{8,9},{9,10},{10,11},{12,13},{... | collective-permute-start | bytes 73736 | tf_op jit(solution)/shard_map/ppermute | solution.py:403
  104.2 8.8 %collective-permute-start.1 = (f32[3,4,512]{2,1,0:T(4,128)S(1)}, f32[3,4,512]{2,1,0:T(4,128)S(1)}, u32[]{:S(2)}, u32[]{:S(2)}) collective-permute-start(f32[3,4,512]{2,1,0:T(4,128)S(1)} %get-tuple-element.52), channel_id=1, source_target_pairs={{1,0},{2,1},{3,2},{5,4},{6,5},{7,6},{9,8},{10,9},{11,10},{13,12},{... | collective-permute-start | bytes 73736 | tf_op jit(solution)/shard_map/ppermute | solution.py:408
  106.1 16.7 %collective-permute-start.24 = (bf16[48,2048]{1,0:T(8,128)(2,1)S(1)}, bf16[48,2048]{1,0:T(8,128)(2,1)S(1)}, u32[]{:S(2)}, u32[]{:S(2)}) collective-permute-start(bf16[48,2048]{1,0:T(8,128)(2,1)S(1)} %get-tuple-element.46), channel_id=1, source_target_pairs={{0,1},{1,2},{2,3},{4,5},{5,6},{6,7},{8,9},{9,10},{10,11},{12,13},{... | collective-permute-start | bytes 589832 | tf_op jit(solution)/shard_map/ppermute | solution.py:403
  111.0 14.0 %collective-permute-start.25 = (bf16[48,2048]{1,0:T(8,128)(2,1)S(1)}, bf16[48,2048]{1,0:T(8,128)(2,1)S(1)}, u32[]{:S(2)}, u32[]{:S(2)}) collective-permute-start(bf16[48,2048]{1,0:T(8,128)(2,1)S(1)} %get-tuple-element.45), channel_id=1, source_target_pairs={{1,0},{2,1},{3,2},{5,4},{6,5},{7,6},{9,8},{10,9},{11,10},{13,12},{... | collective-permute-start | bytes 589832 | tf_op jit(solution)/shard_map/ppermute | solution.py:408
  113.0 24.4 %collective-permute-start.19 = (bf16[48,2048]{1,0:T(8,128)(2,1)S(1)}, bf16[48,2048]{1,0:T(8,128)(2,1)S(1)}, u32[]{:S(2)}, u32[]{:S(2)}) collective-permute-start(bf16[48,2048]{1,0:T(8,128)(2,1)S(1)} %get-tuple-element.48), channel_id=1, source_target_pairs={{0,1},{1,2},{2,3},{4,5},{5,6},{6,7},{8,9},{9,10},{10,11},{12,13},{... | collective-permute-start | bytes 589832 | tf_op jit(solution)/shard_map/ppermute | solution.py:403
  116.9 20.4 %collective-permute-start.20 = (bf16[48,2048]{1,0:T(8,128)(2,1)S(1)}, bf16[48,2048]{1,0:T(8,128)(2,1)S(1)}, u32[]{:S(2)}, u32[]{:S(2)}) collective-permute-start(bf16[48,2048]{1,0:T(8,128)(2,1)S(1)} %get-tuple-element.47), channel_id=1, source_target_pairs={{1,0},{2,1},{3,2},{5,4},{6,5},{7,6},{9,8},{10,9},{11,10},{13,12},{... | collective-permute-start | bytes 589832 | tf_op jit(solution)/shard_map/ppermute | solution.py:408
  118.8 29.9 %collective-permute-start.14 = (bf16[48,2048]{1,0:T(8,128)(2,1)S(1)}, bf16[48,2048]{1,0:T(8,128)(2,1)S(1)}, u32[]{:S(2)}, u32[]{:S(2)}) collective-permute-start(bf16[48,2048]{1,0:T(8,128)(2,1)S(1)} %get-tuple-element.50), channel_id=1, source_target_pairs={{0,1},{1,2},{2,3},{4,5},{5,6},{6,7},{8,9},{9,10},{10,11},{12,13},{... | collective-permute-start | bytes 589832 | tf_op jit(solution)/shard_map/ppermute | solution.py:403
  122.8 26.0 %collective-permute-start.15 = (bf16[48,2048]{1,0:T(8,128)(2,1)S(1)}, bf16[48,2048]{1,0:T(8,128)(2,1)S(1)}, u32[]{:S(2)}, u32[]{:S(2)}) collective-permute-start(bf16[48,2048]{1,0:T(8,128)(2,1)S(1)} %get-tuple-element.49), channel_id=1, source_target_pairs={{1,0},{2,1},{3,2},{5,4},{6,5},{7,6},{9,8},{10,9},{11,10},{13,12},{... | collective-permute-start | bytes 589832 | tf_op jit(solution)/shard_map/ppermute | solution.py:408
  (22 other events, 179.0 us)

commit v2 on v0

--- a/solution.py
+++ b/solution.py
@@ -1,11 +1,18 @@
+import functools
 import jax
 import jax.numpy as jnp
 from jax import lax
+from jax.experimental import pallas as pl
+from jax.experimental.pallas import tpu as pltpu
 from jax.sharding import PartitionSpec as P
 
 SUBSTEPS = 4
 TILE_ROWS = 2
 TILE_COLS = 16
+GROUP = 16
+SUBLANES = 8
+LANES = 128
+MIB = 1 << 20
 
 
 def with_halo(block, sides, width):
@@ -106,6 +113,567 @@
         energy_field = advect(padded, sea_field, courant_x, courant_y)
     return energy_field
 
+def exchange(value, axis, distance):
+    count = lax.axis_size(axis)
+    return lax.ppermute(value, axis, [(i, i ^ distance) for i in range(count)])
+
+
+def in_hbm(value):
+    return pltpu.with_memory_space_constraint(value, pltpu.MemorySpace.HBM)
+
+
+def spread_kernel(chips, halo, where, energy_ref, *refs):
+    outs, wide = refs[:-1], refs[-1]
+    group, rows, width = energy_ref.shape
+    for block in range(width // LANES):
+        lanes = slice(block * LANES, (block + 1) * LANES)
+        wide[block] = (
+            energy_ref[:, :, lanes].astype(jnp.float32).reshape(group * rows, LANES)
+        )
+
+    def place(out_ref, slot, row):
+        for block in range(width // LANES):
+            start = slot * width + block * LANES
+            picked = wide[block, pl.ds(row, group, stride=rows), :]
+            out_ref[:, start : start + LANES] = picked.astype(jnp.bfloat16)
+
+    for m in range(chips):
+        chip = jnp.bitwise_xor(where[0], m)
+        for slot in range(2):
+            place(outs[m], slot, chip + slot * (rows - halo))
+            place(outs[chips + m], slot, chip + (slot + 1) * halo)
+        for side in range(2):
+            place(outs[2 * chips + side], m, chip + (rows - halo) * where[2 + side])
+
+
+def spread(where, energy, chips, halo):
+    local, rows, width = energy.shape
+    block = 3 * GROUP
+    sizes = [2 * width] * (2 * chips) + [halo * width] * 2
+    return pl.pallas_call(
+        functools.partial(spread_kernel, chips, halo),
+        grid_spec=pltpu.PrefetchScalarGridSpec(
+            num_scalar_prefetch=1,
+            grid=(local // block,),
+            in_specs=[pl.BlockSpec((block, rows, width), lambda i, w: (i, 0, 0))],
+            out_specs=[pl.BlockSpec((block, size), lambda i, w: (i, 0)) for size in sizes],
+            scratch_shapes=[pltpu.VMEM((width // LANES, block * rows, LANES), jnp.float32)],
+        ),
+        out_shape=[pltpu.MemorySpace.HBM((local, size), jnp.bfloat16) for size in sizes],
+        compiler_params=pltpu.CompilerParams(vmem_limit_bytes=12 * MIB),
+        cost_estimate=pl.CostEstimate(
+            flops=energy.size, bytes_accessed=4 * energy.size, transcendentals=0
+        ),
+        name="spread",
+    )(where, energy)
+
+
+def gather_kernel(chips, parts, where, extra_ref, *refs):
+    pieces, outs, sems = refs[:chips], refs[chips:-1], refs[-1]
+    width = pieces[0].shape[1] // 2
+    copies = []
+    for side in range(2):
+        start = pl.multiple_of(width * where[2 + side], LANES)
+        begin = 0
+        for index, part in enumerate(parts):
+            out = outs[2 * index + side]
+            for m in range(chips):
+                copies.append(
+                    pltpu.make_async_copy(
+                        pieces[m].at[begin : begin + part, pl.ds(start, width)],
+                        out.at[:part, m * width : (m + 1) * width],
+                        sems.at[len(copies)],
+                    )
+                )
+            if index == 0:
+                out[part:, :] = extra_ref[side]
+            begin += part
+    for copy in copies:
+        copy.start()
+    for copy in copies:
+        copy.wait()
+
+
+def gather_edges(where, extra, landed, parts):
+    chips = len(landed)
+    width = landed[0].shape[1] // 2
+    shapes = [part + (GROUP if index == 0 else 0) for index, part in enumerate(parts)]
+    whole = pl.BlockSpec(memory_space=pltpu.VMEM)
+    return pl.pallas_call(
+        functools.partial(gather_kernel, chips, parts),
+        in_specs=[pl.BlockSpec(memory_space=pltpu.SMEM), whole]
+        + [pl.BlockSpec(memory_space=pl.ANY)] * chips,
+        out_specs=[whole] * (2 * len(parts)),
+        out_shape=[
+            jax.ShapeDtypeStruct((shape, chips * width), jnp.bfloat16)
+            for shape in shapes
+            for side in range(2)
+        ],
+        scratch_shapes=[pltpu.SemaphoreType.DMA((2 * chips * len(parts),))],
+        compiler_params=pltpu.CompilerParams(vmem_limit_bytes=4 * MIB),
+        cost_estimate=pl.CostEstimate(
+            flops=0, bytes_accessed=4 * chips * sum(shapes) * width, transcendentals=0
+        ),
+        name="gather_edges",
+    )(where, extra, *landed)
+
+
+def weights_kernel(
+    chips,
+    where,
+    column_ref,
+    row_ref,
+    mixing_hbm,
+    transfer_hbm,
+    first_hbm,
+    second_hbm,
+    pick,
+    mixing_ref,
+    transfer_ref,
+    first_ref,
+    second_ref,
+    in_sems,
+    out_sems,
+):
+    total = mixing_ref.shape[0]
+    local = total // (2 * chips)
+    stripe = total // chips
+    loads = [
+        pltpu.make_async_copy(mixing_hbm, mixing_ref, in_sems.at[0]),
+        pltpu.make_async_copy(transfer_hbm, transfer_ref, in_sems.at[1]),
+    ]
+    for load in loads:
+        load.start()
+    pick[...] = (
+        column_ref[...] == lax.broadcasted_iota(jnp.int32, (total, total), 1)
+    ).astype(jnp.bfloat16)
+    extra = first_ref.shape[0] - total
+    first_ref[total:, :] = jnp.ones((extra, total), jnp.bfloat16)
+    stores = []
+
+    def send(source, target, start, size):
+        store = pltpu.make_async_copy(
+            source.at[start : start + size, :],
+            target.at[start : start + size, :],
+            out_sems.at[len(stores)],
+        )
+        store.start()
+        stores.append(store)
+
+    for load in loads:
+        load.wait()
+    for start in range(0, total, stripe):
+        rows = lax.broadcasted_iota(jnp.int32, (stripe, total), 0) + start
+        chosen = (row_ref[...] == rows).astype(jnp.bfloat16)
+        first_ref[start : start + stripe, :] = jnp.dot(
+            chosen, mixing_ref[...], preferred_element_type=jnp.float32
+        ).astype(jnp.bfloat16)
+        send(first_ref, first_hbm, start, stripe + (extra if start + stripe == total else 0))
+    for m in range(chips):
+        block = 2 * jnp.bitwise_xor(where[0], m) + where[1]
+        rows = transfer_ref[pl.ds(pl.multiple_of(block * local, GROUP), local), :]
+        second_ref[m * local : (m + 1) * local, :] = jnp.dot(
+            rows, pick[...], preferred_element_type=jnp.float32
+        ).astype(jnp.bfloat16)
+        send(second_ref, second_hbm, m * local, local)
+    for store in stores:
+        store.wait()
+
+
+def weights(where, pattern, mixing, transfer, chips):
+    total = mixing.shape[0]
+    whole = pl.BlockSpec(memory_space=pltpu.VMEM)
+    outside = pl.BlockSpec(memory_space=pltpu.MemorySpace.HBM)
+    shapes = [(total + GROUP, total), (total // 2, total)]
+    return pl.pallas_call(
+        functools.partial(weights_kernel, chips),
+        in_specs=[pl.BlockSpec(memory_space=pltpu.SMEM)] + [whole] * 2 + [outside] * 2,
+        out_specs=[outside] * 2,
+        out_shape=[pltpu.MemorySpace.HBM(shape, jnp.bfloat16) for shape in shapes],
+        scratch_shapes=[pltpu.VMEM((total, total), jnp.bfloat16)] * 3
+        + [pltpu.VMEM(shape, jnp.bfloat16) for shape in shapes]
+        + [pltpu.SemaphoreType.DMA((2,)), pltpu.SemaphoreType.DMA((2 * chips,))],
+        compiler_params=pltpu.CompilerParams(vmem_limit_bytes=20 * MIB),
+        cost_estimate=pl.CostEstimate(
+            flops=3 * total**3, bytes_accessed=8 * total**2, transcendentals=0
+        ),
+        name="weights",
+    )(where, pattern[:, None], pattern[None, :], in_hbm(mixing), in_hbm(transfer))
+
+
+def terms_kernel(chips, where, dissip_ref, first_hbm, second_hbm, *refs):
+    pieces, outs = refs[: 2 * chips], refs[2 * chips : 3 * chips]
+    spectra, product, result, first_ref, second_ref, in_sems, weight_sems, out_sems = refs[
+        3 * chips :
+    ]
+    total = spectra.shape[0]
+    local = total // (2 * chips)
+    stripe = total // chips
+    extra = first_ref.shape[0] - total
+
+    def start_of(m, other):
+        core = jnp.bitwise_xor(where[1], other)
+        block = 2 * jnp.bitwise_xor(where[0], m) + core
+        return pl.multiple_of(block * local, GROUP)
+
+    copies = [
+        pltpu.make_async_copy(
+            pieces[m + other * chips],
+            spectra.at[pl.ds(start_of(m, other), local), :],
+            in_sems.at[2 * m + other],
+        )
+        for m in range(chips)
+        for other in range(2)
+    ]
+    stripes = []
+    for index in range(chips):
+        begin = index * stripe
+        end = begin + stripe + (extra if index == chips - 1 else 0)
+        stripes.append(
+            pltpu.make_async_copy(
+                first_hbm.at[begin:end, :], first_ref.at[begin:end, :], weight_sems.at[index]
+            )
+        )
+    load = pltpu.make_async_copy(second_hbm, second_ref, weight_sems.at[chips])
+    for copy in [*copies, *stripes, load]:
+        copy.start()
+    for copy in copies:
+        copy.wait()
+
+    for index in range(chips):
+        start = index * stripe
+        last = index == chips - 1
+        stripes[index].wait()
+        mixed = jnp.dot(
+            first_ref[start : start + stripe + (extra if last else 0), :],
+            spectra[...],
+            preferred_element_type=jnp.float32,
+        )
+        product[start : start + stripe, :] = (
+            mixed[:stripe] * spectra[start : start + stripe, :].astype(jnp.float32)
+        ).astype(jnp.bfloat16)
+        if last:
+            mean = mixed[stripe : stripe + 1] * (1.0 / total)
+    load.wait()
+    sent = []
+    for m in range(chips):
+        rows = pl.ds(start_of(m, 0), local)
+        mine = slice(m * local, (m + 1) * local)
+        nonlinear = jnp.dot(
+            second_ref[mine, :], product[...], preferred_element_type=jnp.float32
+        )
+        own = spectra[rows, :].astype(jnp.float32)
+        result[mine, :] = (nonlinear - dissip_ref[rows, :] * mean * own).astype(jnp.bfloat16)
+        copy = pltpu.make_async_copy(result.at[mine, :], outs[m], out_sems.at[m])
+        copy.start()
+        sent.append(copy)
+    for copy in sent:
+        copy.wait()
+
+
+def source_terms(where, first, second, dissip, near, far):
+    chips = len(near)
+    local, cells = near[0].shape
+    total = 2 * chips * local
+    outside = pl.BlockSpec(memory_space=pltpu.MemorySpace.HBM)
+    return pl.pallas_call(
+        functools.partial(terms_kernel, chips),
+        in_specs=[
+            pl.BlockSpec(memory_space=pltpu.SMEM),
+            pl.BlockSpec(memory_space=pltpu.VMEM),
+            outside,
+            outside,
+        ]
+        + [pl.BlockSpec(memory_space=pl.ANY)] * (2 * chips),
+        out_specs=[outside] * chips,
+        out_shape=[pltpu.MemorySpace.HBM((local, cells), jnp.bfloat16)] * chips,
+        scratch_shapes=[
+            pltpu.VMEM((total, cells), jnp.bfloat16),
+            pltpu.VMEM((total, cells), jnp.bfloat16),
+            pltpu.VMEM((total // 2, cells), jnp.bfloat16),
+            pltpu.VMEM(first.shape, jnp.bfloat16),
+            pltpu.VMEM(second.shape, jnp.bfloat16),
+            pltpu.SemaphoreType.DMA((2 * chips,)),
+            pltpu.SemaphoreType.DMA((chips + 1,)),
+            pltpu.SemaphoreType.DMA((chips,)),
+        ],
+        compiler_params=pltpu.CompilerParams(vmem_limit_bytes=18 * MIB),
+        cost_estimate=pl.CostEstimate(
+            flops=3 * total * total * cells, bytes_accessed=8 * total * cells, transcendentals=0
+        ),
+        name="source_terms",
+    )(where, dissip[:, None], in_hbm(first), in_hbm(second), *near, *far)
+
+
+def propagate_kernel(chips, halo, where, coef_ref, fields_ref, *refs):
+    count = 2 * chips + 2
+    energies, edges, terms = refs[:count], refs[count : count + 2], refs[count + 2 : 2 * count + 2]
+    out_ref, field, turned, weather = refs[-4:]
+    rows, blocks, group, lanes = field.shape
+    width = blocks * lanes
+    inner = rows - 2 * halo
+
+    def column(at, number, index):
+        return jnp.broadcast_to(coef_ref[at : at + number, index : index + 1], (number, lanes))
+
+    cosine, sine = column(0, group, 0), column(0, group, 1)
+
+    firsts = [(halo + inner) * where[2 + side] for side in range(2)]
+
+    @pl.when(pl.program_id(0) == 0)
+    def _():
+        for index in range(3):
+            for row in range(inner):
+                for b in range(blocks):
+                    part = slice(b * lanes, (b + 1) * lanes)
+                    weather[index, halo + row, b] = jnp.broadcast_to(
+                        fields_ref[index, row : row + 1, part], (SUBLANES, lanes)
+                    )
+        for side in range(2):
+            pieces = edges[side][...].astype(jnp.float32)
+            for index in range(3):
+                value = pieces[3 * index : 3 * index + 1]
+                value = value + pieces[3 * index + 1 : 3 * index + 2]
+                value = value + pieces[3 * index + 2 : 3 * index + 3]
+                value = jnp.where(where[4 + side] == 1, value, 0.0)
+                for row in range(halo):
+                    for b in range(blocks):
+                        at = row * width + b * lanes
+                        weather[index, firsts[side] + row, b] = jnp.broadcast_to(
+                            value[:, at : at + lanes], (SUBLANES, lanes)
+                        )
+
+    def force(energy_ref, term_ref, slot, row, valid=None):
+        for b in range(blocks):
+            at = slice(slot * width + b * lanes, slot * width + (b + 1) * lanes)
+            wind_u = jnp.concatenate([weather[0, row, b]] * (group // SUBLANES))
+            wind_v = jnp.concatenate([weather[1, row, b]] * (group // SUBLANES))
+            drive = wind_u * cosine + wind_v * sine
+            value = energy_ref[:, at].astype(jnp.float32) * (
+                1.0 + jnp.maximum(drive, 0.0)
+            ) + term_ref[:, at].astype(jnp.float32)
+            if valid is not None:
+                value = jnp.where(valid == 1, value, 0.0)
+            field[row, b] = value
+
+    for m in range(chips):
+        chip = jnp.bitwise_xor(where[0], m)
+        for slot in range(2):
+            force(energies[m], terms[m], slot, halo + chip + slot * (inner - halo))
+            force(energies[chips + m], terms[chips + m], slot, halo + chip + (slot + 1) * halo)
+        for side in range(2):
+            index = 2 * chips + side
+            force(energies[index], terms[index], m, firsts[side] + chip, where[4 + side])
+
+    lane = lax.broadcasted_iota(jnp.int32, (SUBLANES, lanes), 1)
+    for at in range(0, group, SUBLANES):
+        here = slice(at, at + SUBLANES)
+        keep, west, east, south, north = [column(at, SUBLANES, i) for i in range(2, 7)]
+        from_west, from_south = west > 0.0, south > 0.0
+        source = jnp.bitwise_and(jnp.where(from_west, lane - 1, lane + 1), lanes - 1)
+        first_lane = jnp.logical_and(from_west, lane == 0)
+        last_lane = jnp.logical_and(jnp.logical_not(from_west), lane == lanes - 1)
+        along, across = west + east, south + north
+        for substep in range(1, halo + 1):
+            before = [field[substep - 1, b, here] for b in range(blocks)]
+            center = [field[substep, b, here] for b in range(blocks)]
+            for row in range(substep, rows - substep):
+                after = [field[row + 1, b, here] for b in range(blocks)]
+                moved = [jnp.take_along_axis(value, source, axis=1) for value in center]
+                for b in range(blocks):
+                    beside = jnp.where(first_lane, moved[b - 1] if b > 0 else 0.0, moved[b])
+                    beside = jnp.where(
+                        last_lane, moved[b + 1] if b < blocks - 1 else 0.0, beside
+                    )
+                    upwind = jnp.where(from_south, before[b], after[b])
+                    value = (center[b] * keep + beside * along + upwind * across) * weather[
+                        2, row, b
+                    ]
+                    if substep < halo:
+                        field[row, b, here] = value
+                    else:
+                        turned[
+                            b, pl.ds(at * inner + row - halo, SUBLANES, stride=inner), :
+                        ] = value
+                before, center = center, after
+    for b in range(blocks):
+        out_ref[:, b * lanes : (b + 1) * lanes] = turned[b]
+
+
+def propagate(where, coef, fields, energies, edges, terms, begin, part, previous, halo):
+    chips = (len(energies) - 2) // 2
+    local = energies[0].shape[0]
+    inner, width = fields.shape[1:]
+    rows = inner + 2 * halo
+    steps = part // GROUP
+    base = begin // GROUP
+    last = edges[0].shape[0] // GROUP - 1
+    cells, edge = energies[0].shape[1], energies[-1].shape[1]
+    shape = jax.ShapeDtypeStruct((local * inner, width), jnp.float32)
+    at_base = lambda i, w: (base + i, 0)
+    in_specs = (
+        [
+            pl.BlockSpec((GROUP, coef.shape[1]), at_base),
+            pl.BlockSpec(fields.shape, lambda i, w: (0, 0, 0)),
+        ]
+        + [pl.BlockSpec((GROUP, cells), at_base)] * (2 * chips)
+        + [pl.BlockSpec((GROUP, edge), at_base)] * 2
+        + [pl.BlockSpec((GROUP, edge), lambda i, w: (last, 0))] * 2
+        + [pl.BlockSpec((GROUP, cells), at_base)] * (2 * chips)
+        + [pl.BlockSpec((GROUP, edge), lambda i, w: (i, 0))] * 2
+    )
+    operands = [where, coef, fields, *map(in_hbm, energies), *edges]
+    operands += [*map(in_hbm, terms[: 2 * chips]), *terms[2 * chips :]]
+    aliases = {}
+    kernel = functools.partial(propagate_kernel, chips, halo)
+    if previous is not None:
+        aliases = {len(operands): 0}
+        operands.append(previous)
+        in_specs.append(pl.BlockSpec(memory_space=pl.ANY))
+    return pl.pallas_call(
+        kernel,
+        grid_spec=pltpu.PrefetchScalarGridSpec(
+            num_scalar_prefetch=1,
+            grid=(steps,),
+            in_specs=in_specs,
+            out_specs=pl.BlockSpec((GROUP * inner, width), lambda i, w: (base + i, 0)),
+            scratch_shapes=[
+                pltpu.VMEM((rows, width // LANES, GROUP, LANES), jnp.float32),
+                pltpu.VMEM((width // LANES, GROUP * inner, LANES), jnp.float32),
+                pltpu.VMEM((3, rows, width // LANES, SUBLANES, LANES), jnp.float32),
+            ],
+        ),
+        out_shape=shape,
+        input_output_aliases=aliases,
+        compiler_params=pltpu.CompilerParams(vmem_limit_bytes=10 * MIB),
+        cost_estimate=pl.CostEstimate(
+            flops=60 * shape.size * part // local,
+            bytes_accessed=8 * shape.size * part // local,
+            transcendentals=0,
+        ),
+        name="propagate",
+    )(*operands)
+
+
+def thirds(value):
+    pieces, rest = [], value
+    for _ in range(3):
+        piece = lax.reduce_precision(rest, 8, 7)
+        pieces.append(piece)
+        rest = rest - piece
+    stacked = jnp.stack(pieces, axis=1).reshape(3 * value.shape[0], value.shape[1])
+    return jnp.pad(stacked, ((0, GROUP - stacked.shape[0]), (0, 0))).astype(jnp.bfloat16)
+
+
+def pair_up(value, start):
+    count = lax.axis_size("strip")
+    target = list(range(count))
+    for i in range(start, count - 1, 2):
+        target[i], target[i + 1] = i + 1, i
+    return lax.ppermute(value, "strip", list(enumerate(target)))
+
+
+def per_device_paired(
+    energy,
+    heading,
+    growth,
+    courant,
+    dissip,
+    mixing,
+    transfer,
+    pattern,
+    regime_winds,
+    regime,
+    seeds,
+    sea_mask,
+):
+    chips = lax.axis_size("comp") // 2
+    local, rows, width = energy.shape
+    halo = SUBSTEPS
+    units = local // GROUP
+    parts = (units // 2 * GROUP, (units - units // 2) * GROUP)
+    me, strip, strips = lax.axis_index("comp"), lax.axis_index("strip"), lax.axis_size("strip")
+    chip, odd = me // 2, strip % 2
+    has_above = (strip > 0).astype(jnp.int32)
+    has_below = (strip < strips - 1).astype(jnp.int32)
+    where = jnp.stack(
+        [
+            chip,
+            me % 2,
+            1 - odd,
+            odd,
+            jnp.where(odd == 1, has_above, has_below),
+            jnp.where(odd == 1, has_below, has_above),
+        ]
+    ).astype(jnp.int32)
+
+    pieces = spread(where, energy, chips, halo)
+    outer, rest = pieces[:chips], pieces[chips:]
+    near_outer = [outer[0]] + [exchange(outer[m], "comp", 2 * m) for m in range(1, chips)]
+    first, second = weights(where, pattern, mixing, transfer, chips)
+    near_outer, rest, first, second = lax.optimization_barrier(
+        (near_outer, rest, first, second)
+    )
+    middle, sides = rest[:chips], rest[chips:]
+    near_middle = [middle[0]] + [exchange(middle[m], "comp", 2 * m) for m in range(1, chips)]
+    energies = [*outer, *middle] + [pair_up(sides[side], side) for side in range(2)]
+
+    far_outer = [exchange(value, "comp", 1) for value in near_outer]
+    sent_outer = source_terms(where, first, second, dissip, near_outer, far_outer)
+    landed_outer = [sent_outer[0]] + [
+        exchange(sent_outer[m], "comp", 2 * m) for m in range(1, chips)
+    ]
+
+    wind_u, wind_v = strip_winds(regime_winds, regime, seeds)
+    fields = jnp.stack([wind_u, wind_v, sea_mask.astype(jnp.float32)])
+    upper, lower = fields[:, :halo], fields[:, rows - halo :]
+    extra = jnp.stack(
+        [
+            thirds(jnp.where(odd == 1, upper, lower).reshape(3, -1)),
+            thirds(jnp.where(odd == 1, lower, upper).reshape(3, -1)),
+        ]
+    )
+    along, across = courant[:, 0], courant[:, 1]
+    coef = jnp.stack(
+        [
+            growth * jnp.cos(heading),
+            growth * jnp.sin(heading),
+            1.0 - jnp.abs(along) - jnp.abs(across),
+            jnp.maximum(along, 0.0),
+            -jnp.minimum(along, 0.0),
+            jnp.maximum(across, 0.0),
+            -jnp.minimum(across, 0.0),
+            jnp.zeros_like(along),
+        ],
+        axis=1,
+    )
+
+    near_middle, sent_outer = lax.optimization_barrier((near_middle, sent_outer))
+    far_middle = [exchange(value, "comp", 1) for value in near_middle]
+    sent_middle = source_terms(where, first, second, dissip, near_middle, far_middle)
+    landed_middle = [sent_middle[0]] + [
+        exchange(sent_middle[m], "comp", 2 * m) for m in range(1, chips)
+    ]
+
+    edges = gather_edges(where, extra, landed_outer, parts)
+    edges = [pair_up(edge, index % 2) for index, edge in enumerate(edges)]
+    landed = [*landed_outer, *landed_middle]
+    result = None
+    for j in range(len(parts)):
+        result = propagate(
+            where,
+            coef,
+            fields,
+            energies,
+            edges[:2],
+            landed + edges[2 * j : 2 * j + 2],
+            sum(parts[:j]),
+            parts[j],
+            result,
+            halo,
+        )
+    return result.reshape(local, rows, width)
+
 
 def solution(mesh):
     placed = (
@@ -122,6 +690,8 @@
         P("strip", None),
         P("strip", None),
     )
+    paired = mesh.shape["comp"] == 2 * SUBSTEPS
+    body = per_device_paired if paired else per_device
     return jax.shard_map(
-        per_device, mesh=mesh, in_specs=placed, out_specs=P("comp", "strip", None), check_vma=False
-    )
+        body, mesh=mesh, in_specs=placed, out_specs=P("comp", "strip", None), check_vma=False
+    )

time: 195 us -> 101 us (0.52)
  the two profiles are of different devices: /device:TPU:26 before, /device:TPU:8 now
where the time goes in v2:
time: 101 us; the launch traced here: 100 us
  Pallas kernels  52.2 us (52%)
  starting transfers between devices  25.9 us (26%)
  waiting for transfers between devices  11.7 us (12%)
  local copies, waits for them, and re-layouts  9.29 us (9%)
    pallas_call x2, Pallas kernels, propagate(): pl.pallas_call(kernel, grid_spec=pltpu.PrefetchScalarGridSpec(num_scalar_...  18.2 us
    pallas_call x2, Pallas kernels, source_terms(): pl.pallas_call(functools.partial(terms_kernel, chips), in_specs=[pl.Block...  17.1 us
    ppermute x20, starting transfers between devices, exchange(): return lax.ppermute(value, axis, [(i, i ^ distance) for i in range(count)])  16.2 us
    ppermute x20, waiting for transfers between devices, exchange(): return lax.ppermute(value, axis, [(i, i ^ distance) for i in range(count)])  10.4 us
    pallas_call x1, Pallas kernels, weights(): pl.pallas_call(functools.partial(weights_kernel, chips), in_specs=[pl.Blo...  10.1 us
    ppermute x6, starting transfers between devices, pair_up(): return lax.ppermute(value, 'strip', list(enumerate(target)))  9.61 us
    unnamed x54, local copies, waits for them, and re-layouts  5.84 us
    pallas_call x1, Pallas kernels, spread(): pl.pallas_call(functools.partial(spread_kernel, chips, halo), grid_spec=p...  5.01 us
  transfers between devices with their start and end apart: 26, of which 5 were waited for; matrix products, arithmetic and copies ran while one was open for 4% of the time, Pallas kernels for 37%

profile of v2, /device:TPU:8, one launch (start us, length us, event | category | flops | bytes accessed | tf_op | source)
XLA Modules:
  0.0 100.2 jit_solution(15054880230979923787)
XLA Ops:
  0.2 1.7 %copy-done.4 = bf16[144,16,512]{2,1,0:T(8,128)(2,1)S(1)} copy-done((bf16[144,16,512]{2,1,0:T(8,128)(2,1)S(1)}, bf16[144,16,512]{2,1,0:T(8,128)(2,1)}, u32[]{:S(2)}) %copy-start.4) | copy-done | bytes 2359320
  1.8 5.0 %spread.1 = (bf16[144,1024]{1,0:T(8,128)(2,1)}, bf16[144,1024]{1,0:T(8,128)(2,1)}, bf16[144,1024]{1,0:T(8,128)(2,1)}, bf16[144,1024]{1,0:T(8,128)(2,1)}, bf16[14...) custom-call(s32[6]{0:T(128)S(1)} %stack.70.where, ...), custom_call_target="tpu_custom_call" | custom-call | flops 1179648 | bytes 4718592 | tf_op jit(solution)/shard_map/spread/pallas_call | solution.py:153
  6.8 1.5 %collective-permute-start = (bf16[144,1024]{1,0:T(8,128)(2,1)}, bf16[144,1024]{1,0:T(8,128)(2,1)S(1)}, u32[]{:S(2)}, u32[]{:S(2)}) collective-permute-start(bf16[144,1024]{1,0:T(8,128)(2,1)} %get-tuple-element.46.refs_1_), channel_id=1, source_target_pairs={{0,8},{4,12},{8,0},{12,4},{16,24},{20,28},{24,16},{28,20},{1,9},{5... | collective-permute-start | bytes 884744 | tf_op jit(solution)/shard_map/ppermute | solution.py:118
  8.3 1.5 %collective-permute-start.1 = (bf16[144,1024]{1,0:T(8,128)(2,1)}, bf16[144,1024]{1,0:T(8,128)(2,1)S(1)}, u32[]{:S(2)}, u32[]{:S(2)}) collective-permute-start(bf16[144,1024]{1,0:T(8,128)(2,1)} %get-tuple-element.47.refs_2_), channel_id=1, source_target_pairs={{0,16},{4,20},{8,24},{12,28},{16,0},{20,4},{24,8},{28,12},{1,17},{... | collective-permute-start | bytes 884744 | tf_op jit(solution)/shard_map/ppermute | solution.py:118
  10.3 0.7 broadcast_in_dim.29.row_ref
  11.0 0.9 broadcast_in_dim.31.column_ref
  13.1 10.1 %weights.1 = (bf16[1168,1152]{1,0:T(8,128)(2,1)}, bf16[576,1152]{1,0:T(8,128)(2,1)}) custom-call(s32[6]{0:T(128)S(1)} %stack.70.where, s32[1152,1]{1,0:T(8,128)S(1)} %broadcast_in_dim.31.column_ref, s32[1,1152]{1,0:T(1,128)S(1)} %broadcast_in_dim.29.row_ref, bf16[1152,1152]{1,0:T(8,128)(2,1)} %mixing_hbm.1, bf16[1152,1152]{1,0:T(8,128)(2,1)} %transfer_hbm.1), custom_call_target="tpu_custom_call" | custom-call | flops 4586471424 | bytes 10616832 | tf_op jit(solution)/shard_map/weights/pallas_call | solution.py:288
  24.4 1.5 %collective-permute-start.14 = (bf16[144,1024]{1,0:T(8,128)(2,1)S(1)}, bf16[144,1024]{1,0:T(8,128)(2,1)S(1)}, u32[]{:S(2)}, u32[]{:S(2)}) collective-permute-start(bf16[144,1024]{1,0:T(8,128)(2,1)S(1)} %copy-done.13), channel_id=1, source_target_pairs={{0,8},{4,12},{8,0},{12,4},{16,24},{20,28},{24,16},{28,20},{1,9},{5... | collective-permute-start | bytes 884744 | tf_op jit(solution)/shard_map/ppermute | solution.py:118
  25.9 1.5 %collective-permute-start.15 = (bf16[144,1024]{1,0:T(8,128)(2,1)S(1)}, bf16[144,1024]{1,0:T(8,128)(2,1)S(1)}, u32[]{:S(2)}, u32[]{:S(2)}) collective-permute-start(bf16[144,1024]{1,0:T(8,128)(2,1)S(1)} %copy-done.14), channel_id=1, source_target_pairs={{0,16},{4,20},{8,24},{12,28},{16,0},{20,4},{24,8},{28,12},{1,17},{... | collective-permute-start | bytes 884744 | tf_op jit(solution)/shard_map/ppermute | solution.py:118
  28.0 8.7 %source_terms.2 = (bf16[144,1024]{1,0:T(8,128)(2,1)}, bf16[144,1024]{1,0:T(8,128)(2,1)}, bf16[144,1024]{1,0:T(8,128)(2,1)}, bf16[144,1024]{1,0:T(8,128)(2,1)}) custom-call(s32[6]{0:T(128)S(1)} %stack.70.where, f32[1152,1]{1,0:T(8,128)S(1)} %broadcast_in_dim.32.dissip_ref, bf16[1168,1152]{1,0:T(8,128)(2,1)} %get-tuple-element.63.first_hbm, ...), custom_call_target="tpu_custom_call" | custom-call | flops 4076863488 | bytes 9437184 | tf_op jit(solution)/shard_map/source_terms/pallas_call | solution.py:379
  36.7 4.3 %collective-permute-done.15.refs_2_ = bf16[144,1024]{1,0:T(8,128)(2,1)S(1)} collective-permute-done((bf16[144,1024]{1,0:T(8,128)(2,1)S(1)}, bf16[144,1024]{1,0:T(8,128)(2,1)S(1)}, u32[]{:S(2)}, u32[]{:S(2)}) %collective-permute-start.15) | collective-permute-done | bytes 294944 | tf_op jit(solution)/shard_map/ppermute | solution.py:118
  43.4 4.6 %collective-permute-start.4 = (bf16[144,2048]{1,0:T(8,128)(2,1)}, bf16[144,2048]{1,0:T(8,128)(2,1)S(1)}, u32[]{:S(2)}, u32[]{:S(2)}) collective-permute-start(bf16[144,2048]{1,0:T(8,128)(2,1)} %get-tuple-element.62), channel_id=1, source_target_pairs={{0,0},{1,2},{2,1},{3,3},{4,4},{5,6},{6,5},{7,7},{8,8},{9,10},{10,9... | collective-permute-start | bytes 1769480 | tf_op jit(solution)/shard_map/ppermute | solution.py:573
  48.0 1.4 %collective-permute-start.9 = (bf16[144,1024]{1,0:T(8,128)(2,1)}, bf16[144,1024]{1,0:T(8,128)(2,1)S(1)}, u32[]{:S(2)}, u32[]{:S(2)}) collective-permute-start(bf16[144,1024]{1,0:T(8,128)(2,1)} %get-tuple-element.70), channel_id=1, source_target_pairs={{0,8},{4,12},{8,0},{12,4},{16,24},{20,28},{24,16},{28,20},{1,9},{5... | collective-permute-start | bytes 884744 | tf_op jit(solution)/shard_map/ppermute | solution.py:118
  49.4 0.7 copy-done.7
  50.1 1.0 collective-permute-start.10
  51.1 0.7 copy-done.9
  51.8 1.2 %collective-permute-start.11 = (bf16[144,1024]{1,0:T(8,128)(2,1)}, bf16[144,1024]{1,0:T(8,128)(2,1)S(1)}, u32[]{:S(2)}, u32[]{:S(2)}) collective-permute-start(bf16[144,1024]{1,0:T(8,128)(2,1)} %get-tuple-element.72), channel_id=1, source_target_pairs={{0,24},{4,28},{8,16},{12,20},{16,8},{20,12},{24,0},{28,4},{1,25},{... | collective-permute-start | bytes 884744 | tf_op jit(solution)/shard_map/ppermute | solution.py:118
  53.0 1.0 copy-done.8
  54.0 1.0 copy-done.10
  54.9 8.5 %source_terms.3 = (bf16[144,1024]{1,0:T(8,128)(2,1)}, bf16[144,1024]{1,0:T(8,128)(2,1)}, bf16[144,1024]{1,0:T(8,128)(2,1)}, bf16[144,1024]{1,0:T(8,128)(2,1)}) custom-call(s32[6]{0:T(128)S(1)} %stack.70.where, f32[1152,1]{1,0:T(8,128)S(1)} %broadcast_in_dim.32.dissip_ref, bf16[1168,1152]{1,0:T(8,128)(2,1)} %get-tuple-element.63.first_hbm, ...), custom_call_target="tpu_custom_call" | custom-call | flops 4076863488 | bytes 9437184 | tf_op jit(solution)/shard_map/source_terms/pallas_call | solution.py:379
  63.4 1.4 %collective-permute-start.21 = (bf16[144,1024]{1,0:T(8,128)(2,1)}, bf16[144,1024]{1,0:T(8,128)(2,1)S(1)}, u32[]{:S(2)}, u32[]{:S(2)}) collective-permute-start(bf16[144,1024]{1,0:T(8,128)(2,1)} %get-tuple-element.80), channel_id=1, source_target_pairs={{0,8},{4,12},{8,0},{12,4},{16,24},{20,28},{24,16},{28,20},{1,9},{5... | collective-permute-start | bytes 884744 | tf_op jit(solution)/shard_map/ppermute | solution.py:118
  64.8 1.0 collective-permute-start.22
  65.9 1.3 %collective-permute-start.23 = (bf16[144,1024]{1,0:T(8,128)(2,1)}, bf16[144,1024]{1,0:T(8,128)(2,1)}, u32[]{:S(2)}, u32[]{:S(2)}) collective-permute-start(bf16[144,1024]{1,0:T(8,128)(2,1)} %get-tuple-element.82), channel_id=1, source_target_pairs={{0,24},{4,28},{8,16},{12,20},{16,8},{20,12},{24,0},{28,4},{1,25},{... | collective-permute-start | bytes 884744 | tf_op jit(solution)/shard_map/ppermute | solution.py:118
  67.1 1.8 %gather_edges.1 = (bf16[80,2048]{1,0:T(8,128)(2,1)}, bf16[80,2048]{1,0:T(8,128)(2,1)}, bf16[80,2048]{1,0:T(8,128)(2,1)S(1)}, bf16[80,2048]{1,0:T(8,128)(2,1)S(1)}) custom-call(s32[6]{0:T(128)S(1)} %stack.70.where, bf16[2,16,2048]{2,1,0:T(8,128)(2,1)S(1)} %pad_maximum_fusion.extra_ref, bf16[144,1024]{1,0:T(8,128)(2,1)S(1)} %copy-done, ...), custom_call_target="tpu_custom_call" | custom-call | bytes 1310720 | tf_op jit(solution)/shard_map/gather_edges/pallas_call | solution.py:202
  69.0 2.3 %collective-permute-start.13 = (bf16[80,2048]{1,0:T(8,128)(2,1)}, bf16[80,2048]{1,0:T(8,128)(2,1)S(1)}, u32[]{:S(2)}, u32[]{:S(2)}) collective-permute-start(bf16[80,2048]{1,0:T(8,128)(2,1)} %get-tuple-element.74), channel_id=1, source_target_pairs={{0,0},{1,2},{2,1},{3,3},{4,4},{5,6},{6,5},{7,7},{8,8},{9,10},{10,9... | collective-permute-start | bytes 983048 | tf_op jit(solution)/shard_map/ppermute | solution.py:573
  71.3 2.3 %collective-permute-done.21.refs_17_ = bf16[144,1024]{1,0:T(8,128)(2,1)S(1)} collective-permute-done((bf16[144,1024]{1,0:T(8,128)(2,1)}, bf16[144,1024]{1,0:T(8,128)(2,1)S(1)}, u32[]{:S(2)}, u32[]{:S(2)}) %collective-permute-start.21) | collective-permute-done | bytes 294944 | tf_op jit(solution)/shard_map/ppermute | solution.py:118
  73.6 3.6 %collective-permute-done.22.refs_18_ = bf16[144,1024]{1,0:T(8,128)(2,1)S(1)} collective-permute-done((bf16[144,1024]{1,0:T(8,128)(2,1)}, bf16[144,1024]{1,0:T(8,128)(2,1)S(1)}, u32[]{:S(2)}, u32[]{:S(2)}) %collective-permute-start.22) | collective-permute-done | bytes 294944 | tf_op jit(solution)/shard_map/ppermute | solution.py:118
  77.3 0.7 copy-done.17
  78.0 2.2 %collective-permute-start.25 = (bf16[80,2048]{1,0:T(8,128)(2,1)S(1)}, bf16[80,2048]{1,0:T(8,128)(2,1)S(1)}, u32[]{:S(2)}, u32[]{:S(2)}) collective-permute-start(bf16[80,2048]{1,0:T(8,128)(2,1)S(1)} %get-tuple-element.84), channel_id=1, source_target_pairs={{0,0},{1,2},{2,1},{3,3},{4,4},{5,6},{6,5},{7,7},{8,8},{9,10},{10,9... | collective-permute-start | bytes 983048 | tf_op jit(solution)/shard_map/ppermute | solution.py:573
  80.5 1.3 %collective-permute-done.13.refs_11_.refs_21_ = bf16[80,2048]{1,0:T(8,128)(2,1)S(1)} collective-permute-done((bf16[80,2048]{1,0:T(8,128)(2,1)}, bf16[80,2048]{1,0:T(8,128)(2,1)S(1)}, u32[]{:S(2)}, u32[]{:S(2)}) %collective-permute-start.13) | collective-permute-done | bytes 327712 | tf_op jit(solution)/shard_map/ppermute | solution.py:573
  81.8 8.5 %propagate.2.refs_22_ = f32[2304,512]{1,0:T(8,128)} custom-call(s32[6]{0:T(128)S(1)} %stack.70.where, f32[144,8]{1,0:T(8,128)S(1)} %copy.40.coef_ref, f32[3,16,512]{2,1,0:T(8,128)S(1)} %pad_maximum_fusion.1.fields_ref, bf16[144,1024]{1,0:T(8,128)(2,1)} %get-tuple-element.65.refs_0_, bf16[144,1024]{1,0:T(8,128)(2,1)} %get-tuple-element.46.refs_1_, ...), custom_call_target="tpu_custom_call" | custom-call | flops 31457280 | bytes 4194304 | tf_op jit(solution)/shard_map/propagate/pallas_call | solution.py:533
  90.3 9.8 %propagate.3 = f32[2304,512]{1,0:T(8,128)} custom-call(s32[6]{0:T(128)S(1)} %stack.70.where, f32[144,8]{1,0:T(8,128)S(1)} %copy.40.coef_ref, f32[3,16,512]{2,1,0:T(8,128)S(1)} %pad_maximum_fusion.1.fields_ref, bf16[144,1024]{1,0:T(8,128)(2,1)} %get-tuple-element.65.refs_0_, ...), custom_call_target="tpu_custom_call", output_to_operand_aliasing={{}: (25, {})} | custom-call | flops 39321600 | bytes 5242880 | tf_op jit(solution)/shard_map/propagate/pallas_call | solution.py:533
  (114 shorter events, 6.0 us)
Async XLA Ops:
  6.8 16.3 %collective-permute-start = (bf16[144,1024]{1,0:T(8,128)(2,1)}, bf16[144,1024]{1,0:T(8,128)(2,1)S(1)}, u32[]{:S(2)}, u32[]{:S(2)}) collective-permute-start(bf16[144,1024]{1,0:T(8,128)(2,1)} %get-tuple-element.46.refs_1_), channel_id=1, source_target_pairs={{0,8},{4,12},{8,0},{12,4},{16,24},{20,28},{24,16},{28,20},{1,9},{5... | collective-permute-start | bytes 884744 | tf_op jit(solution)/shard_map/ppermute | solution.py:118
  8.3 15.0 %collective-permute-start.1 = (bf16[144,1024]{1,0:T(8,128)(2,1)}, bf16[144,1024]{1,0:T(8,128)(2,1)S(1)}, u32[]{:S(2)}, u32[]{:S(2)}) collective-permute-start(bf16[144,1024]{1,0:T(8,128)(2,1)} %get-tuple-element.47.refs_2_), channel_id=1, source_target_pairs={{0,16},{4,20},{8,24},{12,28},{16,0},{20,4},{24,8},{28,12},{1,17},{... | collective-permute-start | bytes 884744 | tf_op jit(solution)/shard_map/ppermute | solution.py:118
  9.8 13.5 %collective-permute-start.2 = (bf16[144,1024]{1,0:T(8,128)(2,1)}, bf16[144,1024]{1,0:T(8,128)(2,1)S(1)}, u32[]{:S(2)}, u32[]{:S(2)}) collective-permute-start(bf16[144,1024]{1,0:T(8,128)(2,1)} %get-tuple-element.48.refs_3_), channel_id=1, source_target_pairs={{0,24},{4,28},{8,16},{12,20},{16,8},{20,12},{24,0},{28,4},{1,25},{... | collective-permute-start | bytes 884744 | tf_op jit(solution)/shard_map/ppermute | solution.py:118
  23.3 2.6 %collective-permute-start.5 = (bf16[144,1024]{1,0:T(8,128)(2,1)S(1)}, bf16[144,1024]{1,0:T(8,128)(2,1)S(1)}, u32[]{:S(2)}, u32[]{:S(2)}) collective-permute-start(bf16[144,1024]{1,0:T(8,128)(2,1)S(1)} %copy-done.5), channel_id=1, source_target_pairs={{0,4},{4,0},{8,12},{12,8},{16,20},{20,16},{24,28},{28,24},{1,5},{5... | collective-permute-start | bytes 884744 | tf_op jit(solution)/shard_map/ppermute | solution.py:118
  23.3 4.1 %collective-permute-start.6 = (bf16[144,1024]{1,0:T(8,128)(2,1)S(1)}, bf16[144,1024]{1,0:T(8,128)(2,1)S(1)}, u32[]{:S(2)}, u32[]{:S(2)}) collective-permute-start(bf16[144,1024]{1,0:T(8,128)(2,1)S(1)} %collective-permute-done.refs_1_), channel_id=1, source_target_pairs={{0,4},{4,0},{8,12},{12,8},{16,20},{20,16},{24,28},{28,24},{1,5},{5... | collective-permute-start | bytes 884744 | tf_op jit(solution)/shard_map/ppermute | solution.py:118
  23.8 4.1 %collective-permute-start.7 = (bf16[144,1024]{1,0:T(8,128)(2,1)S(1)}, bf16[144,1024]{1,0:T(8,128)(2,1)S(1)}, u32[]{:S(2)}, u32[]{:S(2)}) collective-permute-start(bf16[144,1024]{1,0:T(8,128)(2,1)S(1)} %collective-permute-done.1.refs_2_), channel_id=1, source_target_pairs={{0,4},{4,0},{8,12},{12,8},{16,20},{20,16},{24,28},{28,24},{1,5},{5... | collective-permute-start | bytes 884744 | tf_op jit(solution)/shard_map/ppermute | solution.py:118
  23.9 4.1 %collective-permute-start.8 = (bf16[144,1024]{1,0:T(8,128)(2,1)S(1)}, bf16[144,1024]{1,0:T(8,128)(2,1)S(1)}, u32[]{:S(2)}, u32[]{:S(2)}) collective-permute-start(bf16[144,1024]{1,0:T(8,128)(2,1)S(1)} %collective-permute-done.2.refs_3_), channel_id=1, source_target_pairs={{0,4},{4,0},{8,12},{12,8},{16,20},{20,16},{24,28},{28,24},{1,5},{5... | collective-permute-start | bytes 884744 | tf_op jit(solution)/shard_map/ppermute | solution.py:118
  24.4 12.3 %collective-permute-start.14 = (bf16[144,1024]{1,0:T(8,128)(2,1)S(1)}, bf16[144,1024]{1,0:T(8,128)(2,1)S(1)}, u32[]{:S(2)}, u32[]{:S(2)}) collective-permute-start(bf16[144,1024]{1,0:T(8,128)(2,1)S(1)} %copy-done.13), channel_id=1, source_target_pairs={{0,8},{4,12},{8,0},{12,4},{16,24},{20,28},{24,16},{28,20},{1,9},{5... | collective-permute-start | bytes 884744 | tf_op jit(solution)/shard_map/ppermute | solution.py:118
  25.9 15.0 %collective-permute-start.15 = (bf16[144,1024]{1,0:T(8,128)(2,1)S(1)}, bf16[144,1024]{1,0:T(8,128)(2,1)S(1)}, u32[]{:S(2)}, u32[]{:S(2)}) collective-permute-start(bf16[144,1024]{1,0:T(8,128)(2,1)S(1)} %copy-done.14), channel_id=1, source_target_pairs={{0,16},{4,20},{8,24},{12,28},{16,0},{20,4},{24,8},{28,12},{1,17},{... | collective-permute-start | bytes 884744 | tf_op jit(solution)/shard_map/ppermute | solution.py:118
  27.4 13.5 %collective-permute-start.16 = (bf16[144,1024]{1,0:T(8,128)(2,1)S(1)}, bf16[144,1024]{1,0:T(8,128)(2,1)}, u32[]{:S(2)}, u32[]{:S(2)}) collective-permute-start(bf16[144,1024]{1,0:T(8,128)(2,1)S(1)} %copy-done.15), channel_id=1, source_target_pairs={{0,24},{4,28},{8,16},{12,20},{16,8},{20,12},{24,0},{28,4},{1,25},{... | collective-permute-start | bytes 884744 | tf_op jit(solution)/shard_map/ppermute | solution.py:118
  40.9 2.4 %collective-permute-start.17 = (bf16[144,1024]{1,0:T(8,128)(2,1)S(1)}, bf16[144,1024]{1,0:T(8,128)(2,1)S(1)}, u32[]{:S(2)}, u32[]{:S(2)}) collective-permute-start(bf16[144,1024]{1,0:T(8,128)(2,1)S(1)} %copy-done.6), channel_id=1, source_target_pairs={{0,4},{4,0},{8,12},{12,8},{16,20},{20,16},{24,28},{28,24},{1,5},{5... | collective-permute-start | bytes 884744 | tf_op jit(solution)/shard_map/ppermute | solution.py:118
  41.0 7.0 %collective-permute-start.18 = (bf16[144,1024]{1,0:T(8,128)(2,1)S(1)}, bf16[144,1024]{1,0:T(8,128)(2,1)S(1)}, u32[]{:S(2)}, u32[]{:S(2)}) collective-permute-start(bf16[144,1024]{1,0:T(8,128)(2,1)S(1)} %collective-permute-done.14.refs_1_), channel_id=1, source_target_pairs={{0,4},{4,0},{8,12},{12,8},{16,20},{20,16},{24,28},{28,24},{1,5},{5... | collective-permute-start | bytes 884744 | tf_op jit(solution)/shard_map/ppermute | solution.py:118
  41.5 7.9 %collective-permute-start.19 = (bf16[144,1024]{1,0:T(8,128)(2,1)S(1)}, bf16[144,1024]{1,0:T(8,128)(2,1)S(1)}, u32[]{:S(2)}, u32[]{:S(2)}) collective-permute-start(bf16[144,1024]{1,0:T(8,128)(2,1)S(1)} %collective-permute-done.15.refs_2_), channel_id=1, source_target_pairs={{0,4},{4,0},{8,12},{12,8},{16,20},{20,16},{24,28},{28,24},{1,5},{5... | collective-permute-start | bytes 884744 | tf_op jit(solution)/shard_map/ppermute | solution.py:118
  41.5 9.5 %collective-permute-start.20 = (bf16[144,1024]{1,0:T(8,128)(2,1)}, bf16[144,1024]{1,0:T(8,128)(2,1)S(1)}, u32[]{:S(2)}, u32[]{:S(2)}) collective-permute-start(bf16[144,1024]{1,0:T(8,128)(2,1)} %collective-permute-done.16.refs_3_), channel_id=1, source_target_pairs={{0,4},{4,0},{8,12},{12,8},{16,20},{20,16},{24,28},{28,24},{1,5},{5... | collective-permute-start | bytes 884744 | tf_op jit(solution)/shard_map/ppermute | solution.py:118
  42.2 38.0 %copy-start.25 = (f32[144]{0:T(256)S(1)}, f32[144]{0:T(256)}, u32[]{:S(2)}) copy-start(f32[144]{0:T(256)} %param.14) | copy-start | bytes 1732
  42.2 38.0 %copy-start.26 = (f32[144]{0:T(256)S(1)}, f32[144]{0:T(256)}, u32[]{:S(2)}) copy-start(f32[144]{0:T(256)} %param.13) | copy-start | bytes 1732
  42.2 38.1 %copy-start.23 = (f32[144,2]{0,1:T(2,128)S(1)}, f32[144,2]{0,1:T(2,128)}, u32[]{:S(2)}) copy-start(f32[144,2]{0,1:T(2,128)} %param.15) | copy-start | bytes 3460
  42.9 24.2 %copy-start = (bf16[144,1024]{1,0:T(8,128)(2,1)S(1)}, bf16[144,1024]{1,0:T(8,128)(2,1)}, u32[]{:S(2)}) copy-start(bf16[144,1024]{1,0:T(8,128)(2,1)} %get-tuple-element.69.refs_0_.refs_12_) | copy-start | bytes 884740
  42.9 26.0 %collective-permute-start.3 = (bf16[144,2048]{1,0:T(8,128)(2,1)}, bf16[144,2048]{1,0:T(8,128)(2,1)S(1)}, u32[]{:S(2)}, u32[]{:S(2)}) collective-permute-start(bf16[144,2048]{1,0:T(8,128)(2,1)} %get-tuple-element.61), channel_id=1, source_target_pairs={{0,1},{1,0},{2,3},{3,2},{4,5},{5,4},{6,7},{7,6},{8,9},{9,8},{10,11... | collective-permute-start | bytes 1769480 | tf_op jit(solution)/shard_map/ppermute | solution.py:573
  43.4 25.6 %collective-permute-start.4 = (bf16[144,2048]{1,0:T(8,128)(2,1)}, bf16[144,2048]{1,0:T(8,128)(2,1)S(1)}, u32[]{:S(2)}, u32[]{:S(2)}) collective-permute-start(bf16[144,2048]{1,0:T(8,128)(2,1)} %get-tuple-element.62), channel_id=1, source_target_pairs={{0,0},{1,2},{2,1},{3,3},{4,4},{5,6},{6,5},{7,7},{8,8},{9,10},{10,9... | collective-permute-start | bytes 1769480 | tf_op jit(solution)/shard_map/ppermute | solution.py:573
  48.0 15.4 %collective-permute-start.9 = (bf16[144,1024]{1,0:T(8,128)(2,1)}, bf16[144,1024]{1,0:T(8,128)(2,1)S(1)}, u32[]{:S(2)}, u32[]{:S(2)}) collective-permute-start(bf16[144,1024]{1,0:T(8,128)(2,1)} %get-tuple-element.70), channel_id=1, source_target_pairs={{0,8},{4,12},{8,0},{12,4},{16,24},{20,28},{24,16},{28,20},{1,9},{5... | collective-permute-start | bytes 884744 | tf_op jit(solution)/shard_map/ppermute | solution.py:118
  50.1 14.7 %collective-permute-start.10 = (bf16[144,1024]{1,0:T(8,128)(2,1)}, bf16[144,1024]{1,0:T(8,128)(2,1)S(1)}, u32[]{:S(2)}, u32[]{:S(2)}) collective-permute-start(bf16[144,1024]{1,0:T(8,128)(2,1)} %get-tuple-element.71), channel_id=1, source_target_pairs={{0,16},{4,20},{8,24},{12,28},{16,0},{20,4},{24,8},{28,12},{1,17},{... | collective-permute-start | bytes 884744 | tf_op jit(solution)/shard_map/ppermute | solution.py:118
  51.8 14.0 %collective-permute-start.11 = (bf16[144,1024]{1,0:T(8,128)(2,1)}, bf16[144,1024]{1,0:T(8,128)(2,1)S(1)}, u32[]{:S(2)}, u32[]{:S(2)}) collective-permute-start(bf16[144,1024]{1,0:T(8,128)(2,1)} %get-tuple-element.72), channel_id=1, source_target_pairs={{0,24},{4,28},{8,16},{12,20},{16,8},{20,12},{24,0},{28,4},{1,25},{... | collective-permute-start | bytes 884744 | tf_op jit(solution)/shard_map/ppermute | solution.py:118
  63.4 18.4 %copy-start.1 = (bf16[144,1024]{1,0:T(8,128)(2,1)}, bf16[144,1024]{1,0:T(8,128)(2,1)S(1)}, u32[]{:S(2)}) copy-start(bf16[144,1024]{1,0:T(8,128)(2,1)S(1)} %collective-permute-done.9.refs_1_.refs_13_) | copy-start | bytes 884740
  63.4 10.2 %collective-permute-start.21 = (bf16[144,1024]{1,0:T(8,128)(2,1)}, bf16[144,1024]{1,0:T(8,128)(2,1)S(1)}, u32[]{:S(2)}, u32[]{:S(2)}) collective-permute-start(bf16[144,1024]{1,0:T(8,128)(2,1)} %get-tuple-element.80), channel_id=1, source_target_pairs={{0,8},{4,12},{8,0},{12,4},{16,24},{20,28},{24,16},{28,20},{1,9},{5... | collective-permute-start | bytes 884744 | tf_op jit(solution)/shard_map/ppermute | solution.py:118
  64.8 17.0 %copy-start.2 = (bf16[144,1024]{1,0:T(8,128)(2,1)}, bf16[144,1024]{1,0:T(8,128)(2,1)S(1)}, u32[]{:S(2)}) copy-start(bf16[144,1024]{1,0:T(8,128)(2,1)S(1)} %collective-permute-done.10.refs_2_.refs_14_) | copy-start | bytes 884740
  64.8 12.5 %collective-permute-start.22 = (bf16[144,1024]{1,0:T(8,128)(2,1)}, bf16[144,1024]{1,0:T(8,128)(2,1)S(1)}, u32[]{:S(2)}, u32[]{:S(2)}) collective-permute-start(bf16[144,1024]{1,0:T(8,128)(2,1)} %get-tuple-element.81), channel_id=1, source_target_pairs={{0,16},{4,20},{8,24},{12,28},{16,0},{20,4},{24,8},{28,12},{1,17},{... | collective-permute-start | bytes 884744 | tf_op jit(solution)/shard_map/ppermute | solution.py:118
  65.9 14.6 %collective-permute-start.23 = (bf16[144,1024]{1,0:T(8,128)(2,1)}, bf16[144,1024]{1,0:T(8,128)(2,1)}, u32[]{:S(2)}, u32[]{:S(2)}) collective-permute-start(bf16[144,1024]{1,0:T(8,128)(2,1)} %get-tuple-element.82), channel_id=1, source_target_pairs={{0,24},{4,28},{8,16},{12,20},{16,8},{20,12},{24,0},{28,4},{1,25},{... | collective-permute-start | bytes 884744 | tf_op jit(solution)/shard_map/ppermute | solution.py:118
  68.9 11.6 %collective-permute-start.12 = (bf16[80,2048]{1,0:T(8,128)(2,1)}, bf16[80,2048]{1,0:T(8,128)(2,1)S(1)}, u32[]{:S(2)}, u32[]{:S(2)}) collective-permute-start(bf16[80,2048]{1,0:T(8,128)(2,1)} %get-tuple-element.73), channel_id=1, source_target_pairs={{0,1},{1,0},{2,3},{3,2},{4,5},{5,4},{6,7},{7,6},{8,9},{9,8},{10,11... | collective-permute-start | bytes 983048 | tf_op jit(solution)/shard_map/ppermute | solution.py:573
  69.0 12.8 %collective-permute-start.13 = (bf16[80,2048]{1,0:T(8,128)(2,1)}, bf16[80,2048]{1,0:T(8,128)(2,1)S(1)}, u32[]{:S(2)}, u32[]{:S(2)}) collective-permute-start(bf16[80,2048]{1,0:T(8,128)(2,1)} %get-tuple-element.74), channel_id=1, source_target_pairs={{0,0},{1,2},{2,1},{3,3},{4,4},{5,6},{6,5},{7,7},{8,8},{9,10},{10,9... | collective-permute-start | bytes 983048 | tf_op jit(solution)/shard_map/ppermute | solution.py:573
  73.6 16.6 %collective-permute-start.24 = (bf16[80,2048]{1,0:T(8,128)(2,1)S(1)}, bf16[80,2048]{1,0:T(8,128)(2,1)S(1)}, u32[]{:S(2)}, u32[]{:S(2)}) collective-permute-start(bf16[80,2048]{1,0:T(8,128)(2,1)S(1)} %get-tuple-element.83), channel_id=1, source_target_pairs={{0,1},{1,0},{2,3},{3,2},{4,5},{5,4},{6,7},{7,6},{8,9},{9,8},{10,11... | collective-permute-start | bytes 983048 | tf_op jit(solution)/shard_map/ppermute | solution.py:573
  78.0 12.3 %collective-permute-start.25 = (bf16[80,2048]{1,0:T(8,128)(2,1)S(1)}, bf16[80,2048]{1,0:T(8,128)(2,1)S(1)}, u32[]{:S(2)}, u32[]{:S(2)}) collective-permute-start(bf16[80,2048]{1,0:T(8,128)(2,1)S(1)} %get-tuple-element.84), channel_id=1, source_target_pairs={{0,0},{1,2},{2,1},{3,3},{4,4},{5,6},{6,5},{7,7},{8,8},{9,10},{10,9... | collective-permute-start | bytes 983048 | tf_op jit(solution)/shard_map/ppermute | solution.py:573
  (21 other events, 189.3 us)

commit v3 on v2

--- a/solution.py
+++ b/solution.py
@@ -122,7 +122,7 @@
     return pltpu.with_memory_space_constraint(value, pltpu.MemorySpace.HBM)
 
 
-def spread_kernel(chips, halo, where, energy_ref, *refs):
+def spread_kernel(chips, halo, outer, where, energy_ref, *refs):
     outs, wide = refs[:-1], refs[-1]
     group, rows, width = energy_ref.shape
     for block in range(width // LANES):
@@ -140,18 +140,19 @@
     for m in range(chips):
         chip = jnp.bitwise_xor(where[0], m)
         for slot in range(2):
-            place(outs[m], slot, chip + slot * (rows - halo))
-            place(outs[chips + m], slot, chip + (slot + 1) * halo)
-        for side in range(2):
-            place(outs[2 * chips + side], m, chip + (rows - halo) * where[2 + side])
-
-
-def spread(where, energy, chips, halo):
+            first = slot * (rows - halo) if outer else (slot + 1) * halo
+            place(outs[m], slot, chip + first)
+        if not outer:
+            for side in range(2):
+                place(outs[chips + side], m, chip + (rows - halo) * where[2 + side])
+
+
+def spread(where, energy, chips, halo, outer):
     local, rows, width = energy.shape
     block = 3 * GROUP
-    sizes = [2 * width] * (2 * chips) + [halo * width] * 2
+    sizes = [2 * width] * chips + ([] if outer else [halo * width] * 2)
     return pl.pallas_call(
-        functools.partial(spread_kernel, chips, halo),
+        functools.partial(spread_kernel, chips, halo, outer),
         grid_spec=pltpu.PrefetchScalarGridSpec(
             num_scalar_prefetch=1,
             grid=(local // block,),
@@ -162,9 +163,9 @@
         out_shape=[pltpu.MemorySpace.HBM((local, size), jnp.bfloat16) for size in sizes],
         compiler_params=pltpu.CompilerParams(vmem_limit_bytes=12 * MIB),
         cost_estimate=pl.CostEstimate(
-            flops=energy.size, bytes_accessed=4 * energy.size, transcendentals=0
+            flops=energy.size, bytes_accessed=3 * energy.size, transcendentals=0
         ),
-        name="spread",
+        name="spread_outer" if outer else "spread_rest",
     )(where, energy)
 
 
@@ -221,13 +222,12 @@
 def weights_kernel(
     chips,
     where,
-    column_ref,
     row_ref,
     mixing_hbm,
     transfer_hbm,
     first_hbm,
     second_hbm,
-    pick,
+    pick_t,
     mixing_ref,
     transfer_ref,
     first_ref,
@@ -238,14 +238,21 @@
     total = mixing_ref.shape[0]
     local = total // (2 * chips)
     stripe = total // chips
-    loads = [
-        pltpu.make_async_copy(mixing_hbm, mixing_ref, in_sems.at[0]),
-        pltpu.make_async_copy(transfer_hbm, transfer_ref, in_sems.at[1]),
-    ]
+    loads = []
+    for m in range(chips):
+        block = 2 * jnp.bitwise_xor(where[0], m) + where[1]
+        loads.append(
+            pltpu.make_async_copy(
+                transfer_hbm.at[pl.ds(pl.multiple_of(block * local, GROUP), local), :],
+                transfer_ref.at[m * local : (m + 1) * local, :],
+                in_sems.at[m],
+            )
+        )
+    loads.append(pltpu.make_async_copy(mixing_hbm, mixing_ref, in_sems.at[chips]))
     for load in loads:
         load.start()
-    pick[...] = (
-        column_ref[...] == lax.broadcasted_iota(jnp.int32, (total, total), 1)
+    pick_t[...] = (
+        row_ref[...] == lax.broadcasted_iota(jnp.int32, (total, total), 0)
     ).astype(jnp.bfloat16)
     extra = first_ref.shape[0] - total
     first_ref[total:, :] = jnp.ones((extra, total), jnp.bfloat16)
@@ -260,22 +267,23 @@
         store.start()
         stores.append(store)
 
-    for load in loads:
+    for load in loads[:chips]:
         load.wait()
+    second_ref[...] = lax.dot_general(
+        transfer_ref[...],
+        pick_t[...],
+        (((1,), (1,)), ((), ())),
+        preferred_element_type=jnp.float32,
+    ).astype(jnp.bfloat16)
+    send(second_ref, second_hbm, 0, total // 2)
+    loads[chips].wait()
     for start in range(0, total, stripe):
-        rows = lax.broadcasted_iota(jnp.int32, (stripe, total), 0) + start
-        chosen = (row_ref[...] == rows).astype(jnp.bfloat16)
         first_ref[start : start + stripe, :] = jnp.dot(
-            chosen, mixing_ref[...], preferred_element_type=jnp.float32
+            pick_t[start : start + stripe, :],
+            mixing_ref[...],
+            preferred_element_type=jnp.float32,
         ).astype(jnp.bfloat16)
         send(first_ref, first_hbm, start, stripe + (extra if start + stripe == total else 0))
-    for m in range(chips):
-        block = 2 * jnp.bitwise_xor(where[0], m) + where[1]
-        rows = transfer_ref[pl.ds(pl.multiple_of(block * local, GROUP), local), :]
-        second_ref[m * local : (m + 1) * local, :] = jnp.dot(
-            rows, pick[...], preferred_element_type=jnp.float32
-        ).astype(jnp.bfloat16)
-        send(second_ref, second_hbm, m * local, local)
     for store in stores:
         store.wait()
 
@@ -287,18 +295,19 @@
     shapes = [(total + GROUP, total), (total // 2, total)]
     return pl.pallas_call(
         functools.partial(weights_kernel, chips),
-        in_specs=[pl.BlockSpec(memory_space=pltpu.SMEM)] + [whole] * 2 + [outside] * 2,
+        in_specs=[pl.BlockSpec(memory_space=pltpu.SMEM)] + [whole] + [outside] * 2,
         out_specs=[outside] * 2,
         out_shape=[pltpu.MemorySpace.HBM(shape, jnp.bfloat16) for shape in shapes],
-        scratch_shapes=[pltpu.VMEM((total, total), jnp.bfloat16)] * 3
+        scratch_shapes=[pltpu.VMEM((total, total), jnp.bfloat16)] * 2
+        + [pltpu.VMEM((total // 2, total), jnp.bfloat16)]
         + [pltpu.VMEM(shape, jnp.bfloat16) for shape in shapes]
-        + [pltpu.SemaphoreType.DMA((2,)), pltpu.SemaphoreType.DMA((2 * chips,))],
+        + [pltpu.SemaphoreType.DMA((chips + 1,)), pltpu.SemaphoreType.DMA((chips + 1,))],
         compiler_params=pltpu.CompilerParams(vmem_limit_bytes=20 * MIB),
         cost_estimate=pl.CostEstimate(
             flops=3 * total**3, bytes_accessed=8 * total**2, transcendentals=0
         ),
         name="weights",
-    )(where, pattern[:, None], pattern[None, :], in_hbm(mixing), in_hbm(transfer))
+    )(where, pattern[None, :], in_hbm(mixing), in_hbm(transfer))
 
 
 def terms_kernel(chips, where, dissip_ref, first_hbm, second_hbm, *refs):
@@ -402,7 +411,7 @@
             flops=3 * total * total * cells, bytes_accessed=8 * total * cells, transcendentals=0
         ),
         name="source_terms",
-    )(where, dissip[:, None], in_hbm(first), in_hbm(second), *near, *far)
+    )(where, dissip[:, None], in_hbm(first), in_hbm(second), *map(in_hbm, [*near, *far]))
 
 
 def propagate_kernel(chips, halo, where, coef_ref, fields_ref, *refs):
@@ -607,8 +616,8 @@
         ]
     ).astype(jnp.int32)
 
-    pieces = spread(where, energy, chips, halo)
-    outer, rest = pieces[:chips], pieces[chips:]
+    outer = spread(where, energy, chips, halo, True)
+    rest = spread(where, energy, chips, halo, False)
     near_outer = [outer[0]] + [exchange(outer[m], "comp", 2 * m) for m in range(1, chips)]
     first, second = weights(where, pattern, mixing, transfer, chips)
     near_outer, rest, first, second = lax.optimization_barrier(
@@ -624,6 +633,9 @@
         exchange(sent_outer[m], "comp", 2 * m) for m in range(1, chips)
     ]
 
+    regime_winds, regime, seeds, sea_mask, _ = lax.optimization_barrier(
+        (regime_winds, regime, seeds, sea_mask, sent_outer)
+    )
     wind_u, wind_v = strip_winds(regime_winds, regime, seeds)
     fields = jnp.stack([wind_u, wind_v, sea_mask.astype(jnp.float32)])
     upper, lower = fields[:, :halo], fields[:, rows - halo :]

time: 101 us -> 96.8 us (0.958)
  local copies, waits for them, and re-layouts: 9.29 us -> 4.41 us
  waiting for transfers between devices: 11.7 us -> 9.14 us
  Pallas kernels: 52.2 us -> 54.6 us
  starting transfers between devices: 25.9 us -> 27 us
    unnamed x54 -> x66, local copies, waits for them, and re-layouts: 5.84 us -> 3.18 us
    ppermute x20, waiting for transfers between devices: 10.4 us -> 8.52 us  [exchange(): return lax.ppermute(value, axis, [(i, i ^ distance) for i in range(count)])]
    pallas_call x1 -> x2, Pallas kernels: 5.01 us -> 6.77 us  [spread(): pl.pallas_call(functools.partial(spread_kernel, chips, halo, outer), grid...]
    pallas_call x2, Pallas kernels: 17.1 us -> 18.6 us  [source_terms(): pl.pallas_call(functools.partial(terms_kernel, chips), in_specs=[pl.Block...]
  transfers between devices with their start and end apart: 26 -> 26, of which waited for: 5 -> 5; matrix products, arithmetic and copies ran while one was open for 4% -> 2% of each run, Pallas kernels for 37% -> 44%
where the time goes in v3:
time: 96.8 us; the launch traced here: 96.3 us
  Pallas kernels  54.6 us (56%)
  starting transfers between devices  27 us (28%)
  waiting for transfers between devices  9.14 us (9%)
  local copies, waits for them, and re-layouts  4.41 us (5%)
    pallas_call x2, Pallas kernels, source_terms(): pl.pallas_call(functools.partial(terms_kernel, chips), in_specs=[pl.Block...  18.6 us
    pallas_call x2, Pallas kernels, propagate(): pl.pallas_call(kernel, grid_spec=pltpu.PrefetchScalarGridSpec(num_scalar_...  18 us
    ppermute x20, starting transfers between devices, exchange(): return lax.ppermute(value, axis, [(i, i ^ distance) for i in range(count)])  16.8 us
    ppermute x6, starting transfers between devices, pair_up(): return lax.ppermute(value, 'strip', list(enumerate(target)))  10.2 us
    pallas_call x1, Pallas kernels, weights(): pl.pallas_call(functools.partial(weights_kernel, chips), in_specs=[pl.Blo...  9.47 us
    ppermute x20, waiting for transfers between devices, exchange(): return lax.ppermute(value, axis, [(i, i ^ distance) for i in range(count)])  8.52 us
    pallas_call x2, Pallas kernels, spread(): pl.pallas_call(functools.partial(spread_kernel, chips, halo, outer), grid...  6.77 us
    unnamed x66, local copies, waits for them, and re-layouts  3.18 us
  transfers between devices with their start and end apart: 26, of which 5 were waited for; matrix products, arithmetic and copies ran while one was open for 2% of the time, Pallas kernels for 44%

profile of v3, /device:TPU:8, one launch (start us, length us, event | category | flops | bytes accessed | tf_op | source)
XLA Modules:
  0.0 96.3 jit_solution(1580114111012474720)
XLA Ops:
  0.1 1.7 %copy-done = bf16[144,16,512]{2,1,0:T(8,128)(2,1)S(1)} copy-done((bf16[144,16,512]{2,1,0:T(8,128)(2,1)S(1)}, bf16[144,16,512]{2,1,0:T(8,128)(2,1)}, u32[]{:S(2)}) %copy-start) | copy-done | bytes 2359320
  1.8 2.9 %spread_outer.1 = (bf16[144,1024]{1,0:T(8,128)(2,1)}, bf16[144,1024]{1,0:T(8,128)(2,1)}, bf16[144,1024]{1,0:T(8,128)(2,1)}, bf16[144,1024]{1,0:T(8,128)(2,1)}) custom-call(s32[6]{0:T(128)S(1)} %stack.70.where, bf16[144,16,512]{2,1,0:T(8,128)(2,1)S(1)} %copy-done), custom_call_target="tpu_custom_call" | custom-call | flops 1179648 | bytes 3538944 | tf_op jit(solution)/shard_map/spread_outer/pallas_call | solution.py:154
  4.6 1.5 %collective-permute-start = (bf16[144,1024]{1,0:T(8,128)(2,1)}, bf16[144,1024]{1,0:T(8,128)(2,1)S(1)}, u32[]{:S(2)}, u32[]{:S(2)}) collective-permute-start(bf16[144,1024]{1,0:T(8,128)(2,1)} %get-tuple-element.50.refs_1_), channel_id=1, source_target_pairs={{0,8},{4,12},{8,0},{12,4},{16,24},{20,28},{24,16},{28,20},{1,9},{5... | collective-permute-start | bytes 884744 | tf_op jit(solution)/shard_map/ppermute | solution.py:118
  6.1 1.5 %collective-permute-start.1 = (bf16[144,1024]{1,0:T(8,128)(2,1)}, bf16[144,1024]{1,0:T(8,128)(2,1)S(1)}, u32[]{:S(2)}, u32[]{:S(2)}) collective-permute-start(bf16[144,1024]{1,0:T(8,128)(2,1)} %get-tuple-element.51.refs_2_), channel_id=1, source_target_pairs={{0,16},{4,20},{8,24},{12,28},{16,0},{20,4},{24,8},{28,12},{1,17},{... | collective-permute-start | bytes 884744 | tf_op jit(solution)/shard_map/ppermute | solution.py:118
  7.6 0.5 collective-permute-start.2
  8.1 3.9 %spread_rest.1 = (bf16[144,1024]{1,0:T(8,128)(2,1)}, bf16[144,1024]{1,0:T(8,128)(2,1)}, bf16[144,1024]{1,0:T(8,128)(2,1)}, bf16[144,1024]{1,0:T(8,128)(2,1)}, bf...) custom-call(s32[6]{0:T(128)S(1)} %stack.70.where, bf16[144,16,512]{2,1,0:T(8,128)(2,1)S(1)} %copy-done), custom_call_target="tpu_custom_call" | custom-call | flops 1179648 | bytes 3538944 | tf_op jit(solution)/shard_map/spread_rest/pallas_call | solution.py:154
  12.1 9.5 %weights.1 = (bf16[1168,1152]{1,0:T(8,128)(2,1)}, bf16[576,1152]{1,0:T(8,128)(2,1)}) custom-call(s32[6]{0:T(128)S(1)} %stack.70.where, s32[1,1152]{1,0:T(1,128)S(1)} %broadcast_in_dim.22.row_ref, bf16[1152,1152]{1,0:T(8,128)(2,1)} %mixing_hbm.1, bf16[1152,1152]{1,0:T(8,128)(2,1)} %transfer_hbm.1), custom_call_target="tpu_custom_call" | custom-call | flops 4586471424 | bytes 10616832 | tf_op jit(solution)/shard_map/weights/pallas_call | solution.py:296
  21.7 0.5 collective-permute-start.4
  22.3 0.4 collective-permute-start.6
  23.0 1.6 %collective-permute-start.14 = (bf16[144,1024]{1,0:T(8,128)(2,1)S(1)}, bf16[144,1024]{1,0:T(8,128)(2,1)S(1)}, u32[]{:S(2)}, u32[]{:S(2)}) collective-permute-start(bf16[144,1024]{1,0:T(8,128)(2,1)S(1)} %copy-done.9), channel_id=1, source_target_pairs={{0,8},{4,12},{8,0},{12,4},{16,24},{20,28},{24,16},{28,20},{1,9},{5... | collective-permute-start | bytes 884744 | tf_op jit(solution)/shard_map/ppermute | solution.py:118
  24.6 1.6 %collective-permute-start.15 = (bf16[144,1024]{1,0:T(8,128)(2,1)S(1)}, bf16[144,1024]{1,0:T(8,128)(2,1)S(1)}, u32[]{:S(2)}, u32[]{:S(2)}) collective-permute-start(bf16[144,1024]{1,0:T(8,128)(2,1)S(1)} %copy-done.10), channel_id=1, source_target_pairs={{0,16},{4,20},{8,24},{12,28},{16,0},{20,4},{24,8},{28,12},{1,17},{... | collective-permute-start | bytes 884744 | tf_op jit(solution)/shard_map/ppermute | solution.py:118
  26.2 0.5 collective-permute-start.16
  26.9 0.6 copy-done.31
  27.4 0.7 copy-done.32
  28.2 9.3 %source_terms.2 = (bf16[144,1024]{1,0:T(8,128)(2,1)}, bf16[144,1024]{1,0:T(8,128)(2,1)}, bf16[144,1024]{1,0:T(8,128)(2,1)}, bf16[144,1024]{1,0:T(8,128)(2,1)}) custom-call(s32[6]{0:T(128)S(1)} %stack.70.where, f32[1152,1]{1,0:T(8,128)S(1)} %broadcast_in_dim.27.dissip_ref, bf16[1168,1152]{1,0:T(8,128)(2,1)} %get-tuple-element.61.first_hbm, ...), custom_call_target="tpu_custom_call" | custom-call | flops 4076863488 | bytes 9437184 | tf_op jit(solution)/shard_map/source_terms/pallas_call | solution.py:388
  38.4 1.2 %collective-permute-done.15.refs_2_ = bf16[144,1024]{1,0:T(8,128)(2,1)S(1)} collective-permute-done((bf16[144,1024]{1,0:T(8,128)(2,1)S(1)}, bf16[144,1024]{1,0:T(8,128)(2,1)S(1)}, u32[]{:S(2)}, u32[]{:S(2)}) %collective-permute-start.15) | collective-permute-done | bytes 294944 | tf_op jit(solution)/shard_map/ppermute | solution.py:118
  39.8 0.5 collective-permute-start.18
  41.3 3.6 %collective-permute-start.8 = (bf16[144,2048]{1,0:T(8,128)(2,1)}, bf16[144,2048]{1,0:T(8,128)(2,1)S(1)}, u32[]{:S(2)}, u32[]{:S(2)}) collective-permute-start(bf16[144,2048]{1,0:T(8,128)(2,1)} %get-tuple-element.80), channel_id=1, source_target_pairs={{0,0},{1,2},{2,1},{3,3},{4,4},{5,6},{6,5},{7,7},{8,8},{9,10},{10,9... | collective-permute-start | bytes 1769480 | tf_op jit(solution)/shard_map/ppermute | solution.py:582
  45.0 1.3 %collective-permute-start.9 = (bf16[144,1024]{1,0:T(8,128)(2,1)}, bf16[144,1024]{1,0:T(8,128)(2,1)S(1)}, u32[]{:S(2)}, u32[]{:S(2)}) collective-permute-start(bf16[144,1024]{1,0:T(8,128)(2,1)} %get-tuple-element.68), channel_id=1, source_target_pairs={{0,8},{4,12},{8,0},{12,4},{16,24},{20,28},{24,16},{28,20},{1,9},{5... | collective-permute-start | bytes 884744 | tf_op jit(solution)/shard_map/ppermute | solution.py:118
  46.3 1.5 %collective-permute-start.10 = (bf16[144,1024]{1,0:T(8,128)(2,1)}, bf16[144,1024]{1,0:T(8,128)(2,1)S(1)}, u32[]{:S(2)}, u32[]{:S(2)}) collective-permute-start(bf16[144,1024]{1,0:T(8,128)(2,1)} %get-tuple-element.69), channel_id=1, source_target_pairs={{0,16},{4,20},{8,24},{12,28},{16,0},{20,4},{24,8},{28,12},{1,17},{... | collective-permute-start | bytes 884744 | tf_op jit(solution)/shard_map/ppermute | solution.py:118
  47.8 0.8 collective-permute-start.11
  48.6 9.3 %source_terms.3 = (bf16[144,1024]{1,0:T(8,128)(2,1)}, bf16[144,1024]{1,0:T(8,128)(2,1)}, bf16[144,1024]{1,0:T(8,128)(2,1)}, bf16[144,1024]{1,0:T(8,128)(2,1)}) custom-call(s32[6]{0:T(128)S(1)} %stack.70.where, f32[1152,1]{1,0:T(8,128)S(1)} %broadcast_in_dim.27.dissip_ref, bf16[1168,1152]{1,0:T(8,128)(2,1)} %get-tuple-element.61.first_hbm, ...), custom_call_target="tpu_custom_call" | custom-call | flops 4076863488 | bytes 9437184 | tf_op jit(solution)/shard_map/source_terms/pallas_call | solution.py:388
  57.9 1.3 %collective-permute-start.21 = (bf16[144,1024]{1,0:T(8,128)(2,1)}, bf16[144,1024]{1,0:T(8,128)(2,1)S(1)}, u32[]{:S(2)}, u32[]{:S(2)}) collective-permute-start(bf16[144,1024]{1,0:T(8,128)(2,1)} %get-tuple-element.88), channel_id=1, source_target_pairs={{0,8},{4,12},{8,0},{12,4},{16,24},{20,28},{24,16},{28,20},{1,9},{5... | collective-permute-start | bytes 884744 | tf_op jit(solution)/shard_map/ppermute | solution.py:118
  59.1 1.6 %collective-permute-done.10.refs_2_.refs_14_ = bf16[144,1024]{1,0:T(8,128)(2,1)S(1)} collective-permute-done((bf16[144,1024]{1,0:T(8,128)(2,1)}, bf16[144,1024]{1,0:T(8,128)(2,1)S(1)}, u32[]{:S(2)}, u32[]{:S(2)}) %collective-permute-start.10) | collective-permute-done | bytes 294944 | tf_op jit(solution)/shard_map/ppermute | solution.py:118
  60.7 2.5 %collective-permute-start.22 = (bf16[144,1024]{1,0:T(8,128)(2,1)}, bf16[144,1024]{1,0:T(8,128)(2,1)S(1)}, u32[]{:S(2)}, u32[]{:S(2)}) collective-permute-start(bf16[144,1024]{1,0:T(8,128)(2,1)} %get-tuple-element.89), channel_id=1, source_target_pairs={{0,16},{4,20},{8,24},{12,28},{16,0},{20,4},{24,8},{28,12},{1,17},{... | collective-permute-start | bytes 884744 | tf_op jit(solution)/shard_map/ppermute | solution.py:118
  63.4 1.8 %gather_edges.1 = (bf16[80,2048]{1,0:T(8,128)(2,1)}, bf16[80,2048]{1,0:T(8,128)(2,1)}, bf16[80,2048]{1,0:T(8,128)(2,1)S(1)}, bf16[80,2048]{1,0:T(8,128)(2,1)S(1)}) custom-call(s32[6]{0:T(128)S(1)} %stack.70.where, bf16[2,16,2048]{2,1,0:T(8,128)(2,1)S(1)} %pad_maximum_fusion.extra_ref, bf16[144,1024]{1,0:T(8,128)(2,1)S(1)} %copy-done.1, ...), custom_call_target="tpu_custom_call" | custom-call | bytes 1310720 | tf_op jit(solution)/shard_map/gather_edges/pallas_call | solution.py:203
  65.3 3.3 %collective-permute-start.13 = (bf16[80,2048]{1,0:T(8,128)(2,1)}, bf16[80,2048]{1,0:T(8,128)(2,1)S(1)}, u32[]{:S(2)}, u32[]{:S(2)}) collective-permute-start(bf16[80,2048]{1,0:T(8,128)(2,1)} %get-tuple-element.82), channel_id=1, source_target_pairs={{0,0},{1,2},{2,1},{3,3},{4,4},{5,6},{6,5},{7,7},{8,8},{9,10},{10,9... | collective-permute-start | bytes 983048 | tf_op jit(solution)/shard_map/ppermute | solution.py:582
  69.0 5.5 %collective-permute-done.22.refs_18_ = bf16[144,1024]{1,0:T(8,128)(2,1)S(1)} collective-permute-done((bf16[144,1024]{1,0:T(8,128)(2,1)}, bf16[144,1024]{1,0:T(8,128)(2,1)S(1)}, u32[]{:S(2)}, u32[]{:S(2)}) %collective-permute-start.22) | collective-permute-done | bytes 294944 | tf_op jit(solution)/shard_map/ppermute | solution.py:118
  74.5 2.7 %collective-permute-start.25 = (bf16[80,2048]{1,0:T(8,128)(2,1)S(1)}, bf16[80,2048]{1,0:T(8,128)(2,1)S(1)}, u32[]{:S(2)}, u32[]{:S(2)}) collective-permute-start(bf16[80,2048]{1,0:T(8,128)(2,1)S(1)} %get-tuple-element.92), channel_id=1, source_target_pairs={{0,0},{1,2},{2,1},{3,3},{4,4},{5,6},{6,5},{7,7},{8,8},{9,10},{10,9... | collective-permute-start | bytes 983048 | tf_op jit(solution)/shard_map/ppermute | solution.py:582
  77.5 0.6 collective-permute-done.13.refs_11_.refs_21_
  78.1 8.3 %propagate.2.refs_22_ = f32[2304,512]{1,0:T(8,128)} custom-call(s32[6]{0:T(128)S(1)} %stack.70.where, f32[144,8]{1,0:T(8,128)S(1)} %copy.37.coef_ref, f32[3,16,512]{2,1,0:T(8,128)S(1)} %pad_maximum_fusion.1.fields_ref, bf16[144,1024]{1,0:T(8,128)(2,1)} %get-tuple-element.63.refs_0_, bf16[144,1024]{1,0:T(8,128)(2,1)} %get-tuple-element.50.refs_1_, ...), custom_call_target="tpu_custom_call" | custom-call | flops 31457280 | bytes 4194304 | tf_op jit(solution)/shard_map/propagate/pallas_call | solution.py:542
  86.4 9.8 %propagate.3 = f32[2304,512]{1,0:T(8,128)} custom-call(s32[6]{0:T(128)S(1)} %stack.70.where, f32[144,8]{1,0:T(8,128)S(1)} %copy.37.coef_ref, f32[3,16,512]{2,1,0:T(8,128)S(1)} %pad_maximum_fusion.1.fields_ref, bf16[144,1024]{1,0:T(8,128)(2,1)} %get-tuple-element.63.refs_0_, ...), custom_call_target="tpu_custom_call", output_to_operand_aliasing={{}: (25, {})} | custom-call | flops 39321600 | bytes 5242880 | tf_op jit(solution)/shard_map/propagate/pallas_call | solution.py:542
  (126 shorter events, 3.4 us)
Async XLA Ops:
  4.6 16.9 %collective-permute-start = (bf16[144,1024]{1,0:T(8,128)(2,1)}, bf16[144,1024]{1,0:T(8,128)(2,1)S(1)}, u32[]{:S(2)}, u32[]{:S(2)}) collective-permute-start(bf16[144,1024]{1,0:T(8,128)(2,1)} %get-tuple-element.50.refs_1_), channel_id=1, source_target_pairs={{0,8},{4,12},{8,0},{12,4},{16,24},{20,28},{24,16},{28,20},{1,9},{5... | collective-permute-start | bytes 884744 | tf_op jit(solution)/shard_map/ppermute | solution.py:118
  6.1 15.5 %collective-permute-start.1 = (bf16[144,1024]{1,0:T(8,128)(2,1)}, bf16[144,1024]{1,0:T(8,128)(2,1)S(1)}, u32[]{:S(2)}, u32[]{:S(2)}) collective-permute-start(bf16[144,1024]{1,0:T(8,128)(2,1)} %get-tuple-element.51.refs_2_), channel_id=1, source_target_pairs={{0,16},{4,20},{8,24},{12,28},{16,0},{20,4},{24,8},{28,12},{1,17},{... | collective-permute-start | bytes 884744 | tf_op jit(solution)/shard_map/ppermute | solution.py:118
  7.6 14.0 %collective-permute-start.2 = (bf16[144,1024]{1,0:T(8,128)(2,1)}, bf16[144,1024]{1,0:T(8,128)(2,1)S(1)}, u32[]{:S(2)}, u32[]{:S(2)}) collective-permute-start(bf16[144,1024]{1,0:T(8,128)(2,1)} %get-tuple-element.52.refs_3_), channel_id=1, source_target_pairs={{0,24},{4,28},{8,16},{12,20},{16,8},{20,12},{24,0},{28,4},{1,25},{... | collective-permute-start | bytes 884744 | tf_op jit(solution)/shard_map/ppermute | solution.py:118
  21.6 2.9 %collective-permute-start.3 = (bf16[144,1024]{1,0:T(8,128)(2,1)S(1)}, bf16[144,1024]{1,0:T(8,128)(2,1)S(1)}, u32[]{:S(2)}, u32[]{:S(2)}) collective-permute-start(bf16[144,1024]{1,0:T(8,128)(2,1)S(1)} %copy-done.7), channel_id=1, source_target_pairs={{0,4},{4,0},{8,12},{12,8},{16,20},{20,16},{24,28},{28,24},{1,5},{5... | collective-permute-start | bytes 884744 | tf_op jit(solution)/shard_map/ppermute | solution.py:118
  21.7 4.4 %collective-permute-start.4 = (bf16[144,1024]{1,0:T(8,128)(2,1)S(1)}, bf16[144,1024]{1,0:T(8,128)(2,1)S(1)}, u32[]{:S(2)}, u32[]{:S(2)}) collective-permute-start(bf16[144,1024]{1,0:T(8,128)(2,1)S(1)} %collective-permute-done.refs_1_), channel_id=1, source_target_pairs={{0,4},{4,0},{8,12},{12,8},{16,20},{20,16},{24,28},{28,24},{1,5},{5... | collective-permute-start | bytes 884744 | tf_op jit(solution)/shard_map/ppermute | solution.py:118
  22.2 4.5 %collective-permute-start.5 = (bf16[144,1024]{1,0:T(8,128)(2,1)S(1)}, bf16[144,1024]{1,0:T(8,128)(2,1)S(1)}, u32[]{:S(2)}, u32[]{:S(2)}) collective-permute-start(bf16[144,1024]{1,0:T(8,128)(2,1)S(1)} %collective-permute-done.1.refs_2_), channel_id=1, source_target_pairs={{0,4},{4,0},{8,12},{12,8},{16,20},{20,16},{24,28},{28,24},{1,5},{5... | collective-permute-start | bytes 884744 | tf_op jit(solution)/shard_map/ppermute | solution.py:118
  22.3 4.5 %collective-permute-start.6 = (bf16[144,1024]{1,0:T(8,128)(2,1)S(1)}, bf16[144,1024]{1,0:T(8,128)(2,1)S(1)}, u32[]{:S(2)}, u32[]{:S(2)}) collective-permute-start(bf16[144,1024]{1,0:T(8,128)(2,1)S(1)} %collective-permute-done.2.refs_3_), channel_id=1, source_target_pairs={{0,4},{4,0},{8,12},{12,8},{16,20},{20,16},{24,28},{28,24},{1,5},{5... | collective-permute-start | bytes 884744 | tf_op jit(solution)/shard_map/ppermute | solution.py:118
  23.0 15.4 %collective-permute-start.14 = (bf16[144,1024]{1,0:T(8,128)(2,1)S(1)}, bf16[144,1024]{1,0:T(8,128)(2,1)S(1)}, u32[]{:S(2)}, u32[]{:S(2)}) collective-permute-start(bf16[144,1024]{1,0:T(8,128)(2,1)S(1)} %copy-done.9), channel_id=1, source_target_pairs={{0,8},{4,12},{8,0},{12,4},{16,24},{20,28},{24,16},{28,20},{1,9},{5... | collective-permute-start | bytes 884744 | tf_op jit(solution)/shard_map/ppermute | solution.py:118
  24.6 15.1 %collective-permute-start.15 = (bf16[144,1024]{1,0:T(8,128)(2,1)S(1)}, bf16[144,1024]{1,0:T(8,128)(2,1)S(1)}, u32[]{:S(2)}, u32[]{:S(2)}) collective-permute-start(bf16[144,1024]{1,0:T(8,128)(2,1)S(1)} %copy-done.10), channel_id=1, source_target_pairs={{0,16},{4,20},{8,24},{12,28},{16,0},{20,4},{24,8},{28,12},{1,17},{... | collective-permute-start | bytes 884744 | tf_op jit(solution)/shard_map/ppermute | solution.py:118
  26.2 13.5 %collective-permute-start.16 = (bf16[144,1024]{1,0:T(8,128)(2,1)S(1)}, bf16[144,1024]{1,0:T(8,128)(2,1)}, u32[]{:S(2)}, u32[]{:S(2)}) collective-permute-start(bf16[144,1024]{1,0:T(8,128)(2,1)S(1)} %copy-done.11), channel_id=1, source_target_pairs={{0,24},{4,28},{8,16},{12,20},{16,8},{20,12},{24,0},{28,4},{1,25},{... | collective-permute-start | bytes 884744 | tf_op jit(solution)/shard_map/ppermute | solution.py:118
  26.7 38.5 %collective-permute-start.7 = (bf16[144,2048]{1,0:T(8,128)(2,1)}, bf16[144,2048]{1,0:T(8,128)(2,1)S(1)}, u32[]{:S(2)}, u32[]{:S(2)}) collective-permute-start(bf16[144,2048]{1,0:T(8,128)(2,1)} %get-tuple-element.79), channel_id=1, source_target_pairs={{0,1},{1,0},{2,3},{3,2},{4,5},{5,4},{6,7},{7,6},{8,9},{9,8},{10,11... | collective-permute-start | bytes 1769480 | tf_op jit(solution)/shard_map/ppermute | solution.py:582
  39.7 1.6 %collective-permute-start.17 = (bf16[144,1024]{1,0:T(8,128)(2,1)S(1)}, bf16[144,1024]{1,0:T(8,128)(2,1)S(1)}, u32[]{:S(2)}, u32[]{:S(2)}) collective-permute-start(bf16[144,1024]{1,0:T(8,128)(2,1)S(1)} %copy-done.8), channel_id=1, source_target_pairs={{0,4},{4,0},{8,12},{12,8},{16,20},{20,16},{24,28},{28,24},{1,5},{5... | collective-permute-start | bytes 884744 | tf_op jit(solution)/shard_map/ppermute | solution.py:118
  39.8 5.2 %collective-permute-start.18 = (bf16[144,1024]{1,0:T(8,128)(2,1)S(1)}, bf16[144,1024]{1,0:T(8,128)(2,1)}, u32[]{:S(2)}, u32[]{:S(2)}) collective-permute-start(bf16[144,1024]{1,0:T(8,128)(2,1)S(1)} %collective-permute-done.14.refs_1_), channel_id=1, source_target_pairs={{0,4},{4,0},{8,12},{12,8},{16,20},{20,16},{24,28},{28,24},{1,5},{5... | collective-permute-start | bytes 884744 | tf_op jit(solution)/shard_map/ppermute | solution.py:118
  40.2 6.0 %collective-permute-start.19 = (bf16[144,1024]{1,0:T(8,128)(2,1)S(1)}, bf16[144,1024]{1,0:T(8,128)(2,1)}, u32[]{:S(2)}, u32[]{:S(2)}) collective-permute-start(bf16[144,1024]{1,0:T(8,128)(2,1)S(1)} %collective-permute-done.15.refs_2_), channel_id=1, source_target_pairs={{0,4},{4,0},{8,12},{12,8},{16,20},{20,16},{24,28},{28,24},{1,5},{5... | collective-permute-start | bytes 884744 | tf_op jit(solution)/shard_map/ppermute | solution.py:118
  40.3 7.5 %collective-permute-start.20 = (bf16[144,1024]{1,0:T(8,128)(2,1)}, bf16[144,1024]{1,0:T(8,128)(2,1)}, u32[]{:S(2)}, u32[]{:S(2)}) collective-permute-start(bf16[144,1024]{1,0:T(8,128)(2,1)} %collective-permute-done.16.refs_3_), channel_id=1, source_target_pairs={{0,4},{4,0},{8,12},{12,8},{16,20},{20,16},{24,28},{28,24},{1,5},{5... | collective-permute-start | bytes 884744 | tf_op jit(solution)/shard_map/ppermute | solution.py:118
  41.0 22.4 %copy-start.1 = (bf16[144,1024]{1,0:T(8,128)(2,1)S(1)}, bf16[144,1024]{1,0:T(8,128)(2,1)}, u32[]{:S(2)}) copy-start(bf16[144,1024]{1,0:T(8,128)(2,1)} %get-tuple-element.67.refs_0_.refs_12_) | copy-start | bytes 884740
  41.0 36.2 %copy-start.21 = (f32[144]{0:T(256)S(1)}, f32[144]{0:T(256)}, u32[]{:S(2)}) copy-start(f32[144]{0:T(256)} %param.14) | copy-start | bytes 1732
  41.1 36.2 %copy-start.22 = (f32[144]{0:T(256)S(1)}, f32[144]{0:T(256)}, u32[]{:S(2)}) copy-start(f32[144]{0:T(256)} %param.13) | copy-start | bytes 1732
  41.1 36.2 %copy-start.19 = (f32[144,2]{0,1:T(2,128)S(1)}, f32[144,2]{0,1:T(2,128)}, u32[]{:S(2)}) copy-start(f32[144,2]{0,1:T(2,128)} %param.15) | copy-start | bytes 3460
  41.3 24.0 %collective-permute-start.8 = (bf16[144,2048]{1,0:T(8,128)(2,1)}, bf16[144,2048]{1,0:T(8,128)(2,1)S(1)}, u32[]{:S(2)}, u32[]{:S(2)}) collective-permute-start(bf16[144,2048]{1,0:T(8,128)(2,1)} %get-tuple-element.80), channel_id=1, source_target_pairs={{0,0},{1,2},{2,1},{3,3},{4,4},{5,6},{6,5},{7,7},{8,8},{9,10},{10,9... | collective-permute-start | bytes 1769480 | tf_op jit(solution)/shard_map/ppermute | solution.py:582
  45.0 12.9 %collective-permute-start.9 = (bf16[144,1024]{1,0:T(8,128)(2,1)}, bf16[144,1024]{1,0:T(8,128)(2,1)S(1)}, u32[]{:S(2)}, u32[]{:S(2)}) collective-permute-start(bf16[144,1024]{1,0:T(8,128)(2,1)} %get-tuple-element.68), channel_id=1, source_target_pairs={{0,8},{4,12},{8,0},{12,4},{16,24},{20,28},{24,16},{28,20},{1,9},{5... | collective-permute-start | bytes 884744 | tf_op jit(solution)/shard_map/ppermute | solution.py:118
  46.3 14.4 %collective-permute-start.10 = (bf16[144,1024]{1,0:T(8,128)(2,1)}, bf16[144,1024]{1,0:T(8,128)(2,1)S(1)}, u32[]{:S(2)}, u32[]{:S(2)}) collective-permute-start(bf16[144,1024]{1,0:T(8,128)(2,1)} %get-tuple-element.69), channel_id=1, source_target_pairs={{0,16},{4,20},{8,24},{12,28},{16,0},{20,4},{24,8},{28,12},{1,17},{... | collective-permute-start | bytes 884744 | tf_op jit(solution)/shard_map/ppermute | solution.py:118
  47.8 15.5 %collective-permute-start.11 = (bf16[144,1024]{1,0:T(8,128)(2,1)}, bf16[144,1024]{1,0:T(8,128)(2,1)S(1)}, u32[]{:S(2)}, u32[]{:S(2)}) collective-permute-start(bf16[144,1024]{1,0:T(8,128)(2,1)} %get-tuple-element.70), channel_id=1, source_target_pairs={{0,24},{4,28},{8,16},{12,20},{16,8},{20,12},{24,0},{28,4},{1,25},{... | collective-permute-start | bytes 884744 | tf_op jit(solution)/shard_map/ppermute | solution.py:118
  57.8 20.2 %copy-start.2 = (bf16[144,1024]{1,0:T(8,128)(2,1)}, bf16[144,1024]{1,0:T(8,128)(2,1)S(1)}, u32[]{:S(2)}) copy-start(bf16[144,1024]{1,0:T(8,128)(2,1)S(1)} %collective-permute-done.9.refs_1_.refs_13_) | copy-start | bytes 884740
  57.9 10.8 %collective-permute-start.21 = (bf16[144,1024]{1,0:T(8,128)(2,1)}, bf16[144,1024]{1,0:T(8,128)(2,1)S(1)}, u32[]{:S(2)}, u32[]{:S(2)}) collective-permute-start(bf16[144,1024]{1,0:T(8,128)(2,1)} %get-tuple-element.88), channel_id=1, source_target_pairs={{0,8},{4,12},{8,0},{12,4},{16,24},{20,28},{24,16},{28,20},{1,9},{5... | collective-permute-start | bytes 884744 | tf_op jit(solution)/shard_map/ppermute | solution.py:118
  60.7 17.4 %copy-start.3 = (bf16[144,1024]{1,0:T(8,128)(2,1)}, bf16[144,1024]{1,0:T(8,128)(2,1)S(1)}, u32[]{:S(2)}) copy-start(bf16[144,1024]{1,0:T(8,128)(2,1)S(1)} %collective-permute-done.10.refs_2_.refs_14_) | copy-start | bytes 884740
  60.7 13.7 %collective-permute-start.22 = (bf16[144,1024]{1,0:T(8,128)(2,1)}, bf16[144,1024]{1,0:T(8,128)(2,1)S(1)}, u32[]{:S(2)}, u32[]{:S(2)}) collective-permute-start(bf16[144,1024]{1,0:T(8,128)(2,1)} %get-tuple-element.89), channel_id=1, source_target_pairs={{0,16},{4,20},{8,24},{12,28},{16,0},{20,4},{24,8},{28,12},{1,17},{... | collective-permute-start | bytes 884744 | tf_op jit(solution)/shard_map/ppermute | solution.py:118
  63.3 14.2 %collective-permute-start.23 = (bf16[144,1024]{1,0:T(8,128)(2,1)}, bf16[144,1024]{1,0:T(8,128)(2,1)}, u32[]{:S(2)}, u32[]{:S(2)}) collective-permute-start(bf16[144,1024]{1,0:T(8,128)(2,1)} %get-tuple-element.90), channel_id=1, source_target_pairs={{0,24},{4,28},{8,16},{12,20},{16,8},{20,12},{24,0},{28,4},{1,25},{... | collective-permute-start | bytes 884744 | tf_op jit(solution)/shard_map/ppermute | solution.py:118
  65.2 12.2 %collective-permute-start.12 = (bf16[80,2048]{1,0:T(8,128)(2,1)}, bf16[80,2048]{1,0:T(8,128)(2,1)S(1)}, u32[]{:S(2)}, u32[]{:S(2)}) collective-permute-start(bf16[80,2048]{1,0:T(8,128)(2,1)} %get-tuple-element.81), channel_id=1, source_target_pairs={{0,1},{1,0},{2,3},{3,2},{4,5},{5,4},{6,7},{7,6},{8,9},{9,8},{10,11... | collective-permute-start | bytes 983048 | tf_op jit(solution)/shard_map/ppermute | solution.py:582
  65.3 12.8 %collective-permute-start.13 = (bf16[80,2048]{1,0:T(8,128)(2,1)}, bf16[80,2048]{1,0:T(8,128)(2,1)S(1)}, u32[]{:S(2)}, u32[]{:S(2)}) collective-permute-start(bf16[80,2048]{1,0:T(8,128)(2,1)} %get-tuple-element.82), channel_id=1, source_target_pairs={{0,0},{1,2},{2,1},{3,3},{4,4},{5,6},{6,5},{7,7},{8,8},{9,10},{10,9... | collective-permute-start | bytes 983048 | tf_op jit(solution)/shard_map/ppermute | solution.py:582
  68.7 17.7 %collective-permute-start.24 = (bf16[80,2048]{1,0:T(8,128)(2,1)S(1)}, bf16[80,2048]{1,0:T(8,128)(2,1)S(1)}, u32[]{:S(2)}, u32[]{:S(2)}) collective-permute-start(bf16[80,2048]{1,0:T(8,128)(2,1)S(1)} %get-tuple-element.91), channel_id=1, source_target_pairs={{0,1},{1,0},{2,3},{3,2},{4,5},{5,4},{6,7},{7,6},{8,9},{9,8},{10,11... | collective-permute-start | bytes 983048 | tf_op jit(solution)/shard_map/ppermute | solution.py:582
  74.5 11.9 %collective-permute-start.25 = (bf16[80,2048]{1,0:T(8,128)(2,1)S(1)}, bf16[80,2048]{1,0:T(8,128)(2,1)S(1)}, u32[]{:S(2)}, u32[]{:S(2)}) collective-permute-start(bf16[80,2048]{1,0:T(8,128)(2,1)S(1)} %get-tuple-element.92), channel_id=1, source_target_pairs={{0,0},{1,2},{2,1},{3,3},{4,4},{5,6},{6,5},{7,7},{8,8},{9,10},{10,9... | collective-permute-start | bytes 983048 | tf_op jit(solution)/shard_map/ppermute | solution.py:582
  (27 other events, 232.8 us)

commit v4 on v3

--- a/solution.py
+++ b/solution.py
@@ -123,28 +123,41 @@
 
 
 def spread_kernel(chips, halo, outer, where, energy_ref, *refs):
-    outs, wide = refs[:-1], refs[-1]
-    group, rows, width = energy_ref.shape
-    for block in range(width // LANES):
-        lanes = slice(block * LANES, (block + 1) * LANES)
-        wide[block] = (
-            energy_ref[:, :, lanes].astype(jnp.float32).reshape(group * rows, LANES)
-        )
-
-    def place(out_ref, slot, row):
+    count = chips + (0 if outer else 2)
+    targets, outs, (wide, sems) = refs[:count], refs[count : 2 * count], refs[2 * count :]
+    local, rows, width = energy_ref.shape
+    group = wide.shape[1] // rows
+    sent = []
+    for index in range(local // group):
+        mine = slice(index * group, (index + 1) * group)
         for block in range(width // LANES):
-            start = slot * width + block * LANES
-            picked = wide[block, pl.ds(row, group, stride=rows), :]
-            out_ref[:, start : start + LANES] = picked.astype(jnp.bfloat16)
-
-    for m in range(chips):
-        chip = jnp.bitwise_xor(where[0], m)
-        for slot in range(2):
-            first = slot * (rows - halo) if outer else (slot + 1) * halo
-            place(outs[m], slot, chip + first)
-        if not outer:
-            for side in range(2):
-                place(outs[chips + side], m, chip + (rows - halo) * where[2 + side])
+            lanes = slice(block * LANES, (block + 1) * LANES)
+            wide[block] = (
+                energy_ref[mine, :, lanes].astype(jnp.float32).reshape(group * rows, LANES)
+            )
+
+        def place(out_ref, slot, row):
+            for block in range(width // LANES):
+                start = slot * width + block * LANES
+                picked = wide[block, pl.ds(row, group, stride=rows), :]
+                out_ref[mine, start : start + LANES] = picked.astype(jnp.bfloat16)
+
+        for m in range(chips):
+            chip = jnp.bitwise_xor(where[0], m)
+            for slot in range(2):
+                first = slot * (rows - halo) if outer else (slot + 1) * halo
+                place(outs[m], slot, chip + first)
+            if not outer:
+                for side in range(2):
+                    place(outs[chips + side], m, chip + (rows - halo) * where[2 + side])
+        for number in range(count):
+            copy = pltpu.make_async_copy(
+                outs[number].at[mine, :], targets[number].at[mine, :], sems.at[index, number]
+            )
+            copy.start()
+            sent.append(copy)
+    for copy in sent:
+        copy.wait()
 
 
 def spread(where, energy, chips, halo, outer):
@@ -153,14 +166,17 @@
     sizes = [2 * width] * chips + ([] if outer else [halo * width] * 2)
     return pl.pallas_call(
         functools.partial(spread_kernel, chips, halo, outer),
-        grid_spec=pltpu.PrefetchScalarGridSpec(
-            num_scalar_prefetch=1,
-            grid=(local // block,),
-            in_specs=[pl.BlockSpec((block, rows, width), lambda i, w: (i, 0, 0))],
-            out_specs=[pl.BlockSpec((block, size), lambda i, w: (i, 0)) for size in sizes],
-            scratch_shapes=[pltpu.VMEM((width // LANES, block * rows, LANES), jnp.float32)],
-        ),
+        in_specs=[
+            pl.BlockSpec(memory_space=pltpu.SMEM),
+            pl.BlockSpec(memory_space=pltpu.VMEM),
+        ],
+        out_specs=[pl.BlockSpec(memory_space=pltpu.MemorySpace.HBM)] * len(sizes),
         out_shape=[pltpu.MemorySpace.HBM((local, size), jnp.bfloat16) for size in sizes],
+        scratch_shapes=[pltpu.VMEM((local, size), jnp.bfloat16) for size in sizes]
+        + [
+            pltpu.VMEM((width // LANES, block * rows, LANES), jnp.float32),
+            pltpu.SemaphoreType.DMA((local // block, len(sizes))),
+        ],
         compiler_params=pltpu.CompilerParams(vmem_limit_bytes=12 * MIB),
         cost_estimate=pl.CostEstimate(
             flops=energy.size, bytes_accessed=3 * energy.size, transcendentals=0
@@ -344,10 +360,12 @@
             )
         )
     load = pltpu.make_async_copy(second_hbm, second_ref, weight_sems.at[chips])
-    for copy in [*copies, *stripes, load]:
+    for copy in [*copies, stripes[0]]:
         copy.start()
     for copy in copies:
         copy.wait()
+    for copy in [*stripes[1:], load]:
+        copy.start()
 
     for index in range(chips):
         start = index * stripe
@@ -667,6 +685,7 @@
         exchange(sent_middle[m], "comp", 2 * m) for m in range(1, chips)
     ]
 
+    landed_outer, _ = lax.optimization_barrier((landed_outer, sent_middle))
     edges = gather_edges(where, extra, landed_outer, parts)
     edges = [pair_up(edge, index % 2) for index, edge in enumerate(edges)]
     landed = [*landed_outer, *landed_middle]

time: 96.8 us -> 96.6 us (level)
  Pallas kernels: 54.6 us -> 53.4 us
  waiting for transfers between devices: 9.14 us -> 10.3 us
  transfers between devices with their start and end apart: 26 -> 26, of which waited for: 5 -> 5; matrix products, arithmetic and copies ran while one was open for 2% -> 2% of each run, Pallas kernels for 44% -> 43%
where the time goes in v4:
time: 96.6 us; the launch traced here: 96.2 us
  Pallas kernels  53.4 us (55%)
  starting transfers between devices  26.9 us (28%)
  waiting for transfers between devices  10.3 us (11%)
  local copies, waits for them, and re-layouts  4.41 us (5%)
    pallas_call x2, Pallas kernels, propagate(): pl.pallas_call(kernel, grid_spec=pltpu.PrefetchScalarGridSpec(num_scalar_...  18 us
    pallas_call x2, Pallas kernels, source_terms(): pl.pallas_call(functools.partial(terms_kernel, chips), in_specs=[pl.Block...  17.8 us
    ppermute x20, starting transfers between devices, exchange(): return lax.ppermute(value, axis, [(i, i ^ distance) for i in range(count)])  17.3 us
    ppermute x6, starting transfers between devices, pair_up(): return lax.ppermute(value, 'strip', list(enumerate(target)))  9.62 us
    pallas_call x1, Pallas kernels, weights(): pl.pallas_call(functools.partial(weights_kernel, chips), in_specs=[pl.Blo...  9.47 us
    ppermute x20, waiting for transfers between devices, exchange(): return lax.ppermute(value, axis, [(i, i ^ distance) for i in range(count)])  8.74 us
    pallas_call x2, Pallas kernels, spread(): pl.pallas_call(functools.partial(spread_kernel, chips, halo, outer), in_s...  6.32 us
    unnamed x66, local copies, waits for them, and re-layouts  3.18 us
  transfers between devices with their start and end apart: 26, of which 5 were waited for; matrix products, arithmetic and copies ran while one was open for 2% of the time, Pallas kernels for 43%

profile of v4, /device:TPU:8, one launch (start us, length us, event | category | flops | bytes accessed | tf_op | source)
XLA Modules:
  0.0 96.2 jit_solution(8684002867363788098)
XLA Ops:
  0.1 1.7 %copy-done = bf16[144,16,512]{2,1,0:T(8,128)(2,1)S(1)} copy-done((bf16[144,16,512]{2,1,0:T(8,128)(2,1)S(1)}, bf16[144,16,512]{2,1,0:T(8,128)(2,1)}, u32[]{:S(2)}) %copy-start) | copy-done | bytes 2359320
  1.8 2.6 %spread_outer.1 = (bf16[144,1024]{1,0:T(8,128)(2,1)}, bf16[144,1024]{1,0:T(8,128)(2,1)}, bf16[144,1024]{1,0:T(8,128)(2,1)}, bf16[144,1024]{1,0:T(8,128)(2,1)}) custom-call(s32[6]{0:T(128)S(1)} %stack.70.where, bf16[144,16,512]{2,1,0:T(8,128)(2,1)S(1)} %copy-done), custom_call_target="tpu_custom_call" | custom-call | flops 1179648 | bytes 3538944 | tf_op jit(solution)/shard_map/spread_outer/pallas_call | solution.py:167
  4.3 1.6 %collective-permute-start = (bf16[144,1024]{1,0:T(8,128)(2,1)}, bf16[144,1024]{1,0:T(8,128)(2,1)S(1)}, u32[]{:S(2)}, u32[]{:S(2)}) collective-permute-start(bf16[144,1024]{1,0:T(8,128)(2,1)} %get-tuple-element.54.refs_1_), channel_id=1, source_target_pairs={{0,8},{4,12},{8,0},{12,4},{16,24},{20,28},{24,16},{28,20},{1,9},{5... | collective-permute-start | bytes 884744 | tf_op jit(solution)/shard_map/ppermute | solution.py:118
  5.9 1.5 %collective-permute-start.1 = (bf16[144,1024]{1,0:T(8,128)(2,1)}, bf16[144,1024]{1,0:T(8,128)(2,1)S(1)}, u32[]{:S(2)}, u32[]{:S(2)}) collective-permute-start(bf16[144,1024]{1,0:T(8,128)(2,1)} %get-tuple-element.55.refs_2_), channel_id=1, source_target_pairs={{0,16},{4,20},{8,24},{12,28},{16,0},{20,4},{24,8},{28,12},{1,17},{... | collective-permute-start | bytes 884744 | tf_op jit(solution)/shard_map/ppermute | solution.py:118
  7.4 0.5 collective-permute-start.2
  7.9 3.8 %spread_rest.1 = (bf16[144,1024]{1,0:T(8,128)(2,1)}, bf16[144,1024]{1,0:T(8,128)(2,1)}, bf16[144,1024]{1,0:T(8,128)(2,1)}, bf16[144,1024]{1,0:T(8,128)(2,1)}, bf...) custom-call(s32[6]{0:T(128)S(1)} %stack.70.where, bf16[144,16,512]{2,1,0:T(8,128)(2,1)S(1)} %copy-done), custom_call_target="tpu_custom_call" | custom-call | flops 1179648 | bytes 3538944 | tf_op jit(solution)/shard_map/spread_rest/pallas_call | solution.py:167
  11.7 9.5 %weights.1 = (bf16[1168,1152]{1,0:T(8,128)(2,1)}, bf16[576,1152]{1,0:T(8,128)(2,1)}) custom-call(s32[6]{0:T(128)S(1)} %stack.70.where, s32[1,1152]{1,0:T(1,128)S(1)} %broadcast_in_dim.22.row_ref, bf16[1152,1152]{1,0:T(8,128)(2,1)} %mixing_hbm.1, bf16[1152,1152]{1,0:T(8,128)(2,1)} %transfer_hbm.1), custom_call_target="tpu_custom_call" | custom-call | flops 4586471424 | bytes 10616832 | tf_op jit(solution)/shard_map/weights/pallas_call | solution.py:312
  21.4 0.5 collective-permute-start.4
  22.6 1.6 %collective-permute-start.12 = (bf16[144,1024]{1,0:T(8,128)(2,1)S(1)}, bf16[144,1024]{1,0:T(8,128)(2,1)S(1)}, u32[]{:S(2)}, u32[]{:S(2)}) collective-permute-start(bf16[144,1024]{1,0:T(8,128)(2,1)S(1)} %copy-done.9), channel_id=1, source_target_pairs={{0,8},{4,12},{8,0},{12,4},{16,24},{20,28},{24,16},{28,20},{1,9},{5... | collective-permute-start | bytes 884744 | tf_op jit(solution)/shard_map/ppermute | solution.py:118
  24.2 1.6 %collective-permute-start.13 = (bf16[144,1024]{1,0:T(8,128)(2,1)S(1)}, bf16[144,1024]{1,0:T(8,128)(2,1)S(1)}, u32[]{:S(2)}, u32[]{:S(2)}) collective-permute-start(bf16[144,1024]{1,0:T(8,128)(2,1)S(1)} %copy-done.10), channel_id=1, source_target_pairs={{0,16},{4,20},{8,24},{12,28},{16,0},{20,4},{24,8},{28,12},{1,17},{... | collective-permute-start | bytes 884744 | tf_op jit(solution)/shard_map/ppermute | solution.py:118
  25.8 0.5 collective-permute-start.14
  26.5 0.6 copy-done.31
  27.1 0.7 copy-done.32
  27.8 9.0 %source_terms.2 = (bf16[144,1024]{1,0:T(8,128)(2,1)}, bf16[144,1024]{1,0:T(8,128)(2,1)}, bf16[144,1024]{1,0:T(8,128)(2,1)}, bf16[144,1024]{1,0:T(8,128)(2,1)}) custom-call(s32[6]{0:T(128)S(1)} %stack.70.where, f32[1152,1]{1,0:T(8,128)S(1)} %broadcast_in_dim.27.dissip_ref, bf16[1168,1152]{1,0:T(8,128)(2,1)} %get-tuple-element.65.first_hbm, ...), custom_call_target="tpu_custom_call" | custom-call | flops 4076863488 | bytes 9437184 | tf_op jit(solution)/shard_map/source_terms/pallas_call | solution.py:406
  37.8 1.5 %collective-permute-done.13.refs_2_ = bf16[144,1024]{1,0:T(8,128)(2,1)S(1)} collective-permute-done((bf16[144,1024]{1,0:T(8,128)(2,1)S(1)}, bf16[144,1024]{1,0:T(8,128)(2,1)S(1)}, u32[]{:S(2)}, u32[]{:S(2)}) %collective-permute-start.13) | collective-permute-done | bytes 294944 | tf_op jit(solution)/shard_map/ppermute | solution.py:118
  39.4 0.5 collective-permute-start.16
  41.0 3.5 %collective-permute-start.8 = (bf16[144,2048]{1,0:T(8,128)(2,1)}, bf16[144,2048]{1,0:T(8,128)(2,1)S(1)}, u32[]{:S(2)}, u32[]{:S(2)}) collective-permute-start(bf16[144,2048]{1,0:T(8,128)(2,1)} %get-tuple-element.84), channel_id=1, source_target_pairs={{0,0},{1,2},{2,1},{3,3},{4,4},{5,6},{6,5},{7,7},{8,8},{9,10},{10,9... | collective-permute-start | bytes 1769480 | tf_op jit(solution)/shard_map/ppermute | solution.py:600
  44.5 1.6 %collective-permute-start.9 = (bf16[144,1024]{1,0:T(8,128)(2,1)}, bf16[144,1024]{1,0:T(8,128)(2,1)S(1)}, u32[]{:S(2)}, u32[]{:S(2)}) collective-permute-start(bf16[144,1024]{1,0:T(8,128)(2,1)} %get-tuple-element.72), channel_id=1, source_target_pairs={{0,8},{4,12},{8,0},{12,4},{16,24},{20,28},{24,16},{28,20},{1,9},{5... | collective-permute-start | bytes 884744 | tf_op jit(solution)/shard_map/ppermute | solution.py:118
  46.1 0.9 collective-permute-start.10
  47.0 1.0 %collective-permute-start.11 = (bf16[144,1024]{1,0:T(8,128)(2,1)}, bf16[144,1024]{1,0:T(8,128)(2,1)S(1)}, u32[]{:S(2)}, u32[]{:S(2)}) collective-permute-start(bf16[144,1024]{1,0:T(8,128)(2,1)} %get-tuple-element.74), channel_id=1, source_target_pairs={{0,24},{4,28},{8,16},{12,20},{16,8},{20,12},{24,0},{28,4},{1,25},{... | collective-permute-start | bytes 884744 | tf_op jit(solution)/shard_map/ppermute | solution.py:118
  48.0 8.8 %source_terms.3 = (bf16[144,1024]{1,0:T(8,128)(2,1)}, bf16[144,1024]{1,0:T(8,128)(2,1)}, bf16[144,1024]{1,0:T(8,128)(2,1)}, bf16[144,1024]{1,0:T(8,128)(2,1)}) custom-call(s32[6]{0:T(128)S(1)} %stack.70.where, f32[1152,1]{1,0:T(8,128)S(1)} %broadcast_in_dim.27.dissip_ref, bf16[1168,1152]{1,0:T(8,128)(2,1)} %get-tuple-element.65.first_hbm, ...), custom_call_target="tpu_custom_call" | custom-call | flops 4076863488 | bytes 9437184 | tf_op jit(solution)/shard_map/source_terms/pallas_call | solution.py:406
  56.9 1.6 %collective-permute-start.21 = (bf16[144,1024]{1,0:T(8,128)(2,1)}, bf16[144,1024]{1,0:T(8,128)(2,1)S(1)}, u32[]{:S(2)}, u32[]{:S(2)}) collective-permute-start(bf16[144,1024]{1,0:T(8,128)(2,1)} %get-tuple-element.90), channel_id=1, source_target_pairs={{0,8},{4,12},{8,0},{12,4},{16,24},{20,28},{24,16},{28,20},{1,9},{5... | collective-permute-start | bytes 884744 | tf_op jit(solution)/shard_map/ppermute | solution.py:118
  58.5 2.1 %collective-permute-done.10.refs_2_.refs_14_ = bf16[144,1024]{1,0:T(8,128)(2,1)S(1)} collective-permute-done((bf16[144,1024]{1,0:T(8,128)(2,1)}, bf16[144,1024]{1,0:T(8,128)(2,1)S(1)}, u32[]{:S(2)}, u32[]{:S(2)}) %collective-permute-start.10) | collective-permute-done | bytes 294944 | tf_op jit(solution)/shard_map/ppermute | solution.py:118
  60.6 1.6 %collective-permute-start.22 = (bf16[144,1024]{1,0:T(8,128)(2,1)}, bf16[144,1024]{1,0:T(8,128)(2,1)S(1)}, u32[]{:S(2)}, u32[]{:S(2)}) collective-permute-start(bf16[144,1024]{1,0:T(8,128)(2,1)} %get-tuple-element.91), channel_id=1, source_target_pairs={{0,16},{4,20},{8,24},{12,28},{16,0},{20,4},{24,8},{28,12},{1,17},{... | collective-permute-start | bytes 884744 | tf_op jit(solution)/shard_map/ppermute | solution.py:118
  62.3 1.1 %collective-permute-start.23 = (bf16[144,1024]{1,0:T(8,128)(2,1)}, bf16[144,1024]{1,0:T(8,128)(2,1)}, u32[]{:S(2)}, u32[]{:S(2)}) collective-permute-start(bf16[144,1024]{1,0:T(8,128)(2,1)} %get-tuple-element.92), channel_id=1, source_target_pairs={{0,24},{4,28},{8,16},{12,20},{16,8},{20,12},{24,0},{28,4},{1,25},{... | collective-permute-start | bytes 884744 | tf_op jit(solution)/shard_map/ppermute | solution.py:118
  63.4 1.8 %gather_edges.1 = (bf16[80,2048]{1,0:T(8,128)(2,1)}, bf16[80,2048]{1,0:T(8,128)(2,1)}, bf16[80,2048]{1,0:T(8,128)(2,1)S(1)}, bf16[80,2048]{1,0:T(8,128)(2,1)S(1)}) custom-call(s32[6]{0:T(128)S(1)} %stack.70.where, bf16[2,16,2048]{2,1,0:T(8,128)(2,1)S(1)} %pad_maximum_fusion.extra_ref, bf16[144,1024]{1,0:T(8,128)(2,1)S(1)} %copy-done.1, ...), custom_call_target="tpu_custom_call" | custom-call | bytes 1310720 | tf_op jit(solution)/shard_map/gather_edges/pallas_call | solution.py:219
  65.3 3.2 %collective-permute-start.20 = (bf16[80,2048]{1,0:T(8,128)(2,1)}, bf16[80,2048]{1,0:T(8,128)(2,1)S(1)}, u32[]{:S(2)}, u32[]{:S(2)}) collective-permute-start(bf16[80,2048]{1,0:T(8,128)(2,1)} %get-tuple-element.98), channel_id=1, source_target_pairs={{0,0},{1,2},{2,1},{3,3},{4,4},{5,6},{6,5},{7,7},{8,8},{9,10},{10,9... | collective-permute-start | bytes 983048 | tf_op jit(solution)/shard_map/ppermute | solution.py:600
  68.9 4.9 %collective-permute-done.22.refs_18_ = bf16[144,1024]{1,0:T(8,128)(2,1)S(1)} collective-permute-done((bf16[144,1024]{1,0:T(8,128)(2,1)}, bf16[144,1024]{1,0:T(8,128)(2,1)S(1)}, u32[]{:S(2)}, u32[]{:S(2)}) %collective-permute-start.22) | collective-permute-done | bytes 294944 | tf_op jit(solution)/shard_map/ppermute | solution.py:118
  73.8 2.4 %collective-permute-start.25 = (bf16[80,2048]{1,0:T(8,128)(2,1)S(1)}, bf16[80,2048]{1,0:T(8,128)(2,1)S(1)}, u32[]{:S(2)}, u32[]{:S(2)}) collective-permute-start(bf16[80,2048]{1,0:T(8,128)(2,1)S(1)} %get-tuple-element.100), channel_id=1, source_target_pairs={{0,0},{1,2},{2,1},{3,3},{4,4},{5,6},{6,5},{7,7},{8,8},{9,10},{10,9... | collective-permute-start | bytes 983048 | tf_op jit(solution)/shard_map/ppermute | solution.py:600
  76.5 1.5 %collective-permute-done.20.refs_11_.refs_21_ = bf16[80,2048]{1,0:T(8,128)(2,1)S(1)} collective-permute-done((bf16[80,2048]{1,0:T(8,128)(2,1)}, bf16[80,2048]{1,0:T(8,128)(2,1)S(1)}, u32[]{:S(2)}, u32[]{:S(2)}) %collective-permute-start.20) | collective-permute-done | bytes 327712 | tf_op jit(solution)/shard_map/ppermute | solution.py:600
  78.0 8.3 %propagate.2.refs_22_ = f32[2304,512]{1,0:T(8,128)} custom-call(s32[6]{0:T(128)S(1)} %stack.70.where, f32[144,8]{1,0:T(8,128)S(1)} %copy.37.coef_ref, f32[3,16,512]{2,1,0:T(8,128)S(1)} %pad_maximum_fusion.1.fields_ref, bf16[144,1024]{1,0:T(8,128)(2,1)} %get-tuple-element.67.refs_0_, bf16[144,1024]{1,0:T(8,128)(2,1)} %get-tuple-element.54.refs_1_, ...), custom_call_target="tpu_custom_call" | custom-call | flops 31457280 | bytes 4194304 | tf_op jit(solution)/shard_map/propagate/pallas_call | solution.py:560
  86.3 9.8 %propagate.3 = f32[2304,512]{1,0:T(8,128)} custom-call(s32[6]{0:T(128)S(1)} %stack.70.where, f32[144,8]{1,0:T(8,128)S(1)} %copy.37.coef_ref, f32[3,16,512]{2,1,0:T(8,128)S(1)} %pad_maximum_fusion.1.fields_ref, bf16[144,1024]{1,0:T(8,128)(2,1)} %get-tuple-element.67.refs_0_, ...), custom_call_target="tpu_custom_call", output_to_operand_aliasing={{}: (25, {})} | custom-call | flops 39321600 | bytes 5242880 | tf_op jit(solution)/shard_map/propagate/pallas_call | solution.py:560
  (126 shorter events, 3.8 us)
Async XLA Ops:
  4.3 16.9 %collective-permute-start = (bf16[144,1024]{1,0:T(8,128)(2,1)}, bf16[144,1024]{1,0:T(8,128)(2,1)S(1)}, u32[]{:S(2)}, u32[]{:S(2)}) collective-permute-start(bf16[144,1024]{1,0:T(8,128)(2,1)} %get-tuple-element.54.refs_1_), channel_id=1, source_target_pairs={{0,8},{4,12},{8,0},{12,4},{16,24},{20,28},{24,16},{28,20},{1,9},{5... | collective-permute-start | bytes 884744 | tf_op jit(solution)/shard_map/ppermute | solution.py:118
  5.9 15.3 %collective-permute-start.1 = (bf16[144,1024]{1,0:T(8,128)(2,1)}, bf16[144,1024]{1,0:T(8,128)(2,1)S(1)}, u32[]{:S(2)}, u32[]{:S(2)}) collective-permute-start(bf16[144,1024]{1,0:T(8,128)(2,1)} %get-tuple-element.55.refs_2_), channel_id=1, source_target_pairs={{0,16},{4,20},{8,24},{12,28},{16,0},{20,4},{24,8},{28,12},{1,17},{... | collective-permute-start | bytes 884744 | tf_op jit(solution)/shard_map/ppermute | solution.py:118
  7.4 13.8 %collective-permute-start.2 = (bf16[144,1024]{1,0:T(8,128)(2,1)}, bf16[144,1024]{1,0:T(8,128)(2,1)S(1)}, u32[]{:S(2)}, u32[]{:S(2)}) collective-permute-start(bf16[144,1024]{1,0:T(8,128)(2,1)} %get-tuple-element.56.refs_3_), channel_id=1, source_target_pairs={{0,24},{4,28},{8,16},{12,20},{16,8},{20,12},{24,0},{28,4},{1,25},{... | collective-permute-start | bytes 884744 | tf_op jit(solution)/shard_map/ppermute | solution.py:118
  21.3 2.9 %collective-permute-start.3 = (bf16[144,1024]{1,0:T(8,128)(2,1)S(1)}, bf16[144,1024]{1,0:T(8,128)(2,1)S(1)}, u32[]{:S(2)}, u32[]{:S(2)}) collective-permute-start(bf16[144,1024]{1,0:T(8,128)(2,1)S(1)} %copy-done.7), channel_id=1, source_target_pairs={{0,4},{4,0},{8,12},{12,8},{16,20},{20,16},{24,28},{28,24},{1,5},{5... | collective-permute-start | bytes 884744 | tf_op jit(solution)/shard_map/ppermute | solution.py:118
  21.4 4.4 %collective-permute-start.4 = (bf16[144,1024]{1,0:T(8,128)(2,1)S(1)}, bf16[144,1024]{1,0:T(8,128)(2,1)S(1)}, u32[]{:S(2)}, u32[]{:S(2)}) collective-permute-start(bf16[144,1024]{1,0:T(8,128)(2,1)S(1)} %collective-permute-done.refs_1_), channel_id=1, source_target_pairs={{0,4},{4,0},{8,12},{12,8},{16,20},{20,16},{24,28},{28,24},{1,5},{5... | collective-permute-start | bytes 884744 | tf_op jit(solution)/shard_map/ppermute | solution.py:118
  21.9 4.5 %collective-permute-start.5 = (bf16[144,1024]{1,0:T(8,128)(2,1)S(1)}, bf16[144,1024]{1,0:T(8,128)(2,1)S(1)}, u32[]{:S(2)}, u32[]{:S(2)}) collective-permute-start(bf16[144,1024]{1,0:T(8,128)(2,1)S(1)} %collective-permute-done.1.refs_2_), channel_id=1, source_target_pairs={{0,4},{4,0},{8,12},{12,8},{16,20},{20,16},{24,28},{28,24},{1,5},{5... | collective-permute-start | bytes 884744 | tf_op jit(solution)/shard_map/ppermute | solution.py:118
  21.9 4.5 %collective-permute-start.6 = (bf16[144,1024]{1,0:T(8,128)(2,1)S(1)}, bf16[144,1024]{1,0:T(8,128)(2,1)S(1)}, u32[]{:S(2)}, u32[]{:S(2)}) collective-permute-start(bf16[144,1024]{1,0:T(8,128)(2,1)S(1)} %collective-permute-done.2.refs_3_), channel_id=1, source_target_pairs={{0,4},{4,0},{8,12},{12,8},{16,20},{20,16},{24,28},{28,24},{1,5},{5... | collective-permute-start | bytes 884744 | tf_op jit(solution)/shard_map/ppermute | solution.py:118
  22.6 15.2 %collective-permute-start.12 = (bf16[144,1024]{1,0:T(8,128)(2,1)S(1)}, bf16[144,1024]{1,0:T(8,128)(2,1)S(1)}, u32[]{:S(2)}, u32[]{:S(2)}) collective-permute-start(bf16[144,1024]{1,0:T(8,128)(2,1)S(1)} %copy-done.9), channel_id=1, source_target_pairs={{0,8},{4,12},{8,0},{12,4},{16,24},{20,28},{24,16},{28,20},{1,9},{5... | collective-permute-start | bytes 884744 | tf_op jit(solution)/shard_map/ppermute | solution.py:118
  24.2 15.1 %collective-permute-start.13 = (bf16[144,1024]{1,0:T(8,128)(2,1)S(1)}, bf16[144,1024]{1,0:T(8,128)(2,1)S(1)}, u32[]{:S(2)}, u32[]{:S(2)}) collective-permute-start(bf16[144,1024]{1,0:T(8,128)(2,1)S(1)} %copy-done.10), channel_id=1, source_target_pairs={{0,16},{4,20},{8,24},{12,28},{16,0},{20,4},{24,8},{28,12},{1,17},{... | collective-permute-start | bytes 884744 | tf_op jit(solution)/shard_map/ppermute | solution.py:118
  25.8 13.5 %collective-permute-start.14 = (bf16[144,1024]{1,0:T(8,128)(2,1)S(1)}, bf16[144,1024]{1,0:T(8,128)(2,1)}, u32[]{:S(2)}, u32[]{:S(2)}) collective-permute-start(bf16[144,1024]{1,0:T(8,128)(2,1)S(1)} %copy-done.11), channel_id=1, source_target_pairs={{0,24},{4,28},{8,16},{12,20},{16,8},{20,12},{24,0},{28,4},{1,25},{... | collective-permute-start | bytes 884744 | tf_op jit(solution)/shard_map/ppermute | solution.py:118
  26.3 38.8 %collective-permute-start.7 = (bf16[144,2048]{1,0:T(8,128)(2,1)}, bf16[144,2048]{1,0:T(8,128)(2,1)S(1)}, u32[]{:S(2)}, u32[]{:S(2)}) collective-permute-start(bf16[144,2048]{1,0:T(8,128)(2,1)} %get-tuple-element.83), channel_id=1, source_target_pairs={{0,1},{1,0},{2,3},{3,2},{4,5},{5,4},{6,7},{7,6},{8,9},{9,8},{10,11... | collective-permute-start | bytes 1769480 | tf_op jit(solution)/shard_map/ppermute | solution.py:600
  39.3 1.6 %collective-permute-start.15 = (bf16[144,1024]{1,0:T(8,128)(2,1)S(1)}, bf16[144,1024]{1,0:T(8,128)(2,1)S(1)}, u32[]{:S(2)}, u32[]{:S(2)}) collective-permute-start(bf16[144,1024]{1,0:T(8,128)(2,1)S(1)} %copy-done.8), channel_id=1, source_target_pairs={{0,4},{4,0},{8,12},{12,8},{16,20},{20,16},{24,28},{28,24},{1,5},{5... | collective-permute-start | bytes 884744 | tf_op jit(solution)/shard_map/ppermute | solution.py:118
  39.4 5.0 %collective-permute-start.16 = (bf16[144,1024]{1,0:T(8,128)(2,1)S(1)}, bf16[144,1024]{1,0:T(8,128)(2,1)}, u32[]{:S(2)}, u32[]{:S(2)}) collective-permute-start(bf16[144,1024]{1,0:T(8,128)(2,1)S(1)} %collective-permute-done.12.refs_1_), channel_id=1, source_target_pairs={{0,4},{4,0},{8,12},{12,8},{16,20},{20,16},{24,28},{28,24},{1,5},{5... | collective-permute-start | bytes 884744 | tf_op jit(solution)/shard_map/ppermute | solution.py:118
  39.9 6.2 %collective-permute-start.17 = (bf16[144,1024]{1,0:T(8,128)(2,1)S(1)}, bf16[144,1024]{1,0:T(8,128)(2,1)}, u32[]{:S(2)}, u32[]{:S(2)}) collective-permute-start(bf16[144,1024]{1,0:T(8,128)(2,1)S(1)} %collective-permute-done.13.refs_2_), channel_id=1, source_target_pairs={{0,4},{4,0},{8,12},{12,8},{16,20},{20,16},{24,28},{28,24},{1,5},{5... | collective-permute-start | bytes 884744 | tf_op jit(solution)/shard_map/ppermute | solution.py:118
  40.0 7.0 %collective-permute-start.18 = (bf16[144,1024]{1,0:T(8,128)(2,1)}, bf16[144,1024]{1,0:T(8,128)(2,1)}, u32[]{:S(2)}, u32[]{:S(2)}) collective-permute-start(bf16[144,1024]{1,0:T(8,128)(2,1)} %collective-permute-done.14.refs_3_), channel_id=1, source_target_pairs={{0,4},{4,0},{8,12},{12,8},{16,20},{20,16},{24,28},{28,24},{1,5},{5... | collective-permute-start | bytes 884744 | tf_op jit(solution)/shard_map/ppermute | solution.py:118
  40.7 22.7 %copy-start.1 = (bf16[144,1024]{1,0:T(8,128)(2,1)S(1)}, bf16[144,1024]{1,0:T(8,128)(2,1)}, u32[]{:S(2)}) copy-start(bf16[144,1024]{1,0:T(8,128)(2,1)} %get-tuple-element.93.refs_0_.refs_12_) | copy-start | bytes 884740
  40.7 35.5 %copy-start.21 = (f32[144]{0:T(256)S(1)}, f32[144]{0:T(256)}, u32[]{:S(2)}) copy-start(f32[144]{0:T(256)} %param.14) | copy-start | bytes 1732
  40.7 35.5 %copy-start.22 = (f32[144]{0:T(256)S(1)}, f32[144]{0:T(256)}, u32[]{:S(2)}) copy-start(f32[144]{0:T(256)} %param.13) | copy-start | bytes 1732
  40.7 35.6 %copy-start.19 = (f32[144,2]{0,1:T(2,128)S(1)}, f32[144,2]{0,1:T(2,128)}, u32[]{:S(2)}) copy-start(f32[144,2]{0,1:T(2,128)} %param.15) | copy-start | bytes 3460
  41.0 24.3 %collective-permute-start.8 = (bf16[144,2048]{1,0:T(8,128)(2,1)}, bf16[144,2048]{1,0:T(8,128)(2,1)S(1)}, u32[]{:S(2)}, u32[]{:S(2)}) collective-permute-start(bf16[144,2048]{1,0:T(8,128)(2,1)} %get-tuple-element.84), channel_id=1, source_target_pairs={{0,0},{1,2},{2,1},{3,3},{4,4},{5,6},{6,5},{7,7},{8,8},{9,10},{10,9... | collective-permute-start | bytes 1769480 | tf_op jit(solution)/shard_map/ppermute | solution.py:600
  44.5 12.4 %collective-permute-start.9 = (bf16[144,1024]{1,0:T(8,128)(2,1)}, bf16[144,1024]{1,0:T(8,128)(2,1)S(1)}, u32[]{:S(2)}, u32[]{:S(2)}) collective-permute-start(bf16[144,1024]{1,0:T(8,128)(2,1)} %get-tuple-element.72), channel_id=1, source_target_pairs={{0,8},{4,12},{8,0},{12,4},{16,24},{20,28},{24,16},{28,20},{1,9},{5... | collective-permute-start | bytes 884744 | tf_op jit(solution)/shard_map/ppermute | solution.py:118
  46.1 14.5 %collective-permute-start.10 = (bf16[144,1024]{1,0:T(8,128)(2,1)}, bf16[144,1024]{1,0:T(8,128)(2,1)S(1)}, u32[]{:S(2)}, u32[]{:S(2)}) collective-permute-start(bf16[144,1024]{1,0:T(8,128)(2,1)} %get-tuple-element.73), channel_id=1, source_target_pairs={{0,16},{4,20},{8,24},{12,28},{16,0},{20,4},{24,8},{28,12},{1,17},{... | collective-permute-start | bytes 884744 | tf_op jit(solution)/shard_map/ppermute | solution.py:118
  47.0 15.3 %collective-permute-start.11 = (bf16[144,1024]{1,0:T(8,128)(2,1)}, bf16[144,1024]{1,0:T(8,128)(2,1)S(1)}, u32[]{:S(2)}, u32[]{:S(2)}) collective-permute-start(bf16[144,1024]{1,0:T(8,128)(2,1)} %get-tuple-element.74), channel_id=1, source_target_pairs={{0,24},{4,28},{8,16},{12,20},{16,8},{20,12},{24,0},{28,4},{1,25},{... | collective-permute-start | bytes 884744 | tf_op jit(solution)/shard_map/ppermute | solution.py:118
  56.9 21.2 %copy-start.2 = (bf16[144,1024]{1,0:T(8,128)(2,1)}, bf16[144,1024]{1,0:T(8,128)(2,1)S(1)}, u32[]{:S(2)}) copy-start(bf16[144,1024]{1,0:T(8,128)(2,1)S(1)} %collective-permute-done.9.refs_1_.refs_13_) | copy-start | bytes 884740
  56.9 11.6 %collective-permute-start.21 = (bf16[144,1024]{1,0:T(8,128)(2,1)}, bf16[144,1024]{1,0:T(8,128)(2,1)S(1)}, u32[]{:S(2)}, u32[]{:S(2)}) collective-permute-start(bf16[144,1024]{1,0:T(8,128)(2,1)} %get-tuple-element.90), channel_id=1, source_target_pairs={{0,8},{4,12},{8,0},{12,4},{16,24},{20,28},{24,16},{28,20},{1,9},{5... | collective-permute-start | bytes 884744 | tf_op jit(solution)/shard_map/ppermute | solution.py:118
  60.6 17.4 %copy-start.3 = (bf16[144,1024]{1,0:T(8,128)(2,1)}, bf16[144,1024]{1,0:T(8,128)(2,1)S(1)}, u32[]{:S(2)}) copy-start(bf16[144,1024]{1,0:T(8,128)(2,1)S(1)} %collective-permute-done.10.refs_2_.refs_14_) | copy-start | bytes 884740
  60.6 13.3 %collective-permute-start.22 = (bf16[144,1024]{1,0:T(8,128)(2,1)}, bf16[144,1024]{1,0:T(8,128)(2,1)S(1)}, u32[]{:S(2)}, u32[]{:S(2)}) collective-permute-start(bf16[144,1024]{1,0:T(8,128)(2,1)} %get-tuple-element.91), channel_id=1, source_target_pairs={{0,16},{4,20},{8,24},{12,28},{16,0},{20,4},{24,8},{28,12},{1,17},{... | collective-permute-start | bytes 884744 | tf_op jit(solution)/shard_map/ppermute | solution.py:118
  62.3 14.2 %collective-permute-start.23 = (bf16[144,1024]{1,0:T(8,128)(2,1)}, bf16[144,1024]{1,0:T(8,128)(2,1)}, u32[]{:S(2)}, u32[]{:S(2)}) collective-permute-start(bf16[144,1024]{1,0:T(8,128)(2,1)} %get-tuple-element.92), channel_id=1, source_target_pairs={{0,24},{4,28},{8,16},{12,20},{16,8},{20,12},{24,0},{28,4},{1,25},{... | collective-permute-start | bytes 884744 | tf_op jit(solution)/shard_map/ppermute | solution.py:118
  65.2 11.3 %collective-permute-start.19 = (bf16[80,2048]{1,0:T(8,128)(2,1)}, bf16[80,2048]{1,0:T(8,128)(2,1)S(1)}, u32[]{:S(2)}, u32[]{:S(2)}) collective-permute-start(bf16[80,2048]{1,0:T(8,128)(2,1)} %get-tuple-element.97), channel_id=1, source_target_pairs={{0,1},{1,0},{2,3},{3,2},{4,5},{5,4},{6,7},{7,6},{8,9},{9,8},{10,11... | collective-permute-start | bytes 983048 | tf_op jit(solution)/shard_map/ppermute | solution.py:600
  65.3 12.7 %collective-permute-start.20 = (bf16[80,2048]{1,0:T(8,128)(2,1)}, bf16[80,2048]{1,0:T(8,128)(2,1)S(1)}, u32[]{:S(2)}, u32[]{:S(2)}) collective-permute-start(bf16[80,2048]{1,0:T(8,128)(2,1)} %get-tuple-element.98), channel_id=1, source_target_pairs={{0,0},{1,2},{2,1},{3,3},{4,4},{5,6},{6,5},{7,7},{8,8},{9,10},{10,9... | collective-permute-start | bytes 983048 | tf_op jit(solution)/shard_map/ppermute | solution.py:600
  68.5 17.7 %collective-permute-start.24 = (bf16[80,2048]{1,0:T(8,128)(2,1)S(1)}, bf16[80,2048]{1,0:T(8,128)(2,1)S(1)}, u32[]{:S(2)}, u32[]{:S(2)}) collective-permute-start(bf16[80,2048]{1,0:T(8,128)(2,1)S(1)} %get-tuple-element.99), channel_id=1, source_target_pairs={{0,1},{1,0},{2,3},{3,2},{4,5},{5,4},{6,7},{7,6},{8,9},{9,8},{10,11... | collective-permute-start | bytes 983048 | tf_op jit(solution)/shard_map/ppermute | solution.py:600
  73.8 12.5 %collective-permute-start.25 = (bf16[80,2048]{1,0:T(8,128)(2,1)S(1)}, bf16[80,2048]{1,0:T(8,128)(2,1)S(1)}, u32[]{:S(2)}, u32[]{:S(2)}) collective-permute-start(bf16[80,2048]{1,0:T(8,128)(2,1)S(1)} %get-tuple-element.100), channel_id=1, source_target_pairs={{0,0},{1,2},{2,1},{3,3},{4,4},{5,6},{6,5},{7,7},{8,8},{9,10},{10,9... | collective-permute-start | bytes 983048 | tf_op jit(solution)/shard_map/ppermute | solution.py:600
  (27 other events, 231.1 us)
